TPU v7x, 32 devices: a whole 2x2x4 slice. The times are simulated.
32 devices in a mesh: dp: 8 (over y, x, core), mp: 4 (over z).
Axes of the slice: x: 2, y: 2, z: 4, core: 2. Of those that a mesh axis runs over, the one named last changes fastest.
Arguments:
- tokens: bfloat16 [49152, 768], P(('dp', 'mp')), may hold values from -6 to 6
- out_grad: bfloat16 [49152, 768], P(('dp', 'mp')), may hold values from -6 to 6
- live_images: int32 [32, 2], P(('dp', 'mp')), may hold values from 0 to 2, as said below
- first_gain: float32 [768], replicated, may hold values from 0.5 to 1.5
- first_shift: float32 [768], replicated, may hold values from -1.75 to 1.75
- project_in: bfloat16 [768, 3, 768], P(None, None, 'mp'), may hold values from -0.21875 to 0.21875
- query_value_bias: bfloat16 [2, 768], P(None, 'mp'), may hold values from -3 to 3
- project_out: bfloat16 [768, 768], P('mp'), may hold values from -1.75 to 1.75
- output_bias: float32 [768], replicated, may hold values from -1.75 to 1.75
- second_gain: float32 [768], replicated, may hold values from 0.5 to 1.5
- second_shift: float32 [768], replicated, may hold values from -1.75 to 1.75
- up_weight: bfloat16 [768, 3072], P(None, 'mp'), may hold values from -0.21875 to 0.21875
- up_bias: bfloat16 [3072], P('mp'), may hold values from -3 to 3
- down_weight: bfloat16 [3072, 768], P('mp'), may hold values from -0.109375 to 0.109375
- down_bias: float32 [768], replicated, may hold values from -1.75 to 1.75
Outputs:
- output: bfloat16 [49152, 768], P(('dp', 'mp'))
- input_grad: float32 [49152, 768], P(('dp', 'mp'))
- grad_first_gain: float32 [768], replicated
- grad_first_shift: float32 [768], replicated
- grad_project_in: float32 [768, 3, 768], P(None, None, 'mp')
- grad_query_value_bias: float32 [2, 768], P(None, 'mp')
- grad_project_out: float32 [768, 768], P('mp')
- grad_output_bias: float32 [768], replicated
- grad_second_gain: float32 [768], replicated
- grad_second_shift: float32 [768], replicated
- grad_up_weight: float32 [768, 3072], P(None, 'mp')
- grad_up_bias: float32 [3072], P('mp')
- grad_down_weight: float32 [3072, 768], P('mp')
- grad_down_bias: float32 [768], replicated
Inputs may be any that keep to these rules, and one draw needn't show every extreme that they name: `live_images`: column 0 counts a device's live low-resolution images (1 to 2), column 1 its live high-resolution images (0 to 1); live images fill the first slots of their region; in every draw some device has all its low-resolution slots live and some device all its high-resolution slots.
All inputs are finite; a program needn't handle non-finite values.
Results may differ from a plain program's by a relative error of at most 0.012.
The roundings to bfloat16 on the way count: a program that leaves them out, or rounds other values in their place, can miss the bound.
Values may be sent and summed in bfloat16 or wider, within the bound.
A program may use at most 256 MiB of HBM per device.

v0:
```python
import jax
import jax.numpy as jnp
from jax import lax
from jax.sharding import PartitionSpec as P

HEAD_DIM = 48
SHORT_LEN = 256
LONG_LEN = 1024
SHORT_SLOTS = 2
LONG_SLOTS = 1


epsilon = 1e-05


def layer_norm(rows_in, norm_gain, norm_shift):
    average = jnp.mean(rows_in, axis=-1, keepdims=True)
    centred = rows_in - average
    variance = jnp.mean(centred * centred, axis=-1, keepdims=True)
    return centred * lax.rsqrt(variance + epsilon) * norm_gain + norm_shift


def gelu_exact(values):
    return jax.nn.gelu(values, approximate=False)


def dot_plain(left, right):
    return jnp.dot(left, right, preferred_element_type=jnp.float32)


def dot_right_t(left, right):
    return lax.dot_general(
        left, right, (((1,), (1,)), ((), ())), preferred_element_type=jnp.float32
    )


def dot_left_t(left, right):
    return lax.dot_general(
        left, right, (((0,), (0,)), ((), ())), preferred_element_type=jnp.float32
    )


def term_rows(values, weight, transposed):
    if transposed:
        return dot_right_t(values, weight)
    return dot_plain(values, weight)


def live_mask(live_images, total_rows):
    row_index = lax.broadcasted_iota(jnp.int32, (total_rows, 1), 0)
    short_rows = SHORT_SLOTS * SHORT_LEN
    short_slot = row_index // SHORT_LEN
    long_slot = (row_index - short_rows) // LONG_LEN
    return jnp.where(
        row_index < short_rows, short_slot < live_images[0, 0], long_slot < live_images[0, 1]
    )


def split_images(flat, buffers):
    width = flat.shape[-1]
    short_rows = SHORT_SLOTS * SHORT_LEN
    blocks = flat.reshape(buffers, short_rows + LONG_SLOTS * LONG_LEN, width)
    short_part = blocks[:, :short_rows].reshape(buffers * SHORT_SLOTS, SHORT_LEN, width)
    long_part = blocks[:, short_rows:]
    return (short_part, long_part)


def to_groups(images):
    image_count, length, width = images.shape
    heads = width // HEAD_DIM
    group_heads = 4
    shaped = images.reshape(image_count, length, heads // group_heads, group_heads, HEAD_DIM)
    return jnp.moveaxis(shaped, 2, 1).reshape(
        image_count * (heads // group_heads), length, group_heads, HEAD_DIM
    )


def from_groups(grouped, image_count):
    total, length, group_heads, head_size = grouped.shape
    shaped = grouped.reshape(image_count, total // image_count, length, group_heads, head_size)
    return jnp.moveaxis(shaped, 1, 2).reshape(image_count, length, -1)


def join_images(short_grouped, long_grouped, buffers):
    short_part = from_groups(short_grouped, buffers * SHORT_SLOTS)
    long_part = from_groups(long_grouped, buffers * LONG_SLOTS)
    width = short_part.shape[-1]
    blocks = jnp.concatenate([short_part.reshape(buffers, -1, width), long_part], axis=1)
    return blocks.reshape(-1, width)


def attend(query_img, key_img, value_img):
    scale = query_img.shape[-1] ** (-0.5)
    scores = (
        jnp.einsum("bqhd,bkhd->bhqk", query_img, key_img, preferred_element_type=jnp.float32)
        * scale
    )
    top_score = jnp.max(scores, axis=-1, keepdims=True)
    weights = jnp.exp(scores - top_score)
    totals = jnp.sum(weights, axis=-1, keepdims=True)
    probs = (weights / totals).astype(jnp.bfloat16)
    mixed = jnp.einsum("bhqk,bkhd->bqhd", probs, value_img, preferred_element_type=jnp.float32)
    return (mixed.astype(jnp.bfloat16), (top_score + jnp.log(totals))[..., 0])


def attend_back(query_img, key_img, value_img, back_mixed, logsum):
    scale = query_img.shape[-1] ** (-0.5)
    scores = (
        jnp.einsum("bqhd,bkhd->bhqk", query_img, key_img, preferred_element_type=jnp.float32)
        * scale
    )
    probs = jnp.exp(scores - logsum[..., None])
    back_value = jnp.einsum(
        "bhqk,bqhd->bkhd",
        probs.astype(jnp.bfloat16),
        back_mixed,
        preferred_element_type=jnp.float32,
    )
    back_probs = jnp.einsum(
        "bqhd,bkhd->bhqk", back_mixed, value_img, preferred_element_type=jnp.float32
    )
    inner = jnp.sum(back_probs * probs, axis=-1, keepdims=True)
    back_scores = (probs * (back_probs - inner)).astype(jnp.bfloat16)
    back_query = (
        jnp.einsum("bhqk,bkhd->bqhd", back_scores, key_img, preferred_element_type=jnp.float32)
        * scale
    )
    back_key = (
        jnp.einsum("bhqk,bqhd->bkhd", back_scores, query_img, preferred_element_type=jnp.float32)
        * scale
    )
    return (
        back_query.astype(jnp.bfloat16),
        back_key.astype(jnp.bfloat16),
        back_value.astype(jnp.bfloat16),
    )


def attend_single(members):
    mixed, logsum = attend(members[0][None], members[1][None], members[2][None])
    return (mixed[0], logsum[0])


def attend_single_back(members):
    gradients = attend_back(*[member[None] for member in members])
    return tuple((gradient[0] for gradient in gradients))


def attention_forward(query_rows, key_rows, value_rows, buffers):
    pieces = [split_images(t, buffers) for t in (query_rows, key_rows, value_rows)]
    short_groups = [to_groups(p[0]) for p in pieces]
    long_groups = [to_groups(p[1]) for p in pieces]
    short_mixed, short_logsum = attend(short_groups[0], short_groups[1], short_groups[2])
    long_mixed, long_logsum = lax.map(
        attend_single, (long_groups[0], long_groups[1], long_groups[2])
    )
    return (join_images(short_mixed, long_mixed, buffers), (short_logsum, long_logsum))


def attention_backward(query_rows, key_rows, value_rows, back_mixed, logsums, buffers):
    pieces = [split_images(t, buffers) for t in (query_rows, key_rows, value_rows, back_mixed)]
    short_groups = [to_groups(p[0]) for p in pieces]
    long_groups = [to_groups(p[1]) for p in pieces]
    short_back = attend_back(
        short_groups[0], short_groups[1], short_groups[2], short_groups[3], logsums[0]
    )
    long_back = lax.map(
        attend_single_back,
        (long_groups[0], long_groups[1], long_groups[2], long_groups[3], logsums[1]),
    )
    return tuple((join_images(short_back[i], long_back[i], buffers) for i in range(3)))


def share_first(values):
    return lax.all_gather(values, "mp", axis=0, tiled=True)


def share_second(values):
    return lax.all_gather(values, "mp", axis=0, tiled=True)


def share_output(values):
    return lax.all_gather(values, "mp", axis=0, tiled=True)


def share_branch(values):
    return lax.all_gather(values, "mp", axis=0, tiled=True)


def reduce_attention(values, weight):
    return lax.psum_scatter(term_rows(values, weight, False), "mp", scatter_dimension=0, tiled=True)


def reduce_feed(values, weight):
    return lax.psum_scatter(
        term_rows(values, weight, False).astype(jnp.bfloat16), "mp", scatter_dimension=0, tiled=True
    ).astype(jnp.float32)


def reduce_feed_back(values, weight):
    return lax.psum_scatter(term_rows(values, weight, True), "mp", scatter_dimension=0, tiled=True)


def reduce_attention_back(values, weight):
    return lax.psum_scatter(term_rows(values, weight, True), "mp", scatter_dimension=0, tiled=True)


def local(
    tokens,
    out_grad,
    live_images,
    first_gain,
    first_shift,
    project_in,
    query_value_bias,
    project_out,
    output_bias,
    second_gain,
    second_shift,
    up_weight,
    up_bias,
    down_weight,
    down_bias,
):
    weight_in, pair_bias, weight_out, weight_up, bias_up, weight_down = (
        project_in,
        query_value_bias,
        project_out,
        up_weight,
        up_bias,
        down_weight,
    )
    buffers = lax.axis_size("mp")
    inputs = tokens.astype(jnp.float32)
    first_normed, first_pull = jax.vjp(layer_norm, inputs, first_gain, first_shift)
    first_all = share_first(first_normed.astype(jnp.bfloat16))
    flat_in = weight_in.reshape(weight_in.shape[0], -1)
    projected = dot_plain(first_all, flat_in)
    projected = projected.reshape(projected.shape[0], 3, -1)
    pair_float = pair_bias.astype(jnp.float32)
    query_rows = (projected[:, 0] + pair_float[0]).astype(jnp.bfloat16)
    key_rows = projected[:, 1].astype(jnp.bfloat16)
    value_rows = (projected[:, 2] + pair_float[1]).astype(jnp.bfloat16)
    mixed_rows, logsums = attention_forward(query_rows, key_rows, value_rows, buffers)
    branch = reduce_attention(mixed_rows, weight_out)
    residual = inputs + branch + output_bias
    second_normed, second_pull = jax.vjp(layer_norm, residual, second_gain, second_shift)
    second_all = share_second(second_normed.astype(jnp.bfloat16))
    hidden = dot_plain(second_all, weight_up) + bias_up.astype(jnp.float32)
    activated, gelu_pull = jax.vjp(gelu_exact, hidden)
    act_low = activated.astype(jnp.bfloat16)
    feed = reduce_feed(act_low, weight_down)
    is_live = live_mask(live_images, tokens.shape[0])
    output = jnp.where(is_live, residual + feed + down_bias, 0.0).astype(jnp.bfloat16)
    back_out = jnp.where(is_live, out_grad, jnp.zeros_like(out_grad))
    back_all = share_output(back_out)
    grad_down = dot_left_t(act_low, back_all)
    grad_down_bias = jnp.sum(back_out, axis=0, dtype=jnp.float32)
    back_act = dot_right_t(back_all, weight_down)
    back_hidden = gelu_pull(back_act)[0].astype(jnp.bfloat16)
    grad_up = dot_left_t(second_all, back_hidden)
    grad_up_bias = jnp.sum(back_hidden, axis=0, dtype=jnp.float32)
    back_second = reduce_feed_back(back_hidden, weight_up)
    back_resid_norm, grad_second_gain, grad_second_shift = second_pull(back_second)
    back_residual = back_out.astype(jnp.float32) + back_resid_norm
    grad_output_bias = jnp.sum(back_residual, axis=0)
    back_branch = share_branch(back_residual.astype(jnp.bfloat16))
    grad_out = dot_left_t(mixed_rows, back_branch)
    back_mixed = dot_right_t(back_branch, weight_out).astype(jnp.bfloat16)
    back_query, back_key, back_value = attention_backward(
        query_rows, key_rows, value_rows, back_mixed, logsums, buffers
    )
    grad_pair = jnp.stack(
        [
            jnp.sum(back_query, axis=0, dtype=jnp.float32),
            jnp.sum(back_value, axis=0, dtype=jnp.float32),
        ]
    )
    back_projected = jnp.stack([back_query, back_key, back_value], axis=1).reshape(
        back_query.shape[0], -1
    )
    grad_in = dot_left_t(first_all, back_projected).reshape(weight_in.shape)
    back_first = reduce_attention_back(back_projected, flat_in)
    back_inputs, grad_first_gain, grad_first_shift = first_pull(back_first)
    input_grad = back_residual + back_inputs
    summed = lax.psum(
        (
            grad_in,
            grad_pair,
            grad_out,
            grad_up,
            grad_up_bias,
            grad_down,
            grad_first_gain,
            grad_first_shift,
            grad_output_bias,
            grad_second_gain,
            grad_second_shift,
            grad_down_bias,
        ),
        "dp",
    )
    small_sums = lax.psum(
        (summed[6], summed[7], summed[8], summed[9], summed[10], summed[11]), "mp"
    )
    return (
        output,
        input_grad,
        small_sums[0],
        small_sums[1],
        summed[0],
        summed[1],
        summed[2],
        small_sums[2],
        small_sums[3],
        small_sums[4],
        summed[3],
        summed[4],
        summed[5],
        small_sums[5],
    )


def solution(mesh):
    placed = (
        P(("dp", "mp"), None),
        P(("dp", "mp"), None),
        P(("dp", "mp"), None),
        P(),
        P(),
        P(None, None, "mp"),
        P(None, "mp"),
        P("mp", None),
        P(),
        P(),
        P(),
        P(None, "mp"),
        P("mp"),
        P("mp", None),
        P(),
    )
    return jax.shard_map(
        local,
        mesh=mesh,
        in_specs=placed,
        out_specs=(
            P(("dp", "mp"), None),
            P(("dp", "mp"), None),
            P(),
            P(),
            P(None, None, "mp"),
            P(None, "mp"),
            P("mp", None),
            P(),
            P(),
            P(),
            P(None, "mp"),
            P("mp"),
            P("mp", None),
            P(),
        ),
        check_vma=False,
    )
```

profile of v0, /device:TPU:0, one launch (start us, length us, event | category | flops | bytes accessed | tf_op | source)
XLA Modules:
  0.0 2448.9 jit_solution(10849781490221846792)
XLA Ops:
  15.5 169.6 %all-gather.5.cloned.1.call-done = bf16[6144,768]{1,0:T(8,128)(2,1)} async-done(((bf16[1536,768]{1,0:T(8,128)(2,1)}), bf16[6144,768]{1,0:T(8,128)(2,1)}) %all-gather.5.cloned.1.call-update) | async-done | bytes 9437200 | tf_op jit(solution)/shard_map/all_gather | solution.py:175
  185.1 8.5 fusion.63
  244.0 114.1 %while.26 = (s32[]{:T(128)}, bf16[4,1024,4,48]{1,3,2,0:T(8,128)(2,1)}, f32[4,4,1024]{2,1,0:T(4,128)}, bf16[4,1024,4,48]{1,3,2,0:T(8,128)(2,1)}, bf16[4,1024,4,48...) while((s32[]{:T(128)}, bf16[4,1024,4,48]{1,3,2,0:T(8,128)(2,1)}, ...), condition=%wide.region_7.8_spmd, body=%wide.region_4.7_spmd.sunk | while | flops 843247616 | bytes 52037720 | solution.py:154
  244.2 9.2 multiply_reduce_fusion.9
  253.4 8.5 fusion.176
  262.0 10.1 fusion.177
  272.6 9.2 multiply_reduce_fusion.9
  281.8 8.5 fusion.176
  290.3 10.1 fusion.177
  301.0 9.2 multiply_reduce_fusion.9
  310.2 8.5 fusion.176
  318.7 10.1 fusion.177
  329.4 9.2 multiply_reduce_fusion.9
  338.5 8.5 fusion.176
  347.1 10.1 fusion.177
  375.0 7.9 fusion.130
  383.1 312.1 %reduce-scatter.5.cloned.1.call-done = f32[1536,768]{1,0:T(8,128)} async-done(((f32[6144,768]{1,0:T(8,128)}), f32[1536,768]{1,0:T(8,128)}) %reduce-scatter.5.cloned.1.call-update) | async-done | bytes 4718608 | tf_op jit(solution)/shard_map/reduce_scatter | solution.py:191
  707.6 163.5 %all-gather.7.cloned.1.call-done = bf16[6144,768]{1,0:T(8,128)(2,1)} async-done(((bf16[1536,768]{1,0:T(8,128)(2,1)}), bf16[6144,768]{1,0:T(8,128)(2,1)}) %all-gather.7.cloned.1.call-update) | async-done | bytes 9437200 | tf_op jit(solution)/shard_map/all_gather | solution.py:179
  871.1 14.9 fusion.131
  886.0 152.2 %all-gather.9.cloned.1.call-done = bf16[6144,768]{1,0:T(8,128)(2,1)} async-done(((bf16[1536,768]{1,0:T(8,128)(2,1)}), bf16[6144,768]{1,0:T(8,128)(2,1)}) %all-gather.9.cloned.1.call-update) | async-done | bytes 9437200 | tf_op jit(solution)/shard_map/all_gather | solution.py:183
  1038.2 53.6 %convert_reduce_fusion = (f32[768]{0:T(1024)}, bf16[6144,768]{1,0:T(8,128)(2,1)S(1)}, f32[6144,768]{1,0:T(8,128)}) fusion(f32[6144,768]{1,0:T(8,128)} %fusion.131, f32[768]{0:T(1024)S(1)} %convert_element_type.155, bf16[6144,768]{1,0:T(8,128)(2,1)} %all-gather.9.cloned.1.call-done, bf16[768,768]{1,0:T(8,128)(2,1)S(1)} %copy-done), kind=kOutput, calls=%fused_computation.60 | convolution fusion | flops 7601650688 | bytes 57808896 | tf_op jit(solution)/shard_map/dot_general | solution.py:32
  1095.4 10.8 fusion.132
  1106.7 13.5 multiply_convert_fusion.1
  1123.8 9.6 convolution_convert_fusion
  1133.5 284.8 %reduce-scatter.9.cloned.1.call-done = f32[1536,768]{1,0:T(8,128)} async-done(((f32[6144,768]{1,0:T(8,128)}), f32[1536,768]{1,0:T(8,128)}) %reduce-scatter.9.cloned.1.call-update) | async-done | bytes 4718608 | tf_op jit(solution)/shard_map/reduce_scatter | solution.py:201
  1423.7 159.3 %reduce-scatter.7.cloned.1.call-done = bf16[1536,768]{1,0:T(8,128)(2,1)} async-done(((bf16[6144,768]{1,0:T(8,128)(2,1)}), bf16[1536,768]{1,0:T(8,128)(2,1)}) %reduce-scatter.7.cloned.1.call-update) | async-done | bytes 2359312 | tf_op jit(solution)/shard_map/reduce_scatter | solution.py:195
  1583.0 7.3 fusion.124
  1594.8 167.7 %all-gather.11.cloned.1.call-done = bf16[6144,768]{1,0:T(8,128)(2,1)} async-done(((bf16[1536,768]{1,0:T(8,128)(2,1)}), bf16[6144,768]{1,0:T(8,128)(2,1)}) %all-gather.11.cloned.1.call-update) | async-done | bytes 9437200 | tf_op jit(solution)/shard_map/all_gather | solution.py:187
  1762.5 8.3 convolution_convert_fusion.1
  1800.3 155.9 %while.27 = (s32[]{:T(128)}, bf16[4,1024,4,48]{1,3,2,0:T(8,128)(2,1)}, bf16[4,1024,4,48]{1,3,2,0:T(8,128)(2,1)}, bf16[4,1024,4,48]{1,3,2,0:T(8,128)(2,1)}, bf16[...) while((s32[]{:T(128)}, ...), condition=%wide.region_18.19_spmd, body=%wide.region_16.18_spmd.sunk | while | flops 2064576512 | bytes 163435680 | solution.py:167
  1809.4 9.2 multiply_reduce_fusion.10
  1818.6 10.6 multiply_convert_fusion.6
  1829.2 6.9 fusion.188
  1848.3 9.2 multiply_reduce_fusion.10
  1857.5 10.6 multiply_convert_fusion.6
  1887.3 9.2 multiply_reduce_fusion.10
  1896.4 10.6 multiply_convert_fusion.6
  1907.1 6.9 fusion.188
  1926.2 9.2 multiply_reduce_fusion.10
  1935.4 10.6 multiply_convert_fusion.6
  1991.2 10.7 convolution_bitcast_fusion
  2002.1 14.9 fusion.134
  2017.0 14.2 fusion.135
  2034.1 7.1 fusion.61
  2047.5 266.6 %reduce-scatter.11.cloned.1.call-done = f32[1536,768]{1,0:T(8,128)} async-done(((f32[6144,768]{1,0:T(8,128)}), f32[1536,768]{1,0:T(8,128)}) %reduce-scatter.11.cloned.1.call-update) | async-done | bytes 4718608 | tf_op jit(solution)/shard_map/reduce_scatter | solution.py:205
  2326.7 26.2 %all-reduce = (f32[768]{0:T(1024)S(1)}, f32[768]{0:T(1024)S(1)}, f32[2,192]{1,0:T(2,128)}, f32[768]{0:T(1024)S(1)}, f32[768]{0:T(1024)S(1)}, /*index=5*/f32[768]{0:T(1024)S(1)}, f32[768]{0:T(1024)}, f32[768]{0:T(1024)S(1)}) all-reduce(f32[768]{0:T(1024)S(1)} %get-tuple-element.103, ...), channel_id=1, replica_groups=mesh['dp'=8,'mp'=4] {'dp'}, use_global_device_ids=true, to_apply=%region_23.24 | all-reduce | flops 5760 | bytes 46080 | tf_op jit(solution)/shard_map/psum | solution.py:286
  2352.9 19.7 all-reduce.2
  2372.6 61.8 %all-reduce.5.cloned.1.call-done = (f32[768,3,192]{0,2,1:T(8,128)}, f32[192,768]{1,0:T(8,128)}, f32[768,768]{1,0:T(8,128)}, f32[768,768]{1,0:T(8,128)}) async-done(((f32[768,3,192]{0,2,1:T(8,128)}, f32[192,768]{1,0:T(8,128)}, f32[768,768]{1,0:T(8,128)}, f32[768,768]{1,0:T(8,128)}), (f32[768,3,192]{0,2,1:T(8,128)}, f32[192,768]{1,0:T(8,128)}, f32[768,768]{1,0:T(8,128)}, ...) | async-done | bytes 7077904 | tf_op jit(solution)/shard_map/psum | solution.py:286
  (319 shorter events, 264.4 us)
Async XLA Ops:
  7.2 1031.0 %copy-start = (bf16[768,768]{1,0:T(8,128)(2,1)S(1)}, bf16[768,768]{1,0:T(8,128)(2,1)}, u32[]{:S(2)}) copy-start(bf16[768,768]{1,0:T(8,128)(2,1)} %param.32) | copy-start | bytes 3538948
  7.2 177.8 %all-gather.5.cloned.1.call-start = ((), (), s32[]{:S(2)}) async-start(), calls=%async_computation.4 | async-start | bytes 11796480 | tf_op jit(solution)/shard_map/all_gather | solution.py:175
  15.4 679.7 %reduce-scatter.5.cloned.1.call-start = ((), (), s32[]{:S(2)}) async-start(), calls=%async_computation.5 | async-start | bytes 23592960 | tf_op jit(solution)/shard_map/reduce_scatter | solution.py:191
  215.7 8.4 copy-start.19
  244.0 118.4 %copy-start.17 = (bf16[8,256,4,48]{1,0,3,2:T(8,128)(2,1)S(1)}, bf16[8,256,4,48]{1,0,3,2:T(8,128)(2,1)}, u32[]{:S(2)}) copy-start(bf16[8,256,4,48]{1,0,3,2:T(8,128)(2,1)} %reshape_transpose_reshape_reshape.17) | copy-start | bytes 2359300
  358.1 6.9 copy-start.10
  383.0 312.2 %copy-start.6 = (bf16[1536,768]{1,0:T(8,128)(2,1)S(1)}, bf16[1536,768]{1,0:T(8,128)(2,1)}, u32[]{:S(2)}) copy-start(bf16[1536,768]{1,0:T(8,128)(2,1)} %param.19) | copy-start | bytes 7077892
  383.0 312.2 %copy-start.67 = (f32[768]{0:T(1024)S(1)}, f32[768]{0:T(1024)}, u32[]{:S(2)}) copy-start(f32[768]{0:T(1024)} %param.27) | copy-start | bytes 9220
  383.0 488.1 %all-gather.7.cloned.1.call-start = ((), (), s32[]{:S(2)}) async-start(), calls=%async_computation.6 | async-start | bytes 11796480 | tf_op jit(solution)/shard_map/all_gather | solution.py:179
  703.1 335.1 %all-gather.9.cloned.1.call-start = ((), (), s32[]{:S(2)}) async-start(), calls=%async_computation.8 | async-start | bytes 11796480 | tf_op jit(solution)/shard_map/all_gather | solution.py:183
  707.5 710.8 %reduce-scatter.9.cloned.1.call-start = ((), (), s32[]{:S(2)}) async-start(), calls=%async_computation.9 | async-start | bytes 23592960 | tf_op jit(solution)/shard_map/reduce_scatter | solution.py:201
  886.0 209.5 %copy-start.74 = (bf16[768,768]{1,0:T(8,128)(2,1)S(1)}, bf16[768,768]{1,0:T(8,128)(2,1)}, u32[]{:S(2)}) copy-start(bf16[768,768]{1,0:T(8,128)(2,1)} %param.30) | copy-start | bytes 3538948
  1106.2 476.7 %reduce-scatter.7.cloned.1.call-start = ((), (), s32[]{:S(2)}) async-start(), calls=%async_computation.7 | async-start | bytes 11796480 | tf_op jit(solution)/shard_map/reduce_scatter | solution.py:195
  1133.4 285.0 %copy-start.44 = (f32[1536]{0:T(1024)S(1)}, f32[1536]{0:T(1024)}, u32[]{:S(2)}) copy-start(f32[1536]{0:T(1024)} %copy-done.43) | copy-start | bytes 18436
  1133.4 285.0 %copy-start.50 = (f32[1536]{0:T(1024)S(1)}, f32[1536]{0:T(1024)}, u32[]{:S(2)}) copy-start(f32[1536]{0:T(1024)} %copy-done.49) | copy-start | bytes 18436
  1133.4 285.0 %copy-start.63 = (f32[768]{0:T(1024)S(1)}, f32[768]{0:T(1024)}, u32[]{:S(2)}) copy-start(f32[768]{0:T(1024)} %param.28) | copy-start | bytes 9220
  1133.4 290.2 %copy-start.54 = (f32[1536]{0:T(1024)S(1)}, f32[1536]{0:T(1024)}, u32[]{:S(2)}) copy-start(f32[1536]{0:T(1024)} %copy-done.53) | copy-start | bytes 18436
  1133.4 449.5 %copy-start.60 = (pred[1536]{0:T(1024)(128)(4,1)S(1)}, pred[1536]{0:T(1024)(128)(4,1)}, u32[]{:S(2)}) copy-start(pred[1536]{0:T(1024)(128)(4,1)} %copy-done.59) | copy-start | bytes 4612
  1133.4 449.5 %copy-start.69 = (f32[768]{0:T(1024)S(1)}, f32[768]{0:T(1024)}, u32[]{:S(2)}) copy-start(f32[768]{0:T(1024)} %param.33) | copy-start | bytes 9220
  1133.4 629.0 %all-gather.11.cloned.1.call-start = ((), (), s32[]{:S(2)}) async-start(), calls=%async_computation.10 | async-start | bytes 11796480 | tf_op jit(solution)/shard_map/all_gather | solution.py:187
  1423.7 168.8 %copy-start.13 = (bf16[1536,768]{1,0:T(8,128)(2,1)S(1)}, bf16[1536,768]{1,0:T(8,128)(2,1)}, u32[]{:S(2)}) copy-start(bf16[1536,768]{1,0:T(8,128)(2,1)} %param.20) | copy-start | bytes 7077892
  1592.5 170.0 %copy-start.40 = (bf16[192,768]{1,0:T(8,128)(2,1)S(1)}, bf16[192,768]{1,0:T(8,128)(2,1)}, u32[]{:S(2)}) copy-start(bf16[192,768]{1,0:T(8,128)(2,1)} %param.26) | copy-start | bytes 884740
  1594.7 719.4 %reduce-scatter.11.cloned.1.call-start = ((), (), s32[]{:S(2)}) async-start(), calls=%async_computation.11 | async-start | bytes 23592960 | tf_op jit(solution)/shard_map/reduce_scatter | solution.py:205
  1774.3 9.2 copy-start.20
  1777.4 11.0 slice-start
  1800.3 155.9 %copy-start.31 = (bf16[8,256,4,48]{1,3,2,0:T(8,128)(2,1)S(1)}, bf16[8,256,4,48]{1,3,2,0:T(8,128)(2,1)}, u32[]{:S(2)}) copy-start(bf16[8,256,4,48]{1,3,2,0:T(8,128)(2,1)} %fusion.89) | copy-start | bytes 2359300
  1829.2 6.9 copy-start.2
  1868.1 6.9 copy-start.2
  1907.1 6.9 copy-start.2
  1946.0 6.9 copy-start.2
  1960.2 8.5 copy-start.16
  1960.2 7.2 copy-start.28
  2002.0 432.4 %all-reduce.5.cloned.1.call-start = ((), (), s32[]{:S(2)}) async-start(), calls=%async_computation.12 | async-start | bytes 14155776 | tf_op jit(solution)/shard_map/psum | solution.py:286
  2002.0 29.1 %slice-start.9 = ((s8[9437184]{0:T(1024)(128)(4,1)}), s8[4194304]{0:T(1024)(128)(4,1)S(1)}, s32[]{:S(2)}) async-start(s8[9437184]{0:T(1024)(128)(4,1)} %bitcast.237), calls=%async_computation.22 | async-start | bytes 8388608
  2002.0 29.1 %slice-start.10 = ((s8[9437184]{0:T(1024)(128)(4,1)}), s8[4194304]{0:T(1024)(128)(4,1)S(1)}, s32[]{:S(2)}) async-start(s8[9437184]{0:T(1024)(128)(4,1)} %bitcast.237), calls=%async_computation.23 | async-start | bytes 8388608
  2002.0 32.0 %slice-start.4 = ((s8[7077888]{0:T(1024)(128)(4,1)}), s8[4194304]{0:T(1024)(128)(4,1)S(1)}, s32[]{:S(2)}) async-start(s8[7077888]{0:T(1024)(128)(4,1)} %bitcast.224), calls=%async_computation.17 | async-start | bytes 8388608
  2016.9 14.2 copy-start.24
  2016.9 14.2 slice-start.11
  2016.9 17.1 slice-start.5
  2016.9 17.1 slice-start.6
  2017.0 17.1 slice-start.7
  2041.2 272.9 %copy-start.7 = (bf16[1536,768]{1,0:T(8,128)(2,1)S(1)}, bf16[1536,768]{1,0:T(8,128)(2,1)}, u32[]{:S(2)}) copy-start(bf16[1536,768]{1,0:T(8,128)(2,1)} %param.19) | copy-start | bytes 7077892
  2041.2 272.9 %copy-start.42 = (f32[1536]{0:T(1024)S(1)}, f32[1536]{0:T(1024)}, u32[]{:S(2)}) copy-start(f32[1536]{0:T(1024)} %copy-done.41) | copy-start | bytes 18436
  2041.2 272.9 %copy-start.58 = (f32[768]{0:T(1024)S(1)}, f32[768]{0:T(1024)}, u32[]{:S(2)}) copy-start(f32[768]{0:T(1024)} %param.22) | copy-start | bytes 9220
  2044.4 273.5 %copy-start.52 = (f32[1536]{0:T(1024)S(1)}, f32[1536]{0:T(1024)}, u32[]{:S(2)}) copy-start(f32[1536]{0:T(1024)} %copy-done.51) | copy-start | bytes 18436
  2044.4 273.5 %copy-start.48 = (f32[1536]{0:T(1024)S(1)}, f32[1536]{0:T(1024)}, u32[]{:S(2)}) copy-start(f32[1536]{0:T(1024)} %copy-done.47) | copy-start | bytes 18436
  2320.3 6.4 copy-start.64
  2434.4 6.4 copy-start.34
  (53 other events, 182.6 us)
Sparse Core Ops, SparseCore 0:
  15.6 169.4 all-gather.4
  383.1 311.9 reduce-scatter.4
  703.2 167.8 all-gather.6
  873.2 164.9 all-gather.8
  1106.3 311.9 reduce-scatter.8
  1420.6 162.3 reduce-scatter.6
  1594.8 167.5 all-gather.10
  2002.1 311.9 reduce-scatter.10
  2319.4 114.9 all-reduce.4
where the time goes:
time: 2460 us; the launch traced here: 2450 us
  waiting for transfers between devices  1740 us (71%)
  matrix products  370 us (15%)
  other arithmetic  156 us (6%)
  local copies, waits for them, and re-layouts  123 us (5%)
  blocking collectives  45.9 us (2%)
    reduce_scatter x1, waiting for transfers between devices, reduce_attention(): lax.psum_scatter(term_rows(values, weight, False), 'mp', scatter_dimensio...  312 us
    reduce_scatter x1, waiting for transfers between devices, reduce_feed_back(): lax.psum_scatter(term_rows(values, weight, True), 'mp', scatter_dimension...  285 us
    reduce_scatter x1, waiting for transfers between devices, reduce_attention_back(): lax.psum_scatter(term_rows(values, weight, True), 'mp', scatter_dimension...  267 us
    all_gather x1, waiting for transfers between devices, share_first(): return lax.all_gather(values, 'mp', axis=0, tiled=True)  170 us
    all_gather x1, waiting for transfers between devices, share_branch(): return lax.all_gather(values, 'mp', axis=0, tiled=True)  168 us
    all_gather x1, waiting for transfers between devices, share_second(): return lax.all_gather(values, 'mp', axis=0, tiled=True)  164 us
    reduce_scatter x1, waiting for transfers between devices, reduce_feed(): lax.psum_scatter(term_rows(values, weight, False).astype(jnp.bfloat16), '...  159 us
    all_gather x1, waiting for transfers between devices, share_output(): return lax.all_gather(values, 'mp', axis=0, tiled=True)  152 us
  transfers between devices with their start and end apart: 9, of which 9 were waited for; matrix products, arithmetic and copies ran while one was open for 4% of the time, Pallas kernels for 0%

commit v1 on v0

v1 whole, which is shorter than its diff:
```python
import functools
import math

import jax
import jax.numpy as jnp
from jax import lax
from jax.experimental import pallas as pl
from jax.experimental.pallas import tpu as pltpu
from jax.sharding import PartitionSpec as P

HEAD_DIM = 48
SHORT_LEN = 256
LONG_LEN = 1024
SHORT_SLOTS = 2
LONG_SLOTS = 1
SHORT_ROWS = SHORT_SLOTS * SHORT_LEN
IMAGES = tuple((SHORT_LEN * i, SHORT_LEN) for i in range(SHORT_SLOTS)) + tuple(
    (SHORT_ROWS + LONG_LEN * i, LONG_LEN) for i in range(LONG_SLOTS)
)
SCALE = HEAD_DIM**-0.5
SCALE_LOG2 = SCALE * math.log2(math.e)
ALL = ("mp", "dp")
BF16 = jnp.bfloat16
F32 = jnp.float32
CHUNK = 512

epsilon = 1e-05


def layer_norm(rows_in, norm_gain, norm_shift):
    average = jnp.mean(rows_in, axis=-1, keepdims=True)
    centred = rows_in - average
    variance = jnp.mean(centred * centred, axis=-1, keepdims=True)
    return centred * lax.rsqrt(variance + epsilon) * norm_gain + norm_shift


def gelu_exact(values):
    return jax.nn.gelu(values, approximate=False)


def nn(left, right):
    return lax.dot_general(
        left, right, (((1,), (0,)), ((), ())), preferred_element_type=F32
    )


def nt(left, right):
    return lax.dot_general(
        left, right, (((1,), (1,)), ((), ())), preferred_element_type=F32
    )


def tn(left, right):
    return lax.dot_general(
        left, right, (((0,), (0,)), ((), ())), preferred_element_type=F32
    )


def live_mask(live_images, total_rows):
    row_index = lax.broadcasted_iota(jnp.int32, (total_rows, 1), 0)
    short_slot = row_index // SHORT_LEN
    long_slot = (row_index - SHORT_ROWS) // LONG_LEN
    return jnp.where(
        row_index < SHORT_ROWS, short_slot < live_images[0, 0], long_slot < live_images[0, 1]
    )


def attend_kernel(qkv_ref, mixed_ref, logsum_ref):
    for start, length in IMAGES:
        key_t = qkv_ref[48:96, start : start + length]
        value_t = qkv_ref[96:144, start : start + length]
        value_ones = jnp.concatenate([value_t, jnp.ones((16, length), BF16)], axis=0)
        key_rows = key_t.T
        chunk = min(CHUNK, length)
        for first in range(start, start + length, chunk):
            cols = slice(first, first + chunk)
            scores = nn(key_rows, qkv_ref[0:48, cols])
            top = jnp.max(scores, axis=0, keepdims=True)
            weights = jnp.exp2((scores - top) * SCALE_LOG2).astype(BF16)
            sums = nn(value_ones, weights)
            total = sums[48:49]
            mixed_ref[:, cols] = (sums[:48] / total).astype(BF16)
            logsum_ref[0, :, cols] = top * SCALE_LOG2 + jnp.log2(total)


def attend(qkv):
    heads, rows = qkv.shape[0] // 144, qkv.shape[1]
    return pl.pallas_call(
        attend_kernel,
        grid=(heads,),
        in_specs=[pl.BlockSpec((144, rows), lambda h: (h, 0))],
        out_specs=[
            pl.BlockSpec((48, rows), lambda h: (h, 0)),
            pl.BlockSpec((1, 1, rows), lambda h: (h, 0, 0)),
        ],
        out_shape=[
            jax.ShapeDtypeStruct((heads * 48, rows), BF16),
            jax.ShapeDtypeStruct((heads, 1, rows), F32),
        ],
        compiler_params=pltpu.CompilerParams(vmem_limit_bytes=40 << 20),
        cost_estimate=pl.CostEstimate(
            flops=18_000_000_000, bytes_accessed=9_500_000, transcendentals=19_000_000
        ),
        name="attend",
    )(qkv)


def attend_back_kernel(qkv_ref, back_ref, mixed_ref, logsum_ref, out_ref, held):
    for start, length in IMAGES:
        whole = slice(start, start + length)
        key_t = qkv_ref[48:96, whole]
        key_rows = key_t.T
        value_rows = qkv_ref[96:144, whole].T
        chunk = min(CHUNK, length)
        count = length // chunk
        for i in range(count):
            cols = slice(start + i * chunk, start + (i + 1) * chunk)
            query_t = qkv_ref[0:48, cols]
            back_t = back_ref[:, cols]
            inner = jnp.sum(
                back_t.astype(F32) * mixed_ref[:, cols].astype(F32), axis=0, keepdims=True
            )
            scores = nn(key_rows, query_t)
            probs = jnp.exp2(scores * SCALE_LOG2 - logsum_ref[0, :, cols])
            back_probs = nn(value_rows, back_t)
            back_scores = (probs * (back_probs - inner)).astype(BF16)
            out_ref[0:48, cols] = (nn(key_t, back_scores) * SCALE).astype(BF16)
            back_key = nt(query_t, back_scores)
            back_value = nt(back_t, probs.astype(BF16))
            if i > 0:
                back_key = back_key + held[0:48, 0:length]
                back_value = back_value + held[48:96, 0:length]
            if i < count - 1:
                held[0:48, 0:length] = back_key
                held[48:96, 0:length] = back_value
            else:
                out_ref[48:96, whole] = (back_key * SCALE).astype(BF16)
                out_ref[96:144, whole] = back_value.astype(BF16)


def attend_back(qkv, back_mixed, mixed, logsum):
    heads, rows = qkv.shape[0] // 144, qkv.shape[1]
    return pl.pallas_call(
        attend_back_kernel,
        grid=(heads,),
        in_specs=[
            pl.BlockSpec((144, rows), lambda h: (h, 0)),
            pl.BlockSpec((48, rows), lambda h: (h, 0)),
            pl.BlockSpec((48, rows), lambda h: (h, 0)),
            pl.BlockSpec((1, 1, rows), lambda h: (h, 0, 0)),
        ],
        out_specs=pl.BlockSpec((144, rows), lambda h: (h, 0)),
        out_shape=jax.ShapeDtypeStruct((heads * 144, rows), BF16),
        scratch_shapes=[pltpu.VMEM((96, LONG_LEN), F32)],
        compiler_params=pltpu.CompilerParams(vmem_limit_bytes=40 << 20),
        cost_estimate=pl.CostEstimate(
            flops=40_000_000_000, bytes_accessed=19_000_000, transcendentals=19_000_000
        ),
        name="attend_back",
    )(qkv, back_mixed, mixed, logsum)


def gather_rows(shard):
    parts = lax.axis_size("dp")
    size = shard.shape[0] // parts
    own = lax.dynamic_slice_in_dim(shard, lax.axis_index("dp") * size, size, 0)
    return lax.all_gather(own, ALL, axis=0, tiled=True)


def reduce_rows(partial):
    dp, mp = lax.axis_size("dp"), lax.axis_size("mp")
    width = partial.shape[1]
    blocks = partial.reshape(mp, dp, -1, width).transpose(1, 0, 2, 3).reshape(-1, width)
    summed = lax.psum_scatter(blocks, "dp", scatter_dimension=0, tiled=True)
    summed = lax.psum_scatter(summed, "mp", scatter_dimension=0, tiled=True)
    return lax.all_gather(summed, "dp", axis=0, tiled=True).astype(F32)


def local(
    tokens,
    out_grad,
    live_images,
    first_gain,
    first_shift,
    project_in,
    query_value_bias,
    project_out,
    output_bias,
    second_gain,
    second_shift,
    up_weight,
    up_bias,
    down_weight,
    down_bias,
):
    mp = lax.axis_size("mp")
    width = tokens.shape[1]
    own_heads = project_in.shape[2] // HEAD_DIM
    own_hidden = up_weight.shape[1]
    shard_in = (
        project_in.reshape(width, 3, own_heads, HEAD_DIM).transpose(2, 1, 3, 0).reshape(-1, width)
    )
    weight_in = gather_rows(shard_in)
    weight_out = gather_rows(project_out)
    weight_up = gather_rows(up_weight)
    weight_down = gather_rows(down_weight)
    pair_bias = query_value_bias.reshape(2, own_heads, HEAD_DIM)
    own_bias = jnp.stack([pair_bias[0], jnp.zeros_like(pair_bias[0]), pair_bias[1]], axis=1)
    biases = lax.all_gather(
        jnp.concatenate([own_bias.reshape(-1), up_bias])[None], "mp", axis=0, tiled=True
    )
    bias_in = biases[:, : 3 * own_heads * HEAD_DIM].reshape(-1, 1).astype(F32)
    bias_up = biases[:, 3 * own_heads * HEAD_DIM :].astype(F32)

    inputs = tokens.astype(F32)
    first_normed, first_pull = jax.vjp(layer_norm, inputs, first_gain, first_shift)
    first = first_normed.astype(BF16)
    qkv = (nt(weight_in, first) + bias_in).astype(BF16)
    mixed, logsum = attend(qkv)
    residual = inputs + tn(mixed, weight_out) + output_bias
    second_normed, second_pull = jax.vjp(layer_norm, residual, second_gain, second_shift)
    second = second_normed.astype(BF16)
    is_live = live_mask(live_images, tokens.shape[0])
    back_out = jnp.where(is_live, out_grad, jnp.zeros_like(out_grad))

    feed = residual + down_bias
    back_second = jnp.zeros_like(residual)
    grads_up, grads_up_bias, grads_down = [], [], []
    for j in range(mp):
        up_j = weight_up[j * width : (j + 1) * width]
        down_j = weight_down[j * own_hidden : (j + 1) * own_hidden]
        hidden = nn(second, up_j) + bias_up[j]
        activated, gelu_pull = jax.vjp(gelu_exact, hidden)
        act_low = activated.astype(BF16)
        feed = feed + nn(act_low, down_j)
        grads_down.append(tn(act_low, back_out).astype(BF16))
        back_hidden = gelu_pull(nt(back_out, down_j))[0].astype(BF16)
        grads_up.append(tn(second, back_hidden).astype(BF16))
        grads_up_bias.append(jnp.sum(back_hidden, axis=0, dtype=F32))
        back_second = back_second + nt(back_hidden, up_j)
    output = jnp.where(is_live, feed, 0.0).astype(BF16)
    grad_down = reduce_rows(jnp.concatenate(grads_down, axis=0))
    grad_up = reduce_rows(jnp.concatenate(grads_up, axis=0))
    grad_down_bias = jnp.sum(back_out, axis=0, dtype=F32)

    back_resid_norm, grad_second_gain, grad_second_shift = second_pull(back_second)
    back_residual = back_out.astype(F32) + back_resid_norm
    grad_output_bias = jnp.sum(back_residual, axis=0)
    back_branch = back_residual.astype(BF16)
    grad_out = reduce_rows(nn(mixed, back_branch).astype(BF16))
    back_mixed = nt(weight_out, back_branch).astype(BF16)
    back_qkv = attend_back(qkv, back_mixed, mixed, logsum)
    grad_bias_in = jnp.sum(back_qkv, axis=1, dtype=F32)
    grad_in = reduce_rows(nn(back_qkv, first).astype(BF16))
    back_inputs, grad_first_gain, grad_first_shift = first_pull(tn(back_qkv, weight_in))
    input_grad = back_residual + back_inputs

    small = [
        grad_first_gain,
        grad_first_shift,
        grad_output_bias,
        grad_second_gain,
        grad_second_shift,
        grad_down_bias,
    ]
    packed = lax.psum(
        jnp.concatenate(small + [grad_bias_in] + grads_up_bias).reshape(-1, 128), ALL
    ).reshape(-1)
    sums = [packed[i * width : (i + 1) * width] for i in range(len(small))]
    place = lax.axis_index("mp")
    begin = len(small) * width
    own_rows = 3 * own_heads * HEAD_DIM
    own_in = lax.dynamic_slice_in_dim(packed, begin + place * own_rows, own_rows)
    own_in = own_in.reshape(own_heads, 3, HEAD_DIM)
    grad_pair = jnp.stack([own_in[:, 0].reshape(-1), own_in[:, 2].reshape(-1)])
    begin = begin + mp * own_rows
    grad_up_bias = lax.dynamic_slice_in_dim(packed, begin + place * own_hidden, own_hidden)
    grad_in = (
        grad_in.reshape(own_heads, 3, HEAD_DIM, width).transpose(3, 1, 0, 2).reshape(width, 3, -1)
    )
    return (
        output,
        input_grad,
        sums[0],
        sums[1],
        grad_in,
        grad_pair,
        grad_out,
        sums[2],
        sums[3],
        sums[4],
        grad_up,
        grad_up_bias,
        grad_down,
        sums[5],
    )


def solution(mesh):
    rows = P(("dp", "mp"), None)
    return jax.shard_map(
        local,
        mesh=mesh,
        in_specs=(
            rows,
            rows,
            rows,
            P(),
            P(),
            P(None, None, "mp"),
            P(None, "mp"),
            P("mp", None),
            P(),
            P(),
            P(),
            P(None, "mp"),
            P("mp"),
            P("mp", None),
            P(),
        ),
        out_specs=(
            rows,
            rows,
            P(),
            P(),
            P(None, None, "mp"),
            P(None, "mp"),
            P("mp", None),
            P(),
            P(),
            P(),
            P(None, "mp"),
            P("mp"),
            P("mp", None),
            P(),
        ),
        check_vma=False,
    )
```

time: 2460 us -> 697 us (0.28)
  waiting for transfers between devices: 1740 us -> 233 us
  matrix products: 370 us -> 174 us
  other arithmetic: 156 us -> 33.3 us
  Pallas kernels: 0 us -> 93.5 us
  local copies, waits for them, and re-layouts: 123 us -> 55.9 us
  blocking collectives: 45.9 us -> 81.3 us
    reduce_scatter x4 -> x8, waiting for transfers between devices: 1020 us -> 80.5 us  [the longest x4 60.2 us: reduce_rows(): summed = lax.psum_scatter(blocks, 'dp', scatter_dimension=0, tiled=True)]
    all_gather x4 -> x6, waiting for transfers between devices: 653 us -> 152 us  [the longest x4 139 us: gather_rows(): return lax.all_gather(own, ALL, axis=0, tiled=True)]
    dot_general x46 -> x30, matrix products: 370 us -> 174 us  [the longest x10 91 us: nn(): lax.dot_general(left, right, (((1,), (0,)), ((), ())), preferred_element_...]
    pallas_call x0 -> x2, Pallas kernels: none -> 93.5 us  [the longest x1 55.4 us: attend_back(): pl.pallas_call(attend_back_kernel, grid=(heads,), in_specs=[pl.BlockSpec(...]
    psum x1 -> x0, waiting for transfers between devices: 61.8 us -> none  [local(): lax.psum((grad_in, grad_pair, grad_out, grad_up, grad_up_bias, grad_down,...]
    convert_element_type x12 -> x7, other arithmetic: 71.2 us -> 9.61 us  [the longest x3 6.54 us: reduce_rows(): return lax.all_gather(summed, 'dp', axis=0, tiled=True).astype(F32)]
    reduce_sum x8 -> x2, other arithmetic: 48.3 us -> 11.3 us  [the longest x1 7.26 us: local(): grad_down_bias = jnp.sum(back_out, axis=0, dtype=F32)]
    another operation x18 -> x5, local copies, waits for them, and re-layouts: 34.9 us -> 0.41 us  [the longest x3 0.25 us: local(): jnp.stack([pair_bias[0], jnp.zeros_like(pair_bias[0]), pair_bias[1]], axi...]
  transfers between devices with their start and end apart: 9 -> 14, of which waited for: 9 -> 8; matrix products, arithmetic and copies ran while one was open for 4% -> 25% of each run, Pallas kernels for 0% -> 14%
where the time goes in v1:
time: 697 us; the launch traced here: 688 us
  waiting for transfers between devices  233 us (33%)
  matrix products  174 us (25%)
  Pallas kernels  93.5 us (13%)
  blocking collectives  81.3 us (12%)
  local copies, waits for them, and re-layouts  55.9 us (8%)
  other arithmetic  33.3 us (5%)
  between operations  15.8 us (2%)
    all_gather x4, waiting for transfers between devices, gather_rows(): return lax.all_gather(own, ALL, axis=0, tiled=True)  139 us
    dot_general x10, matrix products, nn(): lax.dot_general(left, right, (((1,), (0,)), ((), ())), preferred_element_...  91 us
    reduce_scatter x4, waiting for transfers between devices, reduce_rows(): summed = lax.psum_scatter(blocks, 'dp', scatter_dimension=0, tiled=True)  60.2 us
    pallas_call x1, Pallas kernels, attend_back(): pl.pallas_call(attend_back_kernel, grid=(heads,), in_specs=[pl.BlockSpec(...  55.4 us
    dot_general x10, matrix products, nt(): lax.dot_general(left, right, (((1,), (1,)), ((), ())), preferred_element_...  49.7 us
    psum x1, blocking collectives, local(): lax.psum(jnp.concatenate(small + [grad_bias_in] + grads_up_bias).reshape(...  39.4 us
    pallas_call x1, Pallas kernels, attend(): pl.pallas_call(attend_kernel, grid=(heads,), in_specs=[pl.BlockSpec((144,...  38 us
    dot_general x10, matrix products, tn(): lax.dot_general(left, right, (((0,), (0,)), ((), ())), preferred_element_...  33.1 us
  transfers between devices with their start and end apart: 14, of which 8 were waited for; matrix products, arithmetic and copies ran while one was open for 25% of the time, Pallas kernels for 14%

profile of v1, /device:TPU:0, one launch (start us, length us, event | category | flops | bytes accessed | tf_op | source)
XLA Modules:
  0.0 688.2 jit_solution(652819103444265528)
XLA Ops:
  17.4 20.4 %all-reduce = bf16[5376]{0:T(1024)(128)(2,1)S(1)} all-reduce(bf16[5376]{0:T(1024)(128)(2,1)S(1)} %dynamic-update-slice), channel_id=2, replica_groups=mesh['dp'=8,'mp'=4] {'mp'}, use_global_device_ids=true, to_apply=%add | all-reduce | flops 5376 | bytes 21504
  38.0 2.8 copy.90
  43.2 4.3 copy.102
  48.8 25.5 %all-gather.8.cloned.1.call-done = bf16[2304,768]{1,0:T(8,128)(2,1)} async-done(((bf16[72,768]{1,0:T(8,128)(2,1)}), bf16[2304,768]{1,0:T(8,128)(2,1)}) %all-gather.8.cloned.1.call-update) | async-done | bytes 3538960 | tf_op jit(solution)/shard_map/all_gather | solution.py:167
  74.3 8.3 %add_convert_fusion.qkv_ref = bf16[2304,1536]{1,0:T(8,128)(2,1)S(1)} fusion(bf16[2304,768]{1,0:T(8,128)(2,1)} %all-gather.8.cloned.1.call-done, f32[2304]{0:T(1024)S(1)} %reshape.268, bf16[1536,768]{0,1:T(8,128)(2,1)S(1)} %copy.90, f32[768]{0:T(1024)S(1)} %copy-done.41, f32[768]{0:T(1024)S(1)} %copy-done.28, f32[1536]{0:T(1024)S(1)} %fusion.86, ...), kind=kOutput, calls=%fused_computation.1 | convolution fusion | flops 5449973760 | bytes 13003776 | tf_op jit(solution)/shard_map/dot_general | solution.py:48
  82.7 38.0 %attend.1 = (bf16[768,1536]{1,0:T(8,128)(2,1)S(1)}, f32[16,1,1536]{2,1,0:T(1,128)S(1)}) custom-call(bf16[2304,1536]{1,0:T(8,128)(2,1)S(1)} %add_convert_fusion.qkv_ref), custom_call_target="tpu_custom_call" | custom-call | flops 17999998976 | bytes 9500000 | tf_op jit(solution)/shard_map/attend/pallas_call | solution.py:88
  120.7 2.9 copy-done.5
  123.6 7.1 %all-gather.10.cloned.1.call-done = bf16[768,768]{1,0:T(8,128)(2,1)} async-done(((bf16[24,768]{1,0:T(8,128)(2,1)}), bf16[768,768]{1,0:T(8,128)(2,1)}) %all-gather.10.cloned.1.call-update) | async-done | bytes 1179664 | tf_op jit(solution)/shard_map/all_gather | solution.py:167
  130.7 4.5 fusion.96
  139.5 57.3 %all-gather.12.cloned.1.call-done = bf16[3072,768]{1,0:T(8,128)(2,1)} async-done(((bf16[96,768]{1,0:T(8,128)(2,1)}), bf16[3072,768]{1,0:T(8,128)(2,1)}) %all-gather.12.cloned.1.call-update) | async-done | bytes 4718608 | tf_op jit(solution)/shard_map/all_gather | solution.py:167
  196.7 16.2 %multiply_convert_fusion = (bf16[1536,768]{0,1:T(8,128)(2,1)}, f32[1536,768]{0,1:T(8,128)}, f32[1536,768]{0,1:T(8,128)}) fusion(f32[768]{0:T(1024)S(1)} %get-tuple-element.67, bf16[1536,768]{0,1:T(8,128)(2,1)} %add_convert_fusion.5, bf16[3072,768]{1,0:T(8,128)(2,1)} %all-gather.12.cloned.1.call-done), kind=kOutput, calls=%fused_computation.45 | convolution fusion | flops 1889796096 | bytes 15338496 | tf_op jit(solution)/shard_map/dot_general | solution.py:42
  213.0 49.6 %all-gather.14.cloned.1.call-done = bf16[3072,768]{1,0:T(8,128)(2,1)} async-done(((bf16[96,768]{1,0:T(8,128)(2,1)}), bf16[3072,768]{1,0:T(8,128)(2,1)}) %all-gather.14.cloned.1.call-update) | async-done | bytes 4718608 | tf_op jit(solution)/shard_map/all_gather | solution.py:167
  262.6 7.0 %convert_reduce_fusion.3 = (f32[768]{0:T(1024)}, bf16[1536,768]{0,1:T(8,128)(2,1)S(1)}) fusion(f32[1536,768]{0,1:T(8,128)} %get-tuple-element.78, bf16[1536,768]{0,1:T(8,128)(2,1)S(1)} %copy-done.11, pred[1536]{0:T(1024)(128)(4,1)S(1)} %fusion.83, bf16[3072,768]{1,0:T(8,128)(2,1)} %all-gather.14.cloned.1.call-done, f32[1536,768]{0,1:T(8,128)} %get-tuple-element.99, ...), kind=kOutput, calls=%fused_computation.32 | convolution fusion | flops 1833172224 | bytes 15343104 | tf_op jit(solution)/shard_map/dot_general | solution.py:48
  272.8 13.2 %multiply_convert_fusion.2 = (bf16[1536,768]{0,1:T(8,128)(2,1)}, f32[1536,768]{0,1:T(8,128)S(1)}, f32[1536,768]{0,1:T(8,128)S(1)}) fusion(f32[768]{0:T(1024)S(1)} %get-tuple-element.69, bf16[1536,768]{0,1:T(8,128)(2,1)S(1)} %copy-done.14, bf16[3072,768]{1,0:T(8,128)(2,1)S(1)} %copy-done.15), kind=kOutput, calls=%fused_computation.71 | convolution fusion | flops 1889796096 | bytes 15339520 | tf_op jit(solution)/shard_map/dot_general | solution.py:42
  285.9 4.9 convert_reduce_fusion.5
  292.8 13.2 %multiply_convert_fusion.3 = (bf16[1536,768]{0,1:T(8,128)(2,1)}, f32[1536,768]{0,1:T(8,128)S(1)}, f32[1536,768]{0,1:T(8,128)S(1)}) fusion(f32[768]{0:T(1024)S(1)} %get-tuple-element.70, bf16[1536,768]{0,1:T(8,128)(2,1)S(1)} %copy-done.14, bf16[3072,768]{1,0:T(8,128)(2,1)S(1)} %copy-done.15), kind=kOutput, calls=%fused_computation.84 | convolution fusion | flops 1889796096 | bytes 15339520 | tf_op jit(solution)/shard_map/dot_general | solution.py:42
  306.1 4.5 convert_reduce_fusion.6
  312.6 13.4 %multiply_convert_fusion.1 = (bf16[1536,768]{0,1:T(8,128)(2,1)}, f32[1536,768]{0,1:T(8,128)S(1)}, f32[1536,768]{0,1:T(8,128)S(1)}) fusion(f32[768]{0:T(1024)S(1)} %copy-done.33, bf16[1536,768]{0,1:T(8,128)(2,1)S(1)} %copy-done.14, bf16[3072,768]{1,0:T(8,128)(2,1)S(1)} %copy-done.15), kind=kOutput, calls=%fused_computation.58 | convolution fusion | flops 1889796096 | bytes 15339520 | tf_op jit(solution)/shard_map/dot_general | solution.py:42
  326.0 3.9 convert_reduce_fusion.4
  333.8 2.6 copy.120
  336.5 3.8 convolution_convert_fusion.2
  347.1 2.5 copy.121
  350.1 4.2 fusion.62
  354.3 3.4 fusion.72
  357.8 5.8 fusion.52
  363.7 5.8 multiply_reduce_fusion
  379.3 55.4 %attend_back.1 = bf16[2304,1536]{1,0:T(8,128)(2,1)S(1)} custom-call(bf16[2304,1536]{1,0:T(8,128)(2,1)} %copy-done.5, bf16[768,1536]{1,0:T(8,128)(2,1)S(1)} %convolution_convert_fusion.1.back_ref, bf16[768,1536]{1,0:T(8,128)(2,1)S(1)} %copy-done.4, f32[16,1,1536]{2,1,0:T(1,128)S(1)} %get-tuple-element.17.logsum_ref), custom_call_target="tpu_custom_call" | custom-call | flops 40000000000 | bytes 19000000 | tf_op jit(solution)/shard_map/attend_back/pallas_call | solution.py:143
  434.8 2.9 copy-done.2
  438.0 8.1 %convolution_convert_fusion = bf16[2304,768]{1,0:T(8,128)(2,1)S(1)} fusion(bf16[2304,1536]{1,0:T(8,128)(2,1)} %copy-done.2, bf16[1536,768]{0,1:T(8,128)(2,1)S(1)} %copy-done.8, f32[768]{0:T(1024)S(1)} %copy-done.42, f32[768]{0:T(1024)S(1)} %copy-done.29, f32[1536]{0:T(1024)S(1)} %copy-done.27, f32[1536]{0:T(1024)S(1)} %copy-done.17), kind=kOutput, calls=%fused_computation.19 | convolution fusion | flops 5444665344 | bytes 12994560 | tf_op jit(solution)/shard_map/dot_general | solution.py:42
  449.0 10.6 %fusion.97 = (f32[768]{0:T(1024)S(1)}, f32[1536,768]{1,0:T(8,128)}) fusion(bf16[2304,1536]{1,0:T(8,128)(2,1)} %copy-done.2, bf16[2304,768]{1,0:T(8,128)(2,1)} %all-gather.8.cloned.1.call-done), kind=kOutput, calls=%fused_computation.215 | convolution fusion | flops 5436996608 | bytes 15338496 | tf_op jit(solution)/shard_map/dot_general | solution.py:54
  459.6 6.1 copy.115
  465.9 3.3 fusion.10
  472.0 15.5 %reduce-scatter.13.cloned.1.call-done = bf16[96,768]{1,0:T(8,128)(2,1)} async-done(((bf16[768,768]{1,0:T(8,128)(2,1)}), bf16[96,768]{1,0:T(8,128)(2,1)}) %reduce-scatter.13.cloned.1.call-update) | async-done | bytes 147472 | tf_op jit(solution)/shard_map/reduce_scatter | solution.py:174
  487.6 7.3 %convert_reduce_fusion.2 = (f32[768]{0:T(1024)S(1)}, f32[768]{0:T(1024)S(1)}, f32[1536,768]{0,1:T(8,128)}) fusion(bf16[1536,768]{0,1:T(8,128)(2,1)} %copy.102, pred[1536]{0:T(1024)(128)(4,1)S(1)} %fusion.83, f32[1536,768]{0,1:T(8,128)} %copy-done.10, f32[1536]{0:T(1024)S(1)} %negate_multiply_fusion.5, f32[1536]{0:T(1024)S(1)} %negate_multiply_fusion.4, ...), kind=kLoop, calls=%fused_computation.15 | loop fusion | flops 17693184 | bytes 18915840 | tf_op jit(solution)/shard_map/reduce_sum | solution.py:244
  494.9 44.6 %reduce-scatter.9.cloned.1.call-done = bf16[288,768]{1,0:T(8,128)(2,1)} async-done(((bf16[2304,768]{1,0:T(8,128)(2,1)}), bf16[288,768]{1,0:T(8,128)(2,1)}) %reduce-scatter.9.cloned.1.call-update) | async-done | bytes 442384 | tf_op jit(solution)/shard_map/reduce_scatter | solution.py:174
  539.6 4.0 convert_reduce_fusion
  543.6 20.3 %reduce-scatter.19.cloned.1.call-done = bf16[96,768]{1,0:T(8,128)(2,1)} async-done(((bf16[384,768]{1,0:T(8,128)(2,1)}), bf16[96,768]{1,0:T(8,128)(2,1)}) %reduce-scatter.19.cloned.1.call-update) | async-done | bytes 147472 | tf_op jit(solution)/shard_map/reduce_scatter | solution.py:175
  564.1 39.4 %psum.7 = f32[78,128]{1,0:T(8,128)S(1)} all-reduce(f32[78,128]{1,0:T(8,128)S(1)} %bitcast.97), channel_id=1, replica_groups=mesh['dp'=8,'mp'=4] {'mp','dp'}, use_global_device_ids=true, to_apply=%region_19.20 | all-reduce | flops 9984 | bytes 79872 | tf_op jit(solution)/shard_map/psum | solution.py:266
  604.5 6.1 copy.123
  610.6 6.3 fusion.58
  617.0 4.2 fusion.68
  621.2 4.2 fusion.48
  625.4 10.2 %select_convert_fusion = bf16[1536,768]{0,1:T(8,128)(2,1)S(1)} fusion(f32[1536,768]{0,1:T(8,128)} %fusion.48, f32[1536,768]{0,1:T(8,128)} %fusion.58, f32[1536,768]{0,1:T(8,128)} %fusion.68, f32[1536,768]{0,1:T(8,128)} %copy-done.6, bf16[1536,768]{0,1:T(8,128)(2,1)} %get-tuple-element.77, f32[768]{0:T(1024)S(1)} %copy-done.37, ...), kind=kOutput, calls=%fused_computation.44 | convolution fusion | flops 1820196864 | bytes 24777216 | tf_op jit(solution)/shard_map/dot_general | solution.py:42
  639.2 10.9 %all_gather.33 = bf16[192,768]{1,0:T(8,128)(2,1)S(1)} all-gather(bf16[24,768]{1,0:T(8,128)(2,1)} %reduce-scatter.15.cloned.1.call-done), channel_id=1, replica_groups=mesh['dp'=8,'mp'=4] {'dp'}, dimensions={0}, use_global_device_ids=true | all-gather | bytes 331776 | tf_op jit(solution)/shard_map/all_gather | solution.py:176
  651.0 10.6 %all_gather.32 = bf16[576,768]{1,0:T(8,128)(2,1)S(1)} all-gather(bf16[72,768]{1,0:T(8,128)(2,1)} %reduce-scatter.11.cloned.1.call-done), channel_id=1, replica_groups=mesh['dp'=8,'mp'=4] {'dp'}, dimensions={0}, use_global_device_ids=true | all-gather | bytes 995328 | tf_op jit(solution)/shard_map/all_gather | solution.py:176
  663.1 2.8 convert_element_type.149
  665.9 12.6 %all-gather.18.cloned.1.call-done = bf16[768,768]{1,0:T(8,128)(2,1)} async-done(((bf16[96,768]{1,0:T(8,128)(2,1)}), bf16[768,768]{1,0:T(8,128)(2,1)}) %all-gather.18.cloned.1.call-update) | async-done | bytes 1179664 | tf_op jit(solution)/shard_map/all_gather | solution.py:176
  678.6 2.8 convert_element_type.154
  (227 shorter events, 58.9 us)
Async XLA Ops:
  7.2 67.1 %all-gather.8.cloned.1.call-start = ((), (), s32[]{:S(2)}) async-start(), calls=%async_computation.8 | async-start | bytes 3649536 | tf_op jit(solution)/shard_map/all_gather | solution.py:167
  9.2 121.4 %all-gather.10.cloned.1.call-start = ((), (), s32[]{:S(2)}) async-start(), calls=%async_computation.9 | async-start | bytes 1216512 | tf_op jit(solution)/shard_map/all_gather | solution.py:167
  10.7 186.0 %all-gather.12.cloned.1.call-start = ((), (), s32[]{:S(2)}) async-start(), calls=%async_computation.10 | async-start | bytes 4866048 | tf_op jit(solution)/shard_map/all_gather | solution.py:167
  11.5 251.1 %all-gather.14.cloned.1.call-start = ((), (), s32[]{:S(2)}) async-start(), calls=%async_computation.11 | async-start | bytes 4866048 | tf_op jit(solution)/shard_map/all_gather | solution.py:167
  13.1 435.2 %reduce-scatter.17.cloned.1.call-start = ((), (), s32[]{:S(2)}) async-start(), calls=%async_computation.16 | async-start | bytes 5308416 | tf_op jit(solution)/shard_map/reduce_scatter | solution.py:174
  38.0 4.7 copy-start.38
  40.8 33.5 %copy-start.7 = (bf16[1536,768]{0,1:T(8,128)(2,1)}, bf16[1536,768]{0,1:T(8,128)(2,1)S(1)}, u32[]{:S(2)}) copy-start(bf16[1536,768]{0,1:T(8,128)(2,1)S(1)} %copy.90) | copy-start | bytes 7077892
  40.8 33.5 %copy-start.28 = (f32[768]{0:T(1024)S(1)}, f32[768]{0:T(1024)}, u32[]{:S(2)}) copy-start(f32[768]{0:T(1024)} %param.18) | copy-start | bytes 9220
  40.9 33.5 %copy-start.41 = (f32[768]{0:T(1024)S(1)}, f32[768]{0:T(1024)}, u32[]{:S(2)}) copy-start(f32[768]{0:T(1024)} %param.19) | copy-start | bytes 9220
  41.2 33.0 %copy-start.16 = (f32[1536]{0:T(1024)}, f32[1536]{0:T(1024)S(1)}, u32[]{:S(2)}) copy-start(f32[1536]{0:T(1024)S(1)} %broadcast_multiply_fusion.1) | copy-start | bytes 18436
  41.9 32.4 %copy-start.22 = (f32[1536]{0:T(1024)}, f32[1536]{0:T(1024)S(1)}, u32[]{:S(2)}) copy-start(f32[1536]{0:T(1024)S(1)} %fusion.9) | copy-start | bytes 18436
  41.9 32.4 %copy-start.26 = (f32[1536]{0:T(1024)}, f32[1536]{0:T(1024)S(1)}, u32[]{:S(2)}) copy-start(f32[1536]{0:T(1024)S(1)} %fusion.86) | copy-start | bytes 18436
  82.7 48.0 %copy-start.40 = (f32[768]{0:T(1024)S(1)}, f32[768]{0:T(1024)}, u32[]{:S(2)}) copy-start(f32[768]{0:T(1024)} %param.23) | copy-start | bytes 9220
  123.6 11.6 %copy-start.3 = (bf16[768,1536]{1,0:T(8,128)(2,1)}, bf16[768,1536]{1,0:T(8,128)(2,1)S(1)}, u32[]{:S(2)}) copy-start(bf16[768,1536]{1,0:T(8,128)(2,1)S(1)} %get-tuple-element.16.mixed_ref) | copy-start | bytes 7077892
  135.8 77.2 %copy-start.24 = (f32[1536]{0:T(1024)}, f32[1536]{0:T(1024)S(1)}, u32[]{:S(2)}) copy-start(f32[1536]{0:T(1024)S(1)} %multiply_reduce_fusion.2) | copy-start | bytes 18436
  137.3 75.7 %copy-start.20 = (f32[1536]{0:T(1024)}, f32[1536]{0:T(1024)S(1)}, u32[]{:S(2)}) copy-start(f32[1536]{0:T(1024)S(1)} %fusion.87) | copy-start | bytes 18436
  196.7 65.8 %copy-start.11 = (bf16[1536,768]{0,1:T(8,128)(2,1)S(1)}, bf16[1536,768]{0,1:T(8,128)(2,1)}, u32[]{:S(2)}) copy-start(bf16[1536,768]{0,1:T(8,128)(2,1)} %copy.102) | copy-start | bytes 7077892
  262.6 7.0 %copy-start.14 = (bf16[1536,768]{0,1:T(8,128)(2,1)S(1)}, bf16[1536,768]{0,1:T(8,128)(2,1)}, u32[]{:S(2)}) copy-start(bf16[1536,768]{0,1:T(8,128)(2,1)} %add_convert_fusion.5) | copy-start | bytes 7077892
  269.6 16.4 %slice-start.2 = ((s8[4718592]{0:T(1024)(128)(4,1)}), s8[4194304]{0:T(1024)(128)(4,1)S(1)}, s32[]{:S(2)}) async-start(s8[4718592]{0:T(1024)(128)(4,1)} %bitcast.91), calls=%async_computation.24 | async-start | bytes 8388608
  272.7 13.2 %slice-start.3 = ((s8[4718592]{0:T(1024)(128)(4,1)}), s8[524288]{0:T(1024)(128)(4,1)S(1)}, s32[]{:S(2)}) async-start(s8[4718592]{0:T(1024)(128)(4,1)} %bitcast.91), calls=%async_computation.25 | async-start | bytes 1048576
  336.4 129.3 %reduce-scatter.21.cloned.1.call-start = ((), (), s32[]{:S(2)}) async-start(), calls=%async_computation.19 | async-start | bytes 5308416 | tf_op jit(solution)/shard_map/reduce_scatter | solution.py:174
  349.6 137.9 %reduce-scatter.13.cloned.1.call-start = ((), (), s32[]{:S(2)}) async-start(), calls=%async_computation.14 | async-start | bytes 1327104 | tf_op jit(solution)/shard_map/reduce_scatter | solution.py:174
  354.3 9.3 %slice-start = ((s8[4718592]{0:T(1024)(128)(4,1)}), s8[4194304]{0:T(1024)(128)(4,1)S(1)}, s32[]{:S(2)}) async-start(s8[4718592]{0:T(1024)(128)(4,1)} %bitcast.77), calls=%async_computation.22 | async-start | bytes 8388608
  357.7 5.9 slice-start.1
  357.7 5.9 copy-start.13
  357.7 5.9 copy-start.19
  357.7 5.9 copy-start.21
  357.8 5.9 copy-start.31
  363.6 5.9 copy-start.25
  379.3 58.6 %copy-start.8 = (bf16[1536,768]{0,1:T(8,128)(2,1)S(1)}, bf16[1536,768]{0,1:T(8,128)(2,1)}, u32[]{:S(2)}) copy-start(bf16[1536,768]{0,1:T(8,128)(2,1)} %copy-done.7) | copy-start | bytes 7077892
  379.3 58.6 %copy-start.17 = (f32[1536]{0:T(1024)S(1)}, f32[1536]{0:T(1024)}, u32[]{:S(2)}) copy-start(f32[1536]{0:T(1024)} %copy-done.16) | copy-start | bytes 18436
  379.3 58.6 %copy-start.27 = (f32[1536]{0:T(1024)S(1)}, f32[1536]{0:T(1024)}, u32[]{:S(2)}) copy-start(f32[1536]{0:T(1024)} %copy-done.26) | copy-start | bytes 18436
  379.3 58.6 %copy-start.29 = (f32[768]{0:T(1024)S(1)}, f32[768]{0:T(1024)}, u32[]{:S(2)}) copy-start(f32[768]{0:T(1024)} %param.18) | copy-start | bytes 9220
  379.3 58.6 %copy-start.42 = (f32[768]{0:T(1024)S(1)}, f32[768]{0:T(1024)}, u32[]{:S(2)}) copy-start(f32[768]{0:T(1024)} %param.19) | copy-start | bytes 9220
  437.7 101.8 %reduce-scatter.9.cloned.1.call-start = ((), (), s32[]{:S(2)}) async-start(), calls=%async_computation.12 | async-start | bytes 3981312 | tf_op jit(solution)/shard_map/reduce_scatter | solution.py:174
  448.3 115.7 %reduce-scatter.19.cloned.1.call-start = ((), (), s32[]{:S(2)}) async-start(), calls=%async_computation.17 | async-start | bytes 737280 | tf_op jit(solution)/shard_map/reduce_scatter | solution.py:175
  449.0 176.4 %reduce-scatter.23.cloned.1.call-start = ((), (), s32[]{:S(2)}) async-start(), calls=%async_computation.20 | async-start | bytes 737280 | tf_op jit(solution)/shard_map/reduce_scatter | solution.py:175
  465.8 173.4 %reduce-scatter.15.cloned.1.call-start = ((), (), s32[]{:S(2)}) async-start(), calls=%async_computation.15 | async-start | bytes 184320 | tf_op jit(solution)/shard_map/reduce_scatter | solution.py:175
  487.5 163.4 %reduce-scatter.11.cloned.1.call-start = ((), (), s32[]{:S(2)}) async-start(), calls=%async_computation.13 | async-start | bytes 552960 | tf_op jit(solution)/shard_map/reduce_scatter | solution.py:175
  494.9 69.1 %copy-start.36 = (f32[768]{0:T(1024)S(1)}, f32[768]{0:T(1024)}, u32[]{:S(2)}) copy-start(f32[768]{0:T(1024)} %get-tuple-element.103) | copy-start | bytes 9220
  494.9 69.2 %copy-start.35 = (f32[768]{0:T(1024)S(1)}, f32[768]{0:T(1024)}, u32[]{:S(2)}) copy-start(f32[768]{0:T(1024)} %get-tuple-element.105) | copy-start | bytes 9220
  494.9 69.2 %copy-start.34 = (f32[768]{0:T(1024)S(1)}, f32[768]{0:T(1024)}, u32[]{:S(2)}) copy-start(f32[768]{0:T(1024)} %get-tuple-element.109) | copy-start | bytes 9220
  539.5 123.5 %all-gather.16.cloned.1.call-start = ((), (), s32[]{:S(2)}) async-start(), calls=%async_computation.18 | async-start | bytes 1327104 | tf_op jit(solution)/shard_map/all_gather | solution.py:176
  563.9 114.6 %all-gather.18.cloned.1.call-start = ((), (), s32[]{:S(2)}) async-start(), calls=%async_computation.21 | async-start | bytes 1327104 | tf_op jit(solution)/shard_map/all_gather | solution.py:176
  604.5 12.4 %slice-start.4 = ((s8[4718592]{0:T(1024)(128)(4,1)}), s8[524288]{0:T(1024)(128)(4,1)S(1)}, s32[]{:S(2)}) async-start(s8[4718592]{0:T(1024)(128)(4,1)} %bitcast.93), calls=%async_computation.26 | async-start | bytes 1048576
  610.6 6.3 slice-start.5
  610.6 6.3 copy-start.45
  661.6 19.8 %copy-start.1 = (bf16[768,768]{1,0:T(8,128)(2,1)S(1)}, bf16[768,768]{1,0:T(8,128)(2,1)}, u32[]{:S(2)}) copy-start(bf16[768,768]{1,0:T(8,128)(2,1)} %param.26) | copy-start | bytes 3538948
  (25 other events, 72.7 us)
Sparse Core Ops, SparseCore 0:
  11.5 62.7 all-gather.7
  77.8 52.8 all-gather.9
  134.1 62.5 all-gather.11
  200.1 62.4 all-gather.13
  336.6 52.6 reduce-scatter.16
  393.0 53.8 reduce-scatter.20
  450.7 36.7 reduce-scatter.12
  491.4 48.0 reduce-scatter.8
  541.9 21.9 reduce-scatter.18
  566.1 20.3 reduce-scatter.22
  588.9 17.7 reduce-scatter.14
  608.8 19.2 reduce-scatter.10
  630.1 22.7 all-gather.15
  654.9 23.6 all-gather.17

commit v2 on v1

--- a/solution.py
+++ b/solution.py
@@ -65,16 +65,140 @@
     )
 
 
-def attend_kernel(qkv_ref, mixed_ref, logsum_ref):
+GROUP = 8
+MESH = pl.DeviceIdType.MESH
+IN_ROWS = 144
+FF_PIECE = 216
+
+
+def place():
+    dp, mp = lax.axis_index("dp"), lax.axis_index("mp")
+    g = lax.rem(dp, GROUP)
+    return dp, dp - g, g // 4, lax.rem(g // 2, 2), lax.rem(g, 2), mp
+
+
+def flip(bit):
+    return 1 - bit
+
+
+class Gather:
+    def __init__(self, own, buffer, piece, split, send, recv):
+        self.own, self.buffer, self.piece, self.split, self.send, self.recv = (
+            own,
+            buffer,
+            piece,
+            split,
+            send,
+            recv,
+        )
+        self.dp, self.base, self.y, self.x, self.core, self.mp = place()
+
+    def device(self, y, x, core):
+        return (self.base + 4 * y + 2 * x + core, self.mp)
+
+    def view(self, ref, y, x, core, part=None):
+        view = self.piece(ref, 2 * y + x, core)
+        if part is None:
+            return view
+        rows = view.shape[0]
+        return view.at[pl.ds(0, self.split)] if part == 0 else view.at[pl.ds(self.split, rows - self.split)]
+
+    def copy(self, kind, slot):
+        y, x, core = self.y, self.x, self.core
+        mine = (y, x, core)
+        buffer = self.buffer.at[slot]
+        if kind == 0:
+            ways = lax.axis_size("mp")
+            hop = 1 if slot == 2 else slot
+            src = self.view(self.buffer.at[1] if slot == 2 else self.own, *mine)
+            dst = self.view(buffer, *mine)
+            device = (self.dp, lax.rem(self.mp + ways - hop, ways))
+        else:
+            near_x, near_y = (y, flip(x), core), (flip(y), x, core)
+            src, device = {
+                1: (self.view(buffer, *mine), near_x),
+                2: (self.view(buffer, *mine), near_y),
+                3: (self.view(buffer, *near_x, 0), near_y),
+                4: (self.view(buffer, *near_y, 1), near_x),
+                5: (self.view(buffer, *mine), (y, x, flip(core))),
+                6: (self.view(buffer, *near_x), (y, x, flip(core))),
+                7: (self.view(buffer, *near_y), (y, x, flip(core))),
+                8: (self.view(buffer, flip(y), flip(x), core), (y, x, flip(core))),
+            }[kind]
+            dst, device = src, self.device(*device)
+        index = kind * 4 + slot
+        return pltpu.make_async_remote_copy(
+            src_ref=src,
+            dst_ref=dst,
+            send_sem=self.send.at[index],
+            recv_sem=self.recv.at[index],
+            device_id=device,
+            device_id_type=MESH,
+        )
+
+    def start(self, slot, *kinds):
+        for kind in kinds:
+            self.copy(kind, slot).start()
+
+    def arrived(self, slot, *kinds):
+        for kind in kinds:
+            self.copy(kind, slot).wait_recv()
+
+    def along(self, slot):
+        self.start(slot, 0)
+
+    def spread(self, slot):
+        self.arrived(slot, 0)
+        self.start(slot, 1, 2, 5)
+
+    def forward(self, slot):
+        self.arrived(slot, 1)
+        self.start(slot, 3, 6)
+        self.arrived(slot, 2)
+        self.start(slot, 4, 7)
+
+    def last(self, slot):
+        self.arrived(slot, 3, 4)
+        self.start(slot, 8)
+
+    def complete(self, slot):
+        self.arrived(slot, 5, 6, 7, 8)
+
+    def finish(self):
+        for slot in (1, 2, 3):
+            for kind in range(GATHER_KINDS):
+                self.copy(kind, slot).wait_send()
+
+
+GATHER_KINDS = 9
+
+
+def in_piece(ref, chip, core):
+    return ref.at[chip, :, pl.ds(pl.multiple_of(core * 384, 128), 384)]
+
+
+def ff_piece(ref, chip, core):
+    return ref.at[2 * chip + core]
+
+
+def greet(partners):
+    barrier = pltpu.get_barrier_semaphore()
+    for partner in partners:
+        pl.semaphore_signal(barrier, inc=1, device_id=partner, device_id_type=MESH)
+    pl.semaphore_wait(barrier, len(partners))
+
+
+def attend_head(qkv_ref, offset, mixed_ref, logsum_ref):
     for start, length in IMAGES:
-        key_t = qkv_ref[48:96, start : start + length]
-        value_t = qkv_ref[96:144, start : start + length]
+        whole = slice(start, start + length)
+        key_t = qkv_ref[pl.ds(offset + 48, 48), whole]
+        value_t = qkv_ref[pl.ds(offset + 96, 48), whole]
         value_ones = jnp.concatenate([value_t, jnp.ones((16, length), BF16)], axis=0)
         key_rows = key_t.T
         chunk = min(CHUNK, length)
         for first in range(start, start + length, chunk):
             cols = slice(first, first + chunk)
-            scores = nn(key_rows, qkv_ref[0:48, cols])
+            scores = nn(key_rows, qkv_ref[pl.ds(offset, 48), cols])
             top = jnp.max(scores, axis=0, keepdims=True)
             weights = jnp.exp2((scores - top) * SCALE_LOG2).astype(BF16)
             sums = nn(value_ones, weights)
@@ -83,26 +207,197 @@
             logsum_ref[0, :, cols] = top * SCALE_LOG2 + jnp.log2(total)
 
 
-def attend(qkv):
-    heads, rows = qkv.shape[0] // 144, qkv.shape[1]
+def slot_order(step):
+    turn = step // 4
+    return turn + (turn // 2) * (1 - 2 * (turn % 2))
+
+
+def attend_kernel(
+    first_ref,
+    in_own,
+    ff_own,
+    bias_own,
+    qkv_ref,
+    mixed_ref,
+    logsum_ref,
+    in_out,
+    ff_all,
+    bias_out,
+    in_all,
+    bias_all,
+    in_send,
+    in_recv,
+    ff_send,
+    ff_recv,
+    bias_send,
+    bias_recv,
+    local_sem,
+):
+    step = pl.program_id(0)
+    dp, base, y, x, core, mp = place()
+    ways = lax.axis_size("mp")
+    gather_in = Gather(in_own, in_all, in_piece, 64, in_send, in_recv)
+    gather_ff = Gather(ff_own, ff_all, ff_piece, 112, ff_send, ff_recv)
+    local_in = pltpu.make_async_copy(in_own, in_all.at[0], local_sem.at[0])
+    local_bias = pltpu.make_async_copy(bias_own, bias_all.at[0], local_sem.at[1])
+    local_ff = pltpu.make_async_copy(ff_own, ff_all.at[0], local_sem.at[2])
+    out_in = pltpu.make_async_copy(in_all, in_out, local_sem.at[3])
+    out_bias = pltpu.make_async_copy(bias_all, bias_out, local_sem.at[4])
+
+    def bias_copy(slot):
+        return pltpu.make_async_remote_copy(
+            src_ref=bias_own,
+            dst_ref=bias_all.at[slot],
+            send_sem=bias_send.at[slot],
+            recv_sem=bias_recv.at[slot],
+            device_id=(dp, lax.rem(mp + ways - slot, ways)),
+            device_id_type=MESH,
+        )
+
+    @pl.when(step == 0)
+    def _():
+        local_in.start()
+        local_bias.start()
+        greet(
+            [
+                (dp, lax.rem(mp + 1, ways)),
+                (dp, lax.rem(mp + 2, ways)),
+                (dp, lax.rem(mp + 3, ways)),
+                (base + 4 * y + 2 * flip(x) + core, mp),
+                (base + 4 * flip(y) + 2 * x + core, mp),
+                (base + 4 * y + 2 * x + flip(core), mp),
+            ]
+        )
+        gather_in.along(1)
+        gather_in.along(3)
+        for slot in (1, 2, 3):
+            bias_copy(slot).start()
+        local_ff.start()
+        local_in.wait()
+        local_bias.wait()
+
+    @pl.when(step == 1)
+    def _():
+        gather_in.spread(1)
+        gather_in.along(2)
+
+    @pl.when(step == 2)
+    def _():
+        gather_in.forward(1)
+        gather_in.spread(3)
+        gather_ff.along(1)
+        gather_ff.along(3)
+
+    @pl.when(step == 3)
+    def _():
+        gather_in.last(1)
+        gather_in.spread(2)
+        gather_in.forward(3)
+        for slot in (1, 2, 3):
+            bias_copy(slot).wait()
+
+    @pl.when(step == 4)
+    def _():
+        gather_in.complete(1)
+        gather_in.last(3)
+        gather_in.forward(2)
+
+    @pl.when(step == 6)
+    def _():
+        gather_in.last(2)
+
+    @pl.when(step == 8)
+    def _():
+        gather_in.complete(3)
+        gather_ff.spread(1)
+        gather_ff.along(2)
+        gather_ff.spread(3)
+
+    @pl.when(step == 12)
+    def _():
+        gather_in.complete(2)
+        out_in.start()
+        out_bias.start()
+        gather_ff.spread(2)
+        gather_ff.forward(1)
+
+    @pl.when(step == 14)
+    def _():
+        gather_ff.forward(3)
+
+    slot = slot_order(step)
+    head = step % 4
+
+    @pl.when(head == 0)
+    def _():
+        bias_t = bias_all[slot, :, 0:256].T
+        for part in range(4):
+            product = nt(in_all[slot, part], first_ref[...])
+            qkv_ref[part * IN_ROWS : (part + 1) * IN_ROWS, :] = (
+                product + bias_t[:IN_ROWS, part : part + 1]
+            ).astype(BF16)
+
+    attend_head(qkv_ref, pl.multiple_of(head * IN_ROWS, 16), mixed_ref, logsum_ref)
+
+    @pl.when(step == 15)
+    def _():
+        gather_ff.last(1)
+        gather_ff.last(3)
+        gather_ff.forward(2)
+        gather_ff.last(2)
+        for slot in (1, 3, 2):
+            gather_ff.complete(slot)
+        local_ff.wait()
+        out_in.wait()
+        out_bias.wait()
+        gather_in.finish()
+        gather_ff.finish()
+
+
+def attend(first, in_own, ff_own, bias_own):
+    rows, width = first.shape
+    heads = 16
+    anywhere = pl.BlockSpec(memory_space=pl.ANY)
+    dma = pltpu.SemaphoreType.DMA
     return pl.pallas_call(
         attend_kernel,
         grid=(heads,),
-        in_specs=[pl.BlockSpec((144, rows), lambda h: (h, 0))],
+        in_specs=[pl.BlockSpec((rows, width), lambda s: (0, 0)), anywhere, anywhere, anywhere],
         out_specs=[
-            pl.BlockSpec((48, rows), lambda h: (h, 0)),
-            pl.BlockSpec((1, 1, rows), lambda h: (h, 0, 0)),
+            pl.BlockSpec((4 * IN_ROWS, rows), lambda s: (slot_order(s), 0)),
+            pl.BlockSpec((48, rows), lambda s: (slot_order(s) * 4 + s % 4, 0)),
+            pl.BlockSpec((1, 1, rows), lambda s: (slot_order(s) * 4 + s % 4, 0, 0)),
+            anywhere,
+            anywhere,
+            anywhere,
         ],
         out_shape=[
+            jax.ShapeDtypeStruct((heads * IN_ROWS, rows), BF16),
             jax.ShapeDtypeStruct((heads * 48, rows), BF16),
             jax.ShapeDtypeStruct((heads, 1, rows), F32),
+            jax.ShapeDtypeStruct((4, 4, IN_ROWS, width), BF16),
+            jax.ShapeDtypeStruct((4, 8, FF_PIECE, width), BF16),
+            jax.ShapeDtypeStruct((4, 8, 1024), F32),
         ],
-        compiler_params=pltpu.CompilerParams(vmem_limit_bytes=40 << 20),
+        scratch_shapes=[
+            pltpu.VMEM((4, 4, IN_ROWS, width), BF16),
+            pltpu.VMEM((4, 8, 1024), F32),
+            dma((4 * GATHER_KINDS,)),
+            dma((4 * GATHER_KINDS,)),
+            dma((4 * GATHER_KINDS,)),
+            dma((4 * GATHER_KINDS,)),
+            dma((4,)),
+            dma((4,)),
+            dma((5,)),
+        ],
+        compiler_params=pltpu.CompilerParams(
+            vmem_limit_bytes=40 << 20, collective_id=0, has_side_effects=True
+        ),
         cost_estimate=pl.CostEstimate(
-            flops=18_000_000_000, bytes_accessed=9_500_000, transcendentals=19_000_000
+            flops=30_000_000_000, bytes_accessed=30_000_000, transcendentals=19_000_000
         ),
         name="attend",
-    )(qkv)
+    )(first, in_own, ff_own, bias_own)
 
 
 def attend_back_kernel(qkv_ref, back_ref, mixed_ref, logsum_ref, out_ref, held):
@@ -160,16 +455,18 @@
     )(qkv, back_mixed, mixed, logsum)
 
 
-def gather_rows(shard):
-    parts = lax.axis_size("dp")
-    size = shard.shape[0] // parts
-    own = lax.dynamic_slice_in_dim(shard, lax.axis_index("dp") * size, size, 0)
-    return lax.all_gather(own, ALL, axis=0, tiled=True)
+def by_shard(slots):
+    mp = lax.axis_size("mp")
+    blocks = slots.reshape(mp, -1, *slots.shape[1:])
+    twice = jnp.concatenate([blocks, blocks], axis=0)
+    start = lax.rem(mp - lax.axis_index("mp"), mp)
+    return lax.dynamic_slice_in_dim(twice, start, mp, 0).reshape(slots.shape)
 
 
 def reduce_rows(partial):
     dp, mp = lax.axis_size("dp"), lax.axis_size("mp")
     width = partial.shape[1]
+    partial = by_shard(partial)
     blocks = partial.reshape(mp, dp, -1, width).transpose(1, 0, 2, 3).reshape(-1, width)
     summed = lax.psum_scatter(blocks, "dp", scatter_dimension=0, tiled=True)
     summed = lax.psum_scatter(summed, "mp", scatter_dimension=0, tiled=True)
@@ -197,26 +494,31 @@
     width = tokens.shape[1]
     own_heads = project_in.shape[2] // HEAD_DIM
     own_hidden = up_weight.shape[1]
-    shard_in = (
-        project_in.reshape(width, 3, own_heads, HEAD_DIM).transpose(2, 1, 3, 0).reshape(-1, width)
-    )
-    weight_in = gather_rows(shard_in)
-    weight_out = gather_rows(project_out)
-    weight_up = gather_rows(up_weight)
-    weight_down = gather_rows(down_weight)
-    pair_bias = query_value_bias.reshape(2, own_heads, HEAD_DIM)
-    own_bias = jnp.stack([pair_bias[0], jnp.zeros_like(pair_bias[0]), pair_bias[1]], axis=1)
-    biases = lax.all_gather(
-        jnp.concatenate([own_bias.reshape(-1), up_bias])[None], "mp", axis=0, tiled=True
-    )
-    bias_in = biases[:, : 3 * own_heads * HEAD_DIM].reshape(-1, 1).astype(F32)
-    bias_up = biases[:, 3 * own_heads * HEAD_DIM :].astype(F32)
+    in_own = project_in.reshape(width, 3, own_heads, HEAD_DIM).transpose(2, 1, 3, 0)
+    in_own = in_own.reshape(own_heads, IN_ROWS, width)
+    ff_own = jnp.concatenate(
+        [
+            up_weight.reshape(8, -1, width),
+            down_weight.reshape(8, -1, width),
+            project_out.reshape(8, -1, width),
+        ],
+        axis=1,
+    )
+    pair_bias = query_value_bias.astype(F32).reshape(2, own_heads, HEAD_DIM)
+    own_bias = jnp.concatenate([pair_bias[0], jnp.zeros_like(pair_bias[0]), pair_bias[1]], axis=1)
+    bias_own = jnp.zeros((8, 1024), F32)
+    bias_own = lax.dynamic_update_slice(bias_own, own_bias, (0, 0))
+    bias_own = lax.dynamic_update_slice(bias_own, up_bias.astype(F32)[None], (0, 256))
 
     inputs = tokens.astype(F32)
     first_normed, first_pull = jax.vjp(layer_norm, inputs, first_gain, first_shift)
     first = first_normed.astype(BF16)
-    qkv = (nt(weight_in, first) + bias_in).astype(BF16)
-    mixed, logsum = attend(qkv)
+    qkv, mixed, logsum, in_all, ff_all, bias_all = attend(first, in_own, ff_own, bias_own)
+    weight_in = in_all.reshape(-1, width)
+    weight_up = ff_all[:, :, 0:96].reshape(-1, width)
+    weight_down = ff_all[:, :, 96:192].reshape(-1, width)
+    weight_out = ff_all[:, :, 192:216].reshape(-1, width)
+    bias_up = bias_all[:, 0, 256:]
     residual = inputs + tn(mixed, weight_out) + output_bias
     second_normed, second_pull = jax.vjp(layer_norm, residual, second_gain, second_shift)
     second = second_normed.astype(BF16)
@@ -264,7 +566,9 @@
         grad_down_bias,
     ]
     packed = lax.psum(
-        jnp.concatenate(small + [grad_bias_in] + grads_up_bias).reshape(-1, 128), ALL
+        jnp.concatenate(
+            small + [by_shard(grad_bias_in), by_shard(jnp.concatenate(grads_up_bias))]
+        ).reshape(-1, 128), ALL
     ).reshape(-1)
     sums = [packed[i * width : (i + 1) * width] for i in range(len(small))]
     place = lax.axis_index("mp")

time: 697 us -> 645 us (0.925)
  waiting for transfers between devices: 233 us -> 105 us
  matrix products: 174 us -> 221 us
  Pallas kernels: 93.5 us -> 133 us
  blocking collectives: 81.3 us -> 60 us
  other arithmetic: 33.3 us -> 51.9 us
  local copies, waits for them, and re-layouts: 55.9 us -> 47.7 us
    all_gather x4 -> x0, waiting for transfers between devices: 139 us -> none  [gather_rows(): return lax.all_gather(own, ALL, axis=0, tiled=True)]
    dot_general x10, matrix products: 91 us -> 137 us  [nn(): lax.dot_general(left, right, (((1,), (0,)), ((), ())), preferred_element_...]
    pallas_call x1, Pallas kernels: 38 us -> 77.3 us  [attend(): pl.pallas_call(attend_kernel, grid=(heads,), in_specs=[pl.BlockSpec((rows...]
    unnamed x1 -> x0, blocking collectives: 20.4 us -> none
    unnamed x135 -> x177, local copies, waits for them, and re-layouts: 30.3 us -> 13 us
    reduce_scatter x4, waiting for transfers between devices: 60.2 us -> 76 us  [reduce_rows(): summed = lax.psum_scatter(blocks, 'dp', scatter_dimension=0, tiled=True)]
    slice x0 -> x2, local copies, waits for them, and re-layouts: none -> 10.2 us  [the longest x1 6.96 us: local(): down_j = weight_down[j * own_hidden:(j + 1) * own_hidden]]
    concatenate x1 -> x8, other arithmetic: 0.76 us -> 9.83 us  [the longest x5 6.33 us: by_shard(): twice = jnp.concatenate([blocks, blocks], axis=0)]
  transfers between devices with their start and end apart: 14 -> 10, of which waited for: 8 -> 4; matrix products, arithmetic and copies ran while one was open for 25% -> 19% of each run, Pallas kernels for 14% -> 9%
where the time goes in v2:
time: 645 us; the launch traced here: 634 us
  matrix products  221 us (34%)
  Pallas kernels  133 us (21%)
  waiting for transfers between devices  105 us (16%)
  blocking collectives  60 us (9%)
  other arithmetic  51.9 us (8%)
  local copies, waits for them, and re-layouts  47.7 us (7%)
  between operations  15.5 us (2%)
    dot_general x10, matrix products, nn(): lax.dot_general(left, right, (((1,), (0,)), ((), ())), preferred_element_...  137 us
    pallas_call x1, Pallas kernels, attend(): pl.pallas_call(attend_kernel, grid=(heads,), in_specs=[pl.BlockSpec((rows...  77.3 us
    reduce_scatter x4, waiting for transfers between devices, reduce_rows(): summed = lax.psum_scatter(blocks, 'dp', scatter_dimension=0, tiled=True)  76 us
    pallas_call x1, Pallas kernels, attend_back(): pl.pallas_call(attend_back_kernel, grid=(heads,), in_specs=[pl.BlockSpec(...  55.4 us
    dot_general x9, matrix products, nt(): lax.dot_general(left, right, (((1,), (1,)), ((), ())), preferred_element_...  41.9 us
    dot_general x10, matrix products, tn(): lax.dot_general(left, right, (((0,), (0,)), ((), ())), preferred_element_...  41.5 us
    psum x1, blocking collectives, local(): lax.psum(jnp.concatenate(small + [by_shard(grad_bias_in), by_shard(jnp.co...  39.2 us
    all_gather x2, blocking collectives, reduce_rows(): return lax.all_gather(summed, 'dp', axis=0, tiled=True).astype(F32)  20.8 us
  transfers between devices with their start and end apart: 10, of which 4 were waited for; matrix products, arithmetic and copies ran while one was open for 19% of the time, Pallas kernels for 9%

profile of v2, /device:TPU:0, one launch (start us, length us, event | category | flops | bytes accessed | tf_op | source)
XLA Modules:
  0.0 634.2 jit_solution(7044448270424816758)
XLA Ops:
  9.5 2.5 fusion.9
  22.8 77.3 %attend.1 = (bf16[2304,1536]{1,0:T(8,128)(2,1)}, bf16[768,1536]{1,0:T(8,128)(2,1)S(1)}, f32[16,1,1536]{2,1,0:T(1,128)S(1)}, bf16[4,4,144,768]{3,2,1,0:T(8,128)(2...) custom-call(bf16[1536,768]{1,0:T(8,128)(2,1)S(1)} %copy-done.1, bf16[4,144,768]{2,1,0:T(8,128)(2,1)S(1)} %bitcast.106, ...), custom_call_target="tpu_custom_call" | custom-call | flops 30000001024 | bytes 30000000 | tf_op jit(solution)/shard_map/attend/pallas_call | solution.py:362
  100.1 3.3 slice.142
  103.4 7.0 %fusion.67 = (bf16[1,8,96,768]{3,2,1,0:T(8,128)(2,1)}, bf16[1,8,96,768]{3,2,1,0:T(8,128)(2,1)}, bf16[1,8,96,768]{3,2,1,0:T(8,128)(2,1)}, bf16[1,8,96,768]{3,2,1,...) fusion(bf16[4,8,216,768]{3,2,1,0:T(8,128)(2,1)} %get-tuple-elem, ...), kind=kLoop, calls=%fused_computation.198 | loop fusion | bytes 18874368 | tf_op jit(solution)/shard_map/slice | solution.py:533
  110.4 4.8 fusion.69
  120.9 12.9 %multiply_convert_fusion.2 = (bf16[1536,768]{1,0:T(8,128)(2,1)}, f32[1536,768]{1,0:T(8,128)S(1)}, f32[1536,768]{1,0:T(8,128)S(1)}) fusion(f32[768]{0:T(1024)S(1)} %get-tuple-element.37, bf16[1536,768]{1,0:T(8,128)(2,1)S(1)} %add_convert_fusion.4, bf16[768,768]{1,0:T(8,128)(2,1)S(1)} %bitcast.138), kind=kOutput, calls=%fused_computation.78 | convolution fusion | flops 1889796096 | bytes 15338496 | tf_op jit(solution)/shard_map/dot_general | solution.py:42
  133.7 4.8 convert_reduce_fusion.5
  138.5 3.2 convolution_convert_fusion.8
  141.7 30.9 %multiply_convert_fusion.3 = (bf16[1536,768]{1,0:T(8,128)(2,1)S(1)}, f32[1536,768]{1,0:T(8,128)S(1)}, f32[1536,768]{1,0:T(8,128)S(1)}) fusion(f32[768]{0:T(1024)S(1)} %get-tuple-element.38, bf16[1536,768]{1,0:T(8,128)(2,1)S(1)} %add_convert_fusion.4, bf16[768,768]{1,0:T(8,128)(2,1)S(1)} %bitcast.135), kind=kOutput, calls=%fused_computation.91 | convolution fusion | flops 1889796096 | bytes 15338496 | tf_op jit(solution)/shard_map/dot_general | solution.py:42
  172.6 4.8 convert_reduce_fusion.6
  177.5 3.2 convolution_convert_fusion.9
  180.6 30.9 %multiply_convert_fusion.1 = (bf16[1536,768]{1,0:T(8,128)(2,1)S(1)}, f32[1536,768]{1,0:T(8,128)S(1)}, f32[1536,768]{1,0:T(8,128)S(1)}) fusion(f32[768]{0:T(1024)S(1)} %get-tuple-element.36, bf16[1536,768]{1,0:T(8,128)(2,1)S(1)} %add_convert_fusion.4, bf16[768,768]{1,0:T(8,128)(2,1)S(1)} %bitcast.133), kind=kOutput, calls=%fused_computation.65 | convolution fusion | flops 1889796096 | bytes 15338496 | tf_op jit(solution)/shard_map/dot_general | solution.py:42
  211.6 5.0 convert_reduce_fusion.4
  216.6 3.1 convolution_convert_fusion.7
  219.7 30.9 %multiply_convert_fusion = (bf16[1536,768]{1,0:T(8,128)(2,1)S(1)}, f32[1536,768]{1,0:T(8,128)S(1)}, f32[1536,768]{1,0:T(8,128)S(1)}) fusion(f32[768]{0:T(1024)S(1)} %copy-done.66, bf16[1536,768]{1,0:T(8,128)(2,1)S(1)} %add_convert_fusion.4, bf16[768,768]{1,0:T(8,128)(2,1)S(1)} %bitcast.118), kind=kOutput, calls=%fused_computation.52 | convolution fusion | flops 1889796096 | bytes 15338496 | tf_op jit(solution)/shard_map/dot_general | solution.py:42
  250.6 4.8 convert_reduce_fusion.3
  255.4 3.1 convolution_convert_fusion.6
  258.5 3.3 convolution_convert_fusion.2
  261.8 3.4 convolution_convert_fusion.5
  265.2 3.3 convolution_convert_fusion.4
  268.5 3.3 convolution_convert_fusion.3
  271.8 4.0 pad_maximum_fusion
  276.6 4.6 fusion.16
  281.2 2.6 copy.38
  283.8 4.9 copy.39
  288.8 4.6 fusion.74
  295.8 4.2 fusion.75
  300.0 5.9 multiply_reduce_fusion
  312.7 5.8 convolution_convert_fusion.1.back_ref
  318.5 55.4 %attend_back.1 = bf16[2304,1536]{1,0:T(8,128)(2,1)S(1)} custom-call(bf16[2304,1536]{1,0:T(8,128)(2,1)} %get-tuple-element.23.qkv_ref, bf16[768,1536]{1,0:T(8,128)(2,1)S(1)} %convolution_convert_fusion.1.back_ref, bf16[768,1536]{1,0:T(8,128)(2,1)S(1)} %copy-done.8, f32[16,1,1536]{2,1,0:T(1,128)S(1)} %copy-done.10), custom_call_target="tpu_custom_call" | custom-call | flops 40000000000 | bytes 19000000 | tf_op jit(solution)/shard_map/attend_back/pallas_call | solution.py:438
  373.9 5.9 convolution_convert_fusion
  386.3 10.8 %fusion.61 = (f32[768]{0:T(1024)}, f32[1536]{0:T(1024)}, f32[1536,768]{1,0:T(8,128)}) fusion(f32[768]{0:T(1024)S(1)} %copy-done.55, f32[1536]{0:T(1024)S(1)} %copy-done.39, bf16[1536,768]{1,0:T(8,128)(2,1)} %param.15, bf16[2304,1536]{1,0:T(8,128)(2,1)} %copy-done, bf16[2304,768]{1,0:T(8,128)(2,1)S(1)} %bitcast.107), kind=kOutput, calls=%fused_computation.196 | convolution fusion | flops 5442893312 | bytes 17713152 | tf_op jit(solution)/shard_map/dot_general | solution.py:54
  397.4 4.2 convert_reduce_fusion
  402.3 3.9 fusion.8
  407.6 26.1 %reduce-scatter.13.cloned.1.call-done = bf16[96,768]{1,0:T(8,128)(2,1)} async-done(((bf16[768,768]{1,0:T(8,128)(2,1)}), bf16[96,768]{1,0:T(8,128)(2,1)}) %reduce-scatter.13.cloned.1.call-update) | async-done | bytes 147472 | tf_op jit(solution)/shard_map/reduce_scatter | solution.py:471
  435.7 49.9 %reduce-scatter.9.cloned.1.call-done = bf16[288,768]{1,0:T(8,128)(2,1)} async-done(((bf16[2304,768]{1,0:T(8,128)(2,1)}), bf16[288,768]{1,0:T(8,128)(2,1)}) %reduce-scatter.9.cloned.1.call-update) | async-done | bytes 442384 | tf_op jit(solution)/shard_map/reduce_scatter | solution.py:471
  485.6 9.3 %convert_reduce_fusion.2 = (f32[768]{0:T(1024)}, f32[768]{0:T(1024)S(1)}, f32[1536,768]{1,0:T(8,128)}) fusion(bf16[1536,768]{1,0:T(8,128)(2,1)} %param.16, pred[1536]{0:T(1024)(128)(4,1)} %copy-done.60, f32[1536,768]{1,0:T(8,128)} %copy-done.15, f32[1536]{0:T(1024)} %copy-done.59, f32[1536]{0:T(1024)} %negate_multiply_fusion.4, f32[1536]{0:T(1024)} %copy-done.51, ...), kind=kLoop, calls=%fused_computation.20 | loop fusion | flops 17693184 | bytes 18915840 | tf_op jit(solution)/shard_map/reduce_sum | solution.py:546
  496.3 13.4 %reduce-scatter.19.cloned.1.call-done = bf16[96,768]{1,0:T(8,128)(2,1)} async-done(((bf16[384,768]{1,0:T(8,128)(2,1)}), bf16[96,768]{1,0:T(8,128)(2,1)}) %reduce-scatter.19.cloned.1.call-update) | async-done | bytes 147472 | tf_op jit(solution)/shard_map/reduce_scatter | solution.py:472
  516.5 39.2 %psum.7 = f32[78,128]{1,0:T(8,128)S(1)} all-reduce(f32[78,128]{1,0:T(8,128)} %bitcast.148), channel_id=1, replica_groups=mesh['dp'=8,'mp'=4] {'mp','dp'}, use_global_device_ids=true, to_apply=%region_19.20 | all-reduce | flops 9984 | bytes 79872 | tf_op jit(solution)/shard_map/psum | solution.py:568
  556.0 6.0 fusion.70
  562.0 4.2 fusion.71
  566.3 4.3 fusion.72
  574.0 9.2 %select_convert_fusion = bf16[1536,768]{1,0:T(8,128)(2,1)} fusion(f32[1536,768]{1,0:T(8,128)} %fusion.72, f32[1536,768]{1,0:T(8,128)} %fusion.71, f32[1536,768]{1,0:T(8,128)} %fusion.70, f32[1536,768]{1,0:T(8,128)} %copy-done.11, bf16[1536,768]{1,0:T(8,128)(2,1)S(1)} %copy-done.22, bf16[768,768]{1,0:T(8,128)(2,1)S(1)} %bitcast.123, f32[768]{0:T(1024)S(1)} %copy-done.68, ...), kind=kOutput, calls=%fused_computation.51 | convolution fusion | flops 1820196864 | bytes 24777216 | tf_op jit(solution)/shard_map/dot_general | solution.py:42
  583.2 10.2 %all_gather.13 = bf16[192,768]{1,0:T(8,128)(2,1)S(1)} all-gather(bf16[24,768]{1,0:T(8,128)(2,1)} %reduce-scatter.15.cloned.1.call-done), channel_id=1, replica_groups=mesh['dp'=8,'mp'=4] {'dp'}, dimensions={0}, use_global_device_ids=true | all-gather | bytes 331776 | tf_op jit(solution)/shard_map/all_gather | solution.py:473
  594.2 10.6 %all_gather.12 = bf16[576,768]{1,0:T(8,128)(2,1)S(1)} all-gather(bf16[72,768]{1,0:T(8,128)(2,1)} %reduce-scatter.11.cloned.1.call-done), channel_id=1, replica_groups=mesh['dp'=8,'mp'=4] {'dp'}, dimensions={0}, use_global_device_ids=true | all-gather | bytes 995328 | tf_op jit(solution)/shard_map/all_gather | solution.py:473
  606.4 2.9 convert_element_type.133
  609.2 15.1 %all-gather.5.cloned.1.call-done = bf16[768,768]{1,0:T(8,128)(2,1)} async-done(((bf16[96,768]{1,0:T(8,128)(2,1)}), bf16[768,768]{1,0:T(8,128)(2,1)}) %all-gather.5.cloned.1.call-update) | async-done | bytes 1179664 | tf_op jit(solution)/shard_map/all_gather | solution.py:473
  624.3 2.8 convert_element_type.138
  (259 shorter events, 53.1 us)
Async XLA Ops:
  7.2 7.6 %copy-start.12 = (bf16[1536,768]{1,0:T(8,128)(2,1)S(1)}, bf16[1536,768]{1,0:T(8,128)(2,1)}, u32[]{:S(2)}) copy-start(bf16[1536,768]{1,0:T(8,128)(2,1)} %param.15) | copy-start | bytes 7077892
  7.2 6.4 %copy-start.69 = (bf16[768]{0:T(1024)(128)(2,1)S(1)}, bf16[768]{0:T(1024)(128)(2,1)}, u32[]{:S(2)}) copy-start(bf16[768]{0:T(1024)(128)(2,1)} %param.27) | copy-start | bytes 4612
  7.2 7.6 %copy-start.54 = (f32[768]{0:T(1024)S(1)}, f32[768]{0:T(1024)}, u32[]{:S(2)}) copy-start(f32[768]{0:T(1024)} %param.18) | copy-start | bytes 9220
  7.2 7.6 %copy-start.63 = (f32[768]{0:T(1024)S(1)}, f32[768]{0:T(1024)}, u32[]{:S(2)}) copy-start(f32[768]{0:T(1024)} %param.19) | copy-start | bytes 9220
  7.2 379.0 %reduce-scatter.17.cloned.1.call-start = ((), (), s32[]{:S(2)}) async-start(), calls=%async_computation.12 | async-start | bytes 5308416 | tf_op jit(solution)/shard_map/reduce_scatter | solution.py:471
  9.5 7.6 %copy-start.38 = (f32[1536]{0:T(1024)}, f32[1536]{0:T(1024)S(1)}, u32[]{:S(2)}) copy-start(f32[1536]{0:T(1024)S(1)} %broadcast_multiply_fusion.1) | copy-start | bytes 18436
  100.1 10.3 %copy-start.4 = (f32[4,8,1024]{2,1,0:T(8,128)}, f32[4,8,1024]{2,1,0:T(8,128)S(1)}, u32[]{:S(2)}) copy-start(f32[4,8,1024]{2,1,0:T(8,128)S(1)} %get-tuple-element.22) | copy-start | bytes 393220
  100.1 10.3 %copy-start.5 = (bf16[4,4,144,768]{3,2,1,0:T(8,128)(2,1)}, bf16[4,4,144,768]{3,2,1,0:T(8,128)(2,1)S(1)}, u32[]{:S(2)}) copy-start(bf16[4,4,144,768]{3,2,1,0:T(8,128)(2,1)S(1)} %get-tuple-element.25) | copy-start | bytes 10616836
  100.1 10.3 %copy-start.7 = (bf16[768,1536]{1,0:T(8,128)(2,1)}, bf16[768,1536]{1,0:T(8,128)(2,1)S(1)}, u32[]{:S(2)}) copy-start(bf16[768,1536]{1,0:T(8,128)(2,1)S(1)} %get-tuple-element.20.mixed_ref) | copy-start | bytes 7077892
  100.1 10.3 %copy-start.9 = (f32[16,1,1536]{2,1,0:T(1,128)}, f32[16,1,1536]{2,1,0:T(1,128)S(1)}, u32[]{:S(2)}) copy-start(f32[16,1,1536]{2,1,0:T(1,128)S(1)} %get-tuple-element.24.logsum_ref) | copy-start | bytes 294916
  103.4 7.0 %copy-start.13 = (bf16[1536,768]{1,0:T(8,128)(2,1)S(1)}, bf16[1536,768]{1,0:T(8,128)(2,1)}, u32[]{:S(2)}) copy-start(bf16[1536,768]{1,0:T(8,128)(2,1)} %param.15) | copy-start | bytes 7077892
  103.4 7.0 %copy-start.72 = (f32[768]{0:T(1024)S(1)}, f32[768]{0:T(1024)}, u32[]{:S(2)}) copy-start(f32[768]{0:T(1024)} %param.23) | copy-start | bytes 9220
  110.4 23.3 %copy-start.25 = (bf16[1,8,96,768]{3,2,1,0:T(8,128)(2,1)}, bf16[1,8,96,768]{3,2,1,0:T(8,128)(2,1)S(1)}, u32[]{:S(2)}) copy-start(bf16[1,8,96,768]{3,2,1,0:T(8,128)(2,1)S(1)} %get-tuple-element.57) | copy-start | bytes 3538948
  116.0 17.7 %copy-start.49 = (f32[1536]{0:T(1024)}, f32[1536]{0:T(1024)S(1)}, u32[]{:S(2)}) copy-start(f32[1536]{0:T(1024)S(1)} %multiply_reduce_fusion.2) | copy-start | bytes 18436
  116.0 17.7 %copy-start.45 = (f32[1536]{0:T(1024)}, f32[1536]{0:T(1024)S(1)}, u32[]{:S(2)}) copy-start(f32[1536]{0:T(1024)S(1)} %fusion.54) | copy-start | bytes 18436
  119.7 192.9 %copy-start.60 = (pred[1536]{0:T(1024)(128)(4,1)}, pred[1536]{0:T(1024)(128)(4,1)S(1)}, u32[]{:S(2)}) copy-start(pred[1536]{0:T(1024)(128)(4,1)S(1)} %fusion.50) | copy-start | bytes 4612
  120.9 12.9 %copy-start.19 = (bf16[1536,768]{1,0:T(8,128)(2,1)S(1)}, bf16[1536,768]{1,0:T(8,128)(2,1)}, u32[]{:S(2)}) copy-start(bf16[1536,768]{1,0:T(8,128)(2,1)} %param.16) | copy-start | bytes 7077892
  138.5 34.1 %copy-start.73 = (bf16[1536,768]{1,0:T(8,128)(2,1)}, bf16[1536,768]{1,0:T(8,128)(2,1)S(1)}, u32[]{:S(2)}) copy-start(bf16[1536,768]{1,0:T(8,128)(2,1)S(1)} %get-tuple-element.83) | copy-start | bytes 7077892
  141.7 30.9 %copy-start.27 = (bf16[1,8,96,768]{3,2,1,0:T(8,128)(2,1)S(1)}, bf16[1,8,96,768]{3,2,1,0:T(8,128)(2,1)}, u32[]{:S(2)}) copy-start(bf16[1,8,96,768]{3,2,1,0:T(8,128)(2,1)} %get-tuple-element.59) | copy-start | bytes 3538948
  172.6 89.2 %copy-start.80 = (bf16[1536,768]{1,0:T(8,128)(2,1)}, bf16[1536,768]{1,0:T(8,128)(2,1)S(1)}, u32[]{:S(2)}) copy-start(bf16[1536,768]{1,0:T(8,128)(2,1)S(1)} %get-tuple-element.47) | copy-start | bytes 7077892
  177.5 34.1 %copy-start.74 = (bf16[1536,768]{1,0:T(8,128)(2,1)}, bf16[1536,768]{1,0:T(8,128)(2,1)S(1)}, u32[]{:S(2)}) copy-start(bf16[1536,768]{1,0:T(8,128)(2,1)S(1)} %get-tuple-element.85) | copy-start | bytes 7077892
  180.6 30.9 %copy-start.23 = (bf16[1,8,96,768]{3,2,1,0:T(8,128)(2,1)S(1)}, bf16[1,8,96,768]{3,2,1,0:T(8,128)(2,1)}, u32[]{:S(2)}) copy-start(bf16[1,8,96,768]{3,2,1,0:T(8,128)(2,1)} %get-tuple-element.55) | copy-start | bytes 3538948
  211.5 57.0 %copy-start.81 = (bf16[1536,768]{1,0:T(8,128)(2,1)}, bf16[1536,768]{1,0:T(8,128)(2,1)S(1)}, u32[]{:S(2)}) copy-start(bf16[1536,768]{1,0:T(8,128)(2,1)S(1)} %get-tuple-element.51) | copy-start | bytes 7077892
  216.6 34.0 %copy-start.76 = (bf16[1536,768]{1,0:T(8,128)(2,1)}, bf16[1536,768]{1,0:T(8,128)(2,1)S(1)}, u32[]{:S(2)}) copy-start(bf16[1536,768]{1,0:T(8,128)(2,1)S(1)} %get-tuple-element.81) | copy-start | bytes 7077892
  219.7 30.9 %copy-start.17 = (bf16[1,8,96,768]{3,2,1,0:T(8,128)(2,1)S(1)}, bf16[1,8,96,768]{3,2,1,0:T(8,128)(2,1)}, u32[]{:S(2)}) copy-start(bf16[1,8,96,768]{3,2,1,0:T(8,128)(2,1)} %get-tuple-element.53) | copy-start | bytes 3538948
  250.6 7.9 %copy-start.21 = (bf16[1536,768]{1,0:T(8,128)(2,1)}, bf16[1536,768]{1,0:T(8,128)(2,1)S(1)}, u32[]{:S(2)}) copy-start(bf16[1536,768]{1,0:T(8,128)(2,1)S(1)} %get-tuple-element.45) | copy-start | bytes 7077892
  283.8 113.4 %reduce-scatter.21.cloned.1.call-start = ((), (), s32[]{:S(2)}) async-start(), calls=%async_computation.15 | async-start | bytes 5308416 | tf_op jit(solution)/shard_map/reduce_scatter | solution.py:471
  288.8 144.9 %reduce-scatter.13.cloned.1.call-start = ((), (), s32[]{:S(2)}) async-start(), calls=%async_computation.10 | async-start | bytes 1327104 | tf_op jit(solution)/shard_map/reduce_scatter | solution.py:471
  293.5 6.5 %slice-start = ((s8[4718592]{0:T(1024)(128)(4,1)}), s8[4194304]{0:T(1024)(128)(4,1)S(1)}, s32[]{:S(2)}) async-start(s8[4718592]{0:T(1024)(128)(4,1)} %bitcast.108), calls=%async_computation.18 | async-start | bytes 8388608
  312.1 6.3 copy-start.10
  312.1 173.4 %reduce-scatter.9.cloned.1.call-start = ((), (), s32[]{:S(2)}) async-start(), calls=%async_computation.8 | async-start | bytes 3981312 | tf_op jit(solution)/shard_map/reduce_scatter | solution.py:471
  318.5 55.5 %copy-start.2 = (bf16[1536,768]{1,0:T(8,128)(2,1)S(1)}, bf16[1536,768]{1,0:T(8,128)(2,1)}, u32[]{:S(2)}) copy-start(bf16[1536,768]{1,0:T(8,128)(2,1)} %fusion.7.first_ref) | copy-start | bytes 7077892
  383.3 126.4 %reduce-scatter.19.cloned.1.call-start = ((), (), s32[]{:S(2)}) async-start(), calls=%async_computation.13 | async-start | bytes 737280 | tf_op jit(solution)/shard_map/reduce_scatter | solution.py:472
  386.2 184.4 %reduce-scatter.23.cloned.1.call-start = ((), (), s32[]{:S(2)}) async-start(), calls=%async_computation.16 | async-start | bytes 737280 | tf_op jit(solution)/shard_map/reduce_scatter | solution.py:472
  397.2 186.0 %reduce-scatter.15.cloned.1.call-start = ((), (), s32[]{:S(2)}) async-start(), calls=%async_computation.11 | async-start | bytes 184320 | tf_op jit(solution)/shard_map/reduce_scatter | solution.py:472
  401.6 32.2 %copy-start.67 = (f32[768]{0:T(1024)S(1)}, f32[768]{0:T(1024)}, u32[]{:S(2)}) copy-start(f32[768]{0:T(1024)} %get-tuple-element.31) | copy-start | bytes 9220
  402.3 83.2 %copy-start.51 = (f32[1536]{0:T(1024)}, f32[1536]{0:T(1024)S(1)}, u32[]{:S(2)}) copy-start(f32[1536]{0:T(1024)S(1)} %multiply_multiply_fusion.20) | copy-start | bytes 18436
  433.7 160.5 %reduce-scatter.11.cloned.1.call-start = ((), (), s32[]{:S(2)}) async-start(), calls=%async_computation.9 | async-start | bytes 552960 | tf_op jit(solution)/shard_map/reduce_scatter | solution.py:472
  485.6 70.4 %copy-start.28 = (bf16[1,8,96,768]{3,2,1,0:T(8,128)(2,1)S(1)}, bf16[1,8,96,768]{3,2,1,0:T(8,128)(2,1)}, u32[]{:S(2)}) copy-start(bf16[1,8,96,768]{3,2,1,0:T(8,128)(2,1)} %get-tuple-element.59) | copy-start | bytes 3538948
  485.6 120.8 %all-gather.3.cloned.1.call-start = ((), (), s32[]{:S(2)}) async-start(), calls=%async_computation.14 | async-start | bytes 1327104 | tf_op jit(solution)/shard_map/all_gather | solution.py:473
  485.6 10.7 %copy-start.53 = (f32[4,576]{1,0:T(4,128)S(1)}, f32[4,576]{1,0:T(4,128)}, u32[]{:S(2)}) copy-start(f32[4,576]{1,0:T(4,128)} %reshape.290) | copy-start | bytes 27652
  485.6 10.7 %copy-start.52 = (f32[4,768]{1,0:T(4,128)S(1)}, f32[4,768]{1,0:T(4,128)}, u32[]{:S(2)}) copy-start(f32[4,768]{1,0:T(4,128)} %reshape.292) | copy-start | bytes 36868
  509.7 114.6 %all-gather.5.cloned.1.call-start = ((), (), s32[]{:S(2)}) async-start(), calls=%async_computation.17 | async-start | bytes 1327104 | tf_op jit(solution)/shard_map/all_gather | solution.py:473
  555.6 6.4 %copy-start.42 = (f32[78,128]{1,0:T(8,128)}, f32[78,128]{1,0:T(8,128)S(1)}, u32[]{:S(2)}) copy-start(f32[78,128]{1,0:T(8,128)S(1)} %psum.7) | copy-start | bytes 119812
  566.3 7.7 %copy-start.18 = (bf16[1,8,96,768]{3,2,1,0:T(8,128)(2,1)S(1)}, bf16[1,8,96,768]{3,2,1,0:T(8,128)(2,1)}, u32[]{:S(2)}) copy-start(bf16[1,8,96,768]{3,2,1,0:T(8,128)(2,1)} %get-tuple-element.53) | copy-start | bytes 3538948
  566.3 7.7 %copy-start.22 = (bf16[1536,768]{1,0:T(8,128)(2,1)S(1)}, bf16[1536,768]{1,0:T(8,128)(2,1)}, u32[]{:S(2)}) copy-start(bf16[1536,768]{1,0:T(8,128)(2,1)} %copy-done.21) | copy-start | bytes 7077892
  566.3 7.7 %copy-start.61 = (pred[1536]{0:T(1024)(128)(4,1)S(1)}, pred[1536]{0:T(1024)(128)(4,1)}, u32[]{:S(2)}) copy-start(pred[1536]{0:T(1024)(128)(4,1)} %copy-done.60) | copy-start | bytes 4612
  566.3 7.7 %copy-start.68 = (f32[768]{0:T(1024)S(1)}, f32[768]{0:T(1024)}, u32[]{:S(2)}) copy-start(f32[768]{0:T(1024)} %param.29) | copy-start | bytes 9220
  (47 other events, 190.4 us)
Sparse Core Ops, SparseCore 0:
  283.9 51.3 reduce-scatter.16
  339.1 53.8 reduce-scatter.20
  396.9 36.7 reduce-scatter.12
  437.4 48.0 reduce-scatter.8
  487.8 21.9 reduce-scatter.18
  512.0 20.3 reduce-scatter.22
  534.7 17.6 reduce-scatter.14
  554.7 19.1 reduce-scatter.10
  576.0 22.3 all-gather.2
  600.2 24.0 all-gather.4

commit v3 on v2

--- a/solution.py
+++ b/solution.py
@@ -19,7 +19,6 @@
 )
 SCALE = HEAD_DIM**-0.5
 SCALE_LOG2 = SCALE * math.log2(math.e)
-ALL = ("mp", "dp")
 BF16 = jnp.bfloat16
 F32 = jnp.float32
 CHUNK = 512
@@ -34,10 +33,6 @@
     return centred * lax.rsqrt(variance + epsilon) * norm_gain + norm_shift
 
 
-def gelu_exact(values):
-    return jax.nn.gelu(values, approximate=False)
-
-
 def nn(left, right):
     return lax.dot_general(
         left, right, (((1,), (0,)), ((), ())), preferred_element_type=F32
@@ -56,19 +51,10 @@
     )
 
 
-def live_mask(live_images, total_rows):
-    row_index = lax.broadcasted_iota(jnp.int32, (total_rows, 1), 0)
-    short_slot = row_index // SHORT_LEN
-    long_slot = (row_index - SHORT_ROWS) // LONG_LEN
-    return jnp.where(
-        row_index < SHORT_ROWS, short_slot < live_images[0, 0], long_slot < live_images[0, 1]
-    )
-
-
 GROUP = 8
 MESH = pl.DeviceIdType.MESH
 IN_ROWS = 144
-FF_PIECE = 216
+HEAD_ROWS = 192
 
 
 def place():
@@ -114,19 +100,25 @@
             dst = self.view(buffer, *mine)
             device = (self.dp, lax.rem(self.mp + ways - hop, ways))
         else:
-            near_x, near_y = (y, flip(x), core), (flip(y), x, core)
-            src, device = {
-                1: (self.view(buffer, *mine), near_x),
-                2: (self.view(buffer, *mine), near_y),
-                3: (self.view(buffer, *near_x, 0), near_y),
-                4: (self.view(buffer, *near_y, 1), near_x),
-                5: (self.view(buffer, *mine), (y, x, flip(core))),
-                6: (self.view(buffer, *near_x), (y, x, flip(core))),
-                7: (self.view(buffer, *near_y), (y, x, flip(core))),
-                8: (self.view(buffer, flip(y), flip(x), core), (y, x, flip(core))),
-            }[kind]
-            dst, device = src, self.device(*device)
-        index = kind * 4 + slot
+            return self.shared(kind, buffer, kind * 4 + slot)
+        return self.remote(src, dst, device, kind * 4 + slot)
+
+    def shared(self, kind, buffer, index):
+        y, x, core = self.y, self.x, self.core
+        mine, near_x, near_y = (y, x, core), (y, flip(x), core), (flip(y), x, core)
+        moved, device = {
+            1: lambda: (self.view(buffer, *mine), near_x),
+            2: lambda: (self.view(buffer, *mine), near_y),
+            3: lambda: (self.view(buffer, *near_x, 0), near_y),
+            4: lambda: (self.view(buffer, *near_y, 1), near_x),
+            5: lambda: (self.view(buffer, *mine), (y, x, flip(core))),
+            6: lambda: (self.view(buffer, *near_x), (y, x, flip(core))),
+            7: lambda: (self.view(buffer, *near_y), (y, x, flip(core))),
+            8: lambda: (self.view(buffer, flip(y), flip(x), core), (y, x, flip(core))),
+        }[kind]()
+        return self.remote(moved, moved, self.device(*device), index)
+
+    def remote(self, src, dst, device, index):
         return pltpu.make_async_remote_copy(
             src_ref=src,
             dst_ref=dst,
@@ -236,8 +228,8 @@
     step = pl.program_id(0)
     dp, base, y, x, core, mp = place()
     ways = lax.axis_size("mp")
-    gather_in = Gather(in_own, in_all, in_piece, 64, in_send, in_recv)
-    gather_ff = Gather(ff_own, ff_all, ff_piece, 112, ff_send, ff_recv)
+    gather_in = Gather(in_own, in_all, in_piece, 96, in_send, in_recv)
+    gather_ff = Gather(ff_own, ff_all, ff_piece, 96, ff_send, ff_recv)
     local_in = pltpu.make_async_copy(in_own, in_all.at[0], local_sem.at[0])
     local_bias = pltpu.make_async_copy(bias_own, bias_all.at[0], local_sem.at[1])
     local_ff = pltpu.make_async_copy(ff_own, ff_all.at[0], local_sem.at[2])
@@ -332,7 +324,7 @@
     def _():
         bias_t = bias_all[slot, :, 0:256].T
         for part in range(4):
-            product = nt(in_all[slot, part], first_ref[...])
+            product = nt(in_all[slot, part, :IN_ROWS], first_ref[...])
             qkv_ref[part * IN_ROWS : (part + 1) * IN_ROWS, :] = (
                 product + bias_t[:IN_ROWS, part : part + 1]
             ).astype(BF16)
@@ -375,12 +367,12 @@
             jax.ShapeDtypeStruct((heads * IN_ROWS, rows), BF16),
             jax.ShapeDtypeStruct((heads * 48, rows), BF16),
             jax.ShapeDtypeStruct((heads, 1, rows), F32),
-            jax.ShapeDtypeStruct((4, 4, IN_ROWS, width), BF16),
-            jax.ShapeDtypeStruct((4, 8, FF_PIECE, width), BF16),
+            jax.ShapeDtypeStruct((4, 4, HEAD_ROWS, width), BF16),
+            jax.ShapeDtypeStruct((4, 8, 192, width), BF16),
             jax.ShapeDtypeStruct((4, 8, 1024), F32),
         ],
         scratch_shapes=[
-            pltpu.VMEM((4, 4, IN_ROWS, width), BF16),
+            pltpu.VMEM((4, 4, HEAD_ROWS, width), BF16),
             pltpu.VMEM((4, 8, 1024), F32),
             dma((4 * GATHER_KINDS,)),
             dma((4 * GATHER_KINDS,)),
@@ -400,17 +392,222 @@
     )(first, in_own, ff_own, bias_own)
 
 
-def attend_back_kernel(qkv_ref, back_ref, mixed_ref, logsum_ref, out_ref, held):
+class Reduce:
+    def __init__(self, slot, other, total, got, split, send, recv):
+        self.slot, self.other, self.total, self.got, self.split = slot, other, total, got, split
+        self.send, self.recv = send, recv
+        self.dp, self.base, self.y, self.x, self.core, self.mp = place()
+
+    def copy(self, kind):
+        y, x, core = self.y, self.x, self.core
+        first, late = pl.ds(0, self.split), pl.ds(self.split, self.total.shape[2] - self.split)
+        got = self.got
+        near = lambda y, x, core: (self.base + 4 * y + 2 * x + core, self.mp)
+        to_x, to_y = near(y, flip(x), core), near(flip(y), x, core)
+        src, dst, device = {
+            0: lambda: (self.other, got[0], near(y, x, flip(core))),
+            1: lambda: (self.total.at[:, flip(x), first], got[1], to_x),
+            2: lambda: (self.total.at[flip(y), :, late], got[2], to_y),
+            3: lambda: (self.total.at[flip(y), x, first], got[3], to_y),
+            4: lambda: (self.total.at[y, flip(x), late], got[4], to_x),
+            5: lambda: (
+                self.total.at[y, x],
+                got[5],
+                (self.dp, lax.rem(self.mp + self.slot, lax.axis_size("mp"))),
+            ),
+        }[kind]()
+        index = kind * 4 + self.slot
+        return pltpu.make_async_remote_copy(
+            src_ref=src,
+            dst_ref=dst,
+            send_sem=self.send.at[index],
+            recv_sem=self.recv.at[index],
+            device_id=device,
+            device_id_type=MESH,
+        )
+
+    def cores(self):
+        self.copy(0).start()
+
+    def chips(self):
+        self.copy(0).wait_recv()
+        for y in range(2):
+            for x in range(2):
+                self.total[y, x] = add(self.total[y, x], self.got[0][y, x])
+        self.copy(1).start()
+        self.copy(2).start()
+
+    def chips_again(self):
+        x, y, split = self.x, self.y, self.split
+        self.copy(1).wait_recv()
+        for i in range(2):
+            self.total[i, x, :split] = add(self.total[i, x, :split], self.got[1][i])
+        self.copy(2).wait_recv()
+        for i in range(2):
+            self.total[y, i, split:] = add(self.total[y, i, split:], self.got[2][i])
+        self.copy(3).start()
+        self.copy(4).start()
+
+    def along(self):
+        x, y, split = self.x, self.y, self.split
+        self.copy(3).wait_recv()
+        self.total[y, x, :split] = add(self.total[y, x, :split], self.got[3][...])
+        self.copy(4).wait_recv()
+        self.total[y, x, split:] = add(self.total[y, x, split:], self.got[4][...])
+        if self.slot:
+            self.copy(5).start()
+
+    def arrived(self):
+        self.copy(5).wait_recv()
+
+    def finish(self):
+        for kind in range(6 if self.slot else 5):
+            self.copy(kind).wait_send()
+
+
+REDUCE_KINDS = 6
+
+
+def add(left, right):
+    return (left.astype(F32) + right.astype(F32)).astype(BF16)
+
+
+def other_bit(index, bit):
+    return index + bit * (1 - 2 * lax.rem(index // bit, 2))
+
+
+def wider_bits():
+    bits, bit = [], GROUP
+    while bit < lax.axis_size("dp"):
+        bits.append(bit)
+        bit *= 2
+    return bits
+
+
+class Share:
+    def __init__(self, pieces, split, send, recv):
+        self.inner = Gather(None, None, ff_piece, split, send, recv)
+        self.inner.buffer = pieces
+
+    def copy(self, kind):
+        return self.inner.shared(kind, self.inner.buffer, kind)
+
+    def start(self, *kinds):
+        for kind in kinds:
+            self.copy(kind).start()
+
+    def arrived(self, *kinds):
+        for kind in kinds:
+            self.copy(kind).wait_recv()
+
+    def spread(self):
+        self.start(1, 2, 5)
+
+    def forward(self):
+        self.arrived(1)
+        self.start(3, 6)
+        self.arrived(2)
+        self.start(4, 7)
+
+    def last(self):
+        self.arrived(3, 4)
+        self.start(8)
+
+    def finish(self):
+        self.arrived(5, 6, 7, 8)
+        for kind in range(1, 9):
+            self.copy(kind).wait_send()
+
+
+class Total:
+    def __init__(self, reduces, arrivals, final, wide, wide_send, wide_recv):
+        self.reduces, self.arrivals, self.final = reduces, arrivals, final
+        self.wide, self.wide_send, self.wide_recv = wide, wide_send, wide_recv
+
+    def copy(self, i, bit):
+        dp, mp = lax.axis_index("dp"), lax.axis_index("mp")
+        return pltpu.make_async_remote_copy(
+            src_ref=self.wide.at[2 * i],
+            dst_ref=self.wide.at[2 * i + 1],
+            send_sem=self.wide_send.at[i],
+            recv_sem=self.wide_recv.at[i],
+            device_id=(other_bit(dp, bit), mp),
+            device_id_type=MESH,
+        )
+
+    def sum(self):
+        own = self.reduces[0]
+        total = own.total[own.y, own.x].astype(F32)
+        for k in (1, 2, 3):
+            self.reduces[k].arrived()
+            total = total + self.arrivals[k - 1].astype(F32)
+        for i, bit in enumerate(wider_bits()):
+            self.wide[2 * i] = total.astype(BF16)
+            self.copy(i, bit).start()
+            self.copy(i, bit).wait()
+            total = total + self.wide[2 * i + 1].astype(F32)
+        self.final[4 * own.y + 2 * own.x + own.core] = total.astype(BF16)
+
+
+def group_partners():
+    dp, base, y, x, core, mp = place()
+    ways = lax.axis_size("mp")
+    return (
+        [(dp, lax.rem(mp + k, ways)) for k in (1, 2, 3)]
+        + [
+            (base + 4 * y + 2 * flip(x) + core, mp),
+            (base + 4 * flip(y) + 2 * x + core, mp),
+            (base + 4 * y + 2 * x + flip(core), mp),
+        ]
+        + [(other_bit(dp, bit), mp) for bit in wider_bits()]
+    )
+
+
+def reduce_refs(scratch, slot):
+    r1, r2a, r2b, r3a, r3b, r4 = scratch
+    return [
+        r1.at[slot],
+        r2a.at[slot],
+        r2b.at[slot],
+        r3a.at[slot],
+        r3b.at[slot],
+        r4.at[max(slot - 1, 0)],
+    ]
+
+
+def reduce_scratch(rows, split, width):
+    late = rows - split
+    dma = pltpu.SemaphoreType.DMA
+    wide = 6
+    return [
+        pltpu.VMEM((4, 2, 2, rows, width), BF16),
+        pltpu.VMEM((4, 2, split, width), BF16),
+        pltpu.VMEM((4, 2, late, width), BF16),
+        pltpu.VMEM((4, split, width), BF16),
+        pltpu.VMEM((4, late, width), BF16),
+        pltpu.VMEM((3, rows, width), BF16),
+        pltpu.VMEM((8, rows, width), BF16),
+        pltpu.VMEM((2 * len(wider_bits()) or 1, rows, width), BF16),
+        dma((4 * REDUCE_KINDS,)),
+        dma((4 * REDUCE_KINDS,)),
+        dma((GATHER_KINDS,)),
+        dma((GATHER_KINDS,)),
+        dma((wide,)),
+        dma((wide,)),
+    ]
+
+
+def attend_back_head(qkv_ref, offset, back_ref, mixed_ref, logsum_ref, out_ref, held):
     for start, length in IMAGES:
         whole = slice(start, start + length)
-        key_t = qkv_ref[48:96, whole]
+        key_t = qkv_ref[pl.ds(offset + 48, 48), whole]
         key_rows = key_t.T
-        value_rows = qkv_ref[96:144, whole].T
+        value_rows = qkv_ref[pl.ds(offset + 96, 48), whole].T
         chunk = min(CHUNK, length)
         count = length // chunk
         for i in range(count):
             cols = slice(start + i * chunk, start + (i + 1) * chunk)
-            query_t = qkv_ref[0:48, cols]
+            query_t = qkv_ref[pl.ds(offset, 48), cols]
             back_t = back_ref[:, cols]
             inner = jnp.sum(
                 back_t.astype(F32) * mixed_ref[:, cols].astype(F32), axis=0, keepdims=True
@@ -419,7 +616,7 @@
             probs = jnp.exp2(scores * SCALE_LOG2 - logsum_ref[0, :, cols])
             back_probs = nn(value_rows, back_t)
             back_scores = (probs * (back_probs - inner)).astype(BF16)
-            out_ref[0:48, cols] = (nn(key_t, back_scores) * SCALE).astype(BF16)
+            out_ref[pl.ds(offset, 48), cols] = (nn(key_t, back_scores) * SCALE).astype(BF16)
             back_key = nt(query_t, back_scores)
             back_value = nt(back_t, probs.astype(BF16))
             if i > 0:
@@ -429,48 +626,471 @@
                 held[0:48, 0:length] = back_key
                 held[48:96, 0:length] = back_value
             else:
-                out_ref[48:96, whole] = (back_key * SCALE).astype(BF16)
-                out_ref[96:144, whole] = back_value.astype(BF16)
-
-
-def attend_back(qkv, back_mixed, mixed, logsum):
-    heads, rows = qkv.shape[0] // 144, qkv.shape[1]
+                out_ref[pl.ds(offset + 48, 48), whole] = (back_key * SCALE).astype(BF16)
+                out_ref[pl.ds(offset + 96, 48), whole] = back_value.astype(BF16)
+
+
+def attend_back_kernel(
+    qkv_ref,
+    back_ref,
+    mixed_ref,
+    logsum_ref,
+    first_ref,
+    out_grad_ref,
+    ff_grad,
+    out_ref,
+    grad_ref,
+    sums_ref,
+    ff_out,
+    held,
+    total,
+    *scratch,
+):
+    step = pl.program_id(0)
+    head = step % 4
+    *got, final, wide, send, recv, share_send, share_recv, wide_send, wide_recv, local = scratch
+    dp, base, y, x, core, mp = place()
+
+    def own(slot):
+        src = ff_grad.at[slot, :, :, core]
+        return pltpu.make_async_copy(src, total.at[slot], local.at[slot])
+
+    reduces = [
+        Reduce(
+            slot,
+            ff_grad.at[slot, :, :, flip(core)],
+            total.at[slot],
+            reduce_refs(got, slot),
+            96,
+            send,
+            recv,
+        )
+        for slot in range(4)
+    ]
+    whole = Total(reduces, got[5], final, wide, wide_send, wide_recv)
+    share = Share(final, 96, share_send, share_recv)
+
+    @pl.when(step == 0)
+    def _():
+        for slot in range(4):
+            own(slot).start()
+        greet(group_partners())
+
+    for turn, slot in enumerate((2, 1, 3, 0)):
+
+        @pl.when(step == 3 * turn)
+        def _(slot=slot):
+            reduces[slot].cores()
+
+        @pl.when(step == 3 * turn + 1)
+        def _(slot=slot):
+            own(slot).wait()
+            reduces[slot].chips()
+
+        @pl.when(step == 3 * turn + 3)
+        def _(slot=slot):
+            reduces[slot].chips_again()
+
+        @pl.when(step == 3 * turn + 5)
+        def _(slot=slot):
+            reduces[slot].along()
+
+    attend_back_head(
+        qkv_ref, pl.multiple_of(head * IN_ROWS, 16), back_ref, mixed_ref, logsum_ref, out_ref, held
+    )
+
+    @pl.when(head == 3)
+    def _():
+        for part in range(4):
+            rows = out_ref[part * IN_ROWS : (part + 1) * IN_ROWS, :]
+            grad_ref[0, part, :IN_ROWS] = nn(rows, first_ref[...]).astype(BF16)
+            grad_ref[0, part, IN_ROWS:] = out_grad_ref[0, part]
+        sums_ref[0] = nt(jnp.ones((8, out_ref.shape[1]), BF16), out_ref[...])
+
+    @pl.when(step == 15)
+    def _():
+        whole.sum()
+        share.spread()
+        share.forward()
+        share.last()
+        share.finish()
+        for reduce in reduces:
+            reduce.finish()
+        result = pltpu.make_async_copy(final, ff_out, local.at[0])
+        result.start()
+        result.wait()
+
+
+def attend_back(qkv, back_mixed, mixed, logsum, first, out_grad, ff_grad):
+    rows, width = first.shape
+    anywhere = pl.BlockSpec(memory_space=pl.ANY)
     return pl.pallas_call(
         attend_back_kernel,
-        grid=(heads,),
+        grid=(16,),
         in_specs=[
-            pl.BlockSpec((144, rows), lambda h: (h, 0)),
-            pl.BlockSpec((48, rows), lambda h: (h, 0)),
-            pl.BlockSpec((48, rows), lambda h: (h, 0)),
-            pl.BlockSpec((1, 1, rows), lambda h: (h, 0, 0)),
+            pl.BlockSpec((4 * IN_ROWS, rows), lambda s: (s // 4, 0)),
+            pl.BlockSpec((48, rows), lambda s: (s, 0)),
+            pl.BlockSpec((48, rows), lambda s: (s, 0)),
+            pl.BlockSpec((1, 1, rows), lambda s: (s, 0, 0)),
+            pl.BlockSpec((rows, width), lambda s: (0, 0), pipeline_mode=pl.Buffered(1)),
+            pl.BlockSpec((1, 4, 48, width), lambda s: (s // 4, 0, 0, 0)),
+            anywhere,
         ],
-        out_specs=pl.BlockSpec((144, rows), lambda h: (h, 0)),
-        out_shape=jax.ShapeDtypeStruct((heads * 144, rows), BF16),
-        scratch_shapes=[pltpu.VMEM((96, LONG_LEN), F32)],
-        compiler_params=pltpu.CompilerParams(vmem_limit_bytes=40 << 20),
+        out_specs=[
+            pl.BlockSpec((4 * IN_ROWS, rows), lambda s: (s // 4, 0)),
+            pl.BlockSpec((1, 4, HEAD_ROWS, width), lambda s: (s // 4, 0, 0, 0)),
+            pl.BlockSpec((1, 8, 4 * IN_ROWS), lambda s: (s // 4, 0, 0)),
+            anywhere,
+        ],
+        out_shape=[
+            jax.ShapeDtypeStruct((16 * IN_ROWS, rows), BF16),
+            jax.ShapeDtypeStruct((4, 4, HEAD_ROWS, width), BF16),
+            jax.ShapeDtypeStruct((4, 8, 4 * IN_ROWS), F32),
+            jax.ShapeDtypeStruct((8, 192, width), BF16),
+        ],
+        scratch_shapes=[pltpu.VMEM((96, LONG_LEN), F32), pltpu.VMEM((4, 2, 2, 192, width), BF16)]
+        + reduce_scratch(192, 96, width)
+        + [pltpu.SemaphoreType.DMA((4,))],
+        compiler_params=pltpu.CompilerParams(
+            vmem_limit_bytes=58 << 20, collective_id=1, has_side_effects=True
+        ),
         cost_estimate=pl.CostEstimate(
-            flops=40_000_000_000, bytes_accessed=19_000_000, transcendentals=19_000_000
+            flops=45_000_000_000, bytes_accessed=40_000_000, transcendentals=19_000_000
         ),
         name="attend_back",
-    )(qkv, back_mixed, mixed, logsum)
-
-
-def by_shard(slots):
-    mp = lax.axis_size("mp")
-    blocks = slots.reshape(mp, -1, *slots.shape[1:])
-    twice = jnp.concatenate([blocks, blocks], axis=0)
-    start = lax.rem(mp - lax.axis_index("mp"), mp)
-    return lax.dynamic_slice_in_dim(twice, start, mp, 0).reshape(slots.shape)
-
-
-def reduce_rows(partial):
-    dp, mp = lax.axis_size("dp"), lax.axis_size("mp")
-    width = partial.shape[1]
-    partial = by_shard(partial)
-    blocks = partial.reshape(mp, dp, -1, width).transpose(1, 0, 2, 3).reshape(-1, width)
-    summed = lax.psum_scatter(blocks, "dp", scatter_dimension=0, tiled=True)
-    summed = lax.psum_scatter(summed, "mp", scatter_dimension=0, tiled=True)
-    return lax.all_gather(summed, "dp", axis=0, tiled=True).astype(F32)
+    )(qkv, back_mixed, mixed, logsum, first, out_grad, ff_grad.reshape(4, 2, 2, 2, 192, width))
+
+
+BLOCK = 256
+
+
+def tail_kernel(
+    back_qkv_ref,
+    in_ref,
+    tokens_ref,
+    resid_ref,
+    vector_ref,
+    feed_small_ref,
+    bias_sums_ref,
+    in_grad,
+    input_ref,
+    small_ref,
+    in_out,
+    total,
+    sums,
+    sum_got,
+    along_got,
+    sum_send,
+    sum_recv,
+    along_send,
+    along_recv,
+    *scratch,
+    blocks,
+):
+    step = pl.program_id(0)
+    width = tokens_ref.shape[1]
+    *got, final, wide, send, recv, share_send, share_recv, wide_send, wide_recv, local = scratch
+    dp, base, y, x, core, mp = place()
+    ways = lax.axis_size("mp")
+
+    def own(slot):
+        src = in_grad.at[slot, :, :, core]
+        return pltpu.make_async_copy(src, total.at[slot], local.at[slot])
+
+    reduces = [
+        Reduce(
+            slot,
+            in_grad.at[slot, :, :, flip(core)],
+            total.at[slot],
+            reduce_refs(got, slot),
+            48,
+            send,
+            recv,
+        )
+        for slot in range(4)
+    ]
+    whole = Total(reduces, got[5], final, wide, wide_send, wide_recv)
+    share = Share(final, 48, share_send, share_recv)
+    order = (2, 1, 3, 0)
+
+    @pl.when(step == 0)
+    def _():
+        for slot in order:
+            own(slot).start()
+        greet(group_partners())
+        for slot in order:
+            reduces[slot].cores()
+        for slot in order:
+            own(slot).wait()
+            reduces[slot].chips()
+        sums[0] = jnp.zeros_like(sums[0])
+        sums[0, 0:8, :] = feed_small_ref[...]
+        for slot in range(4):
+            sums[0, 8 + slot : 9 + slot, 0 : 4 * IN_ROWS] = bias_sums_ref[slot, 0:1]
+
+    @pl.when(step == 2)
+    def _():
+        for slot in order:
+            reduces[slot].chips_again()
+
+    @pl.when(step == 4)
+    def _():
+        for slot in order:
+            reduces[slot].along()
+
+    inputs = tokens_ref[...].astype(F32)
+    average = jnp.mean(inputs, axis=-1, keepdims=True)
+    centred = inputs - average
+    inverse = lax.rsqrt(jnp.mean(centred * centred, axis=-1, keepdims=True) + epsilon)
+    scaled = centred * inverse
+    back_first = None
+    for slot in range(4):
+        weight = in_ref[slot, :, :IN_ROWS].reshape(4 * IN_ROWS, width)
+        part = tn(back_qkv_ref[slot * 4 * IN_ROWS : (slot + 1) * 4 * IN_ROWS, :], weight)
+        back_first = part if slot == 0 else back_first + part
+    sums[0, 12:13, :] += jnp.sum(back_first * scaled, axis=0, keepdims=True)
+    sums[0, 13:14, :] += jnp.sum(back_first, axis=0, keepdims=True)
+    back_norm = back_first * vector_ref[0:1, :]
+    input_ref[...] = resid_ref[...] + inverse * (
+        back_norm
+        - jnp.mean(back_norm, axis=-1, keepdims=True)
+        - scaled * jnp.mean(back_norm * scaled, axis=-1, keepdims=True)
+    )
+
+    @pl.when(step == blocks - 1)
+    def _():
+        bits = [1, 2, 4] + wider_bits()
+
+        def sum_copy(i):
+            return pltpu.make_async_remote_copy(
+                src_ref=sums.at[i],
+                dst_ref=sum_got.at[i],
+                send_sem=sum_send.at[i],
+                recv_sem=sum_recv.at[i],
+                device_id=(other_bit(dp, bits[i]), mp),
+                device_id_type=MESH,
+            )
+
+        def along_copy(slot):
+            return pltpu.make_async_remote_copy(
+                src_ref=sums.at[len(bits)],
+                dst_ref=along_got.at[slot - 1],
+                send_sem=along_send.at[slot - 1],
+                recv_sem=along_recv.at[slot - 1],
+                device_id=(dp, lax.rem(mp + slot, ways)),
+                device_id_type=MESH,
+            )
+
+        sum_copy(0).start()
+        whole.sum()
+        share.spread()
+        for i in range(len(bits)):
+            sum_copy(i).wait_recv()
+            sums[i + 1] = sums[i] + sum_got[i]
+            if i + 1 < len(bits):
+                sum_copy(i + 1).start()
+            if i == 1:
+                share.forward()
+        for slot in (1, 2, 3):
+            along_copy(slot).start()
+        share.last()
+        result = sums[len(bits)]
+        small_ref[...] = result
+        for slot in (1, 2, 3):
+            along_copy(slot).wait_recv()
+            more = along_got[slot - 1]
+            small_ref[0:4, :] += more[0:4]
+            small_ref[12:14, :] += more[12:14]
+            small_ref[4:5, :] += more[4 + slot : 5 + slot]
+            small_ref[8:9, :] += more[8 + slot : 9 + slot]
+        share.finish()
+        for i in range(len(bits)):
+            sum_copy(i).wait_send()
+        for slot in (1, 2, 3):
+            along_copy(slot).wait_send()
+        for reduce in reduces:
+            reduce.finish()
+        written = pltpu.make_async_copy(final, in_out, local.at[0])
+        written.start()
+        written.wait()
+
+
+def tail(back_qkv, in_all, tokens, resid, vectors, feed_small, bias_sums, in_grad):
+    rows, width = tokens.shape
+    blocks = rows // BLOCK
+    bits = 3 + len(wider_bits())
+    anywhere = pl.BlockSpec(memory_space=pl.ANY)
+    one = pl.Buffered(1)
+    dma = pltpu.SemaphoreType.DMA
+    return pl.pallas_call(
+        functools.partial(tail_kernel, blocks=blocks),
+        grid=(blocks,),
+        in_specs=[
+            pl.BlockSpec((16 * IN_ROWS, BLOCK), lambda s: (0, s)),
+            pl.BlockSpec((4, 4, HEAD_ROWS, width), lambda s: (0, 0, 0, 0), pipeline_mode=one),
+            pl.BlockSpec((BLOCK, width), lambda s: (s, 0)),
+            pl.BlockSpec((BLOCK, width), lambda s: (s, 0)),
+            pl.BlockSpec((8, width), lambda s: (0, 0)),
+            pl.BlockSpec((8, width), lambda s: (0, 0)),
+            pl.BlockSpec((4, 8, 4 * IN_ROWS), lambda s: (0, 0, 0)),
+            anywhere,
+        ],
+        out_specs=[
+            pl.BlockSpec((BLOCK, width), lambda s: (s, 0)),
+            pl.BlockSpec((16, width), lambda s: (0, 0)),
+            anywhere,
+        ],
+        out_shape=[
+            jax.ShapeDtypeStruct((rows, width), F32),
+            jax.ShapeDtypeStruct((16, width), F32),
+            jax.ShapeDtypeStruct((8, 96, width), BF16),
+        ],
+        scratch_shapes=[
+            pltpu.VMEM((4, 2, 2, 96, width), BF16),
+            pltpu.VMEM((bits + 1, 16, width), F32),
+            pltpu.VMEM((bits, 16, width), F32),
+            pltpu.VMEM((3, 16, width), F32),
+            dma((bits,)),
+            dma((bits,)),
+            dma((3,)),
+            dma((3,)),
+        ]
+        + reduce_scratch(96, 48, width)
+        + [dma((4,))],
+        compiler_params=pltpu.CompilerParams(
+            vmem_limit_bytes=50 << 20, collective_id=2, has_side_effects=True
+        ),
+        cost_estimate=pl.CostEstimate(
+            flops=6_000_000_000, bytes_accessed=30_000_000, transcendentals=2000
+        ),
+        name="tail",
+    )(back_qkv, in_all, tokens, resid, vectors, feed_small, bias_sums, in_grad)
+
+
+def feed_kernel(live_ref, tokens_ref, grad_ref, mixed_ref, out_w_ref, ff_ref, bias_ref, vec_ref,
+                output_ref, resid_ref, back_mixed_ref, ff_grad_ref, out_grad_ref, small_ref,
+                second_t, back_t, act_s, hid_s, out_acc, *, blocks):
+    step = pl.program_id(0)
+    width = tokens_ref.shape[1]
+
+    @pl.when(step == 0)
+    def _():
+        small_ref[...] = jnp.zeros_like(small_ref)
+        second_t[width:, :] = jnp.ones((16, second_t.shape[1]), BF16)
+
+    @pl.when(step < blocks)
+    def _():
+        row = step * BLOCK + lax.broadcasted_iota(jnp.int32, (BLOCK, 1), 0)
+        limit = jnp.where(row < SHORT_ROWS, live_ref[0, 0] * SHORT_LEN, SHORT_ROWS + live_ref[0, 1] * LONG_LEN)
+        is_live = row < limit
+        out_w = out_w_ref[...].reshape(width, width)
+        mixed = mixed_ref[...]
+        residual = tokens_ref[...].astype(F32) + tn(mixed, out_w) + vec_ref[0:1, :]
+        average = jnp.mean(residual, axis=-1, keepdims=True)
+        centred = residual - average
+        inverse = lax.rsqrt(jnp.mean(centred * centred, axis=-1, keepdims=True) + epsilon)
+        scaled = centred * inverse
+        gain = vec_ref[1:2, :]
+        second = (scaled * gain + vec_ref[2:3, :]).astype(BF16)
+        back = jnp.where(is_live, grad_ref[...].astype(F32), 0.0)
+        back_low = back.astype(BF16)
+        rows = pl.ds(pl.multiple_of(step * BLOCK, BLOCK), BLOCK)
+        second_t[0:width, rows] = second.T
+        back_t[:, rows] = back_low.T
+        feed = None
+        back_second = None
+        for j in range(4):
+            up = ff_ref[j, :, 0:96, :].reshape(width, width)
+            down = ff_ref[j, :, 96:192, :].reshape(width, width)
+            hidden = nn(second, up) + bias_ref[j, 0:1, 256:]
+            half = 0.5 + 0.5 * lax.erf(hidden * (0.5 ** 0.5))
+            act = (hidden * half).astype(BF16)
+            slope = half + hidden * (jnp.exp(hidden * hidden * -0.5) * (1.0 / math.sqrt(2 * math.pi)))
+            back_hid = (nt(back_low, down) * slope).astype(BF16)
+            act_s[j, rows, :] = act
+            hid_s[j, rows, :] = back_hid
+            f = nn(act, down)
+            b = nt(back_hid, up)
+            feed = f if j == 0 else feed + f
+            back_second = b if j == 0 else back_second + b
+        output_ref[...] = jnp.where(is_live, residual + feed + vec_ref[3:4, :], 0.0).astype(BF16)
+        small_ref[1:2, :] += jnp.sum(back_second * scaled, axis=0, keepdims=True)
+        small_ref[2:3, :] += jnp.sum(back_second, axis=0, keepdims=True)
+        small_ref[3:4, :] += jnp.sum(back, axis=0, keepdims=True)
+        back_norm = back_second * gain
+        back_resid = back + inverse * (
+            back_norm - jnp.mean(back_norm, axis=-1, keepdims=True)
+            - scaled * jnp.mean(back_norm * scaled, axis=-1, keepdims=True))
+        small_ref[0:1, :] += jnp.sum(back_resid, axis=0, keepdims=True)
+        resid_ref[...] = back_resid
+        branch = back_resid.astype(BF16)
+        back_mixed_ref[...] = nt(out_w, branch).astype(BF16)
+        part = nn(mixed, branch)
+        @pl.when(step == 0)
+        def _():
+            out_acc[...] = part
+        @pl.when(step > 0)
+        def _():
+            out_acc[...] += part
+        @pl.when(step == blocks - 1)
+        def _():
+            out_grad_ref[...] = out_acc[...].astype(BF16).reshape(out_grad_ref.shape)
+
+    @pl.when(step >= blocks)
+    def _():
+        slot = step - blocks
+        up = nn(second_t[...], hid_s[slot])
+        ff_grad_ref[0, :, 0:96, :] = up[:width].astype(BF16).reshape(8, 96, width)
+        small_ref[pl.ds(4 + slot, 1), :] = up[width:width + 1]
+        down = nn(back_t[...], act_s[slot])
+        ff_grad_ref[0, :, 96:192, :] = down.astype(BF16).reshape(8, 96, width)
+
+def feed(live, tokens, out_grad, mixed, in_all, ff_all, bias_all, vectors):
+    rows, width = tokens.shape
+    blocks = rows // BLOCK
+    blk = lambda s: (jnp.minimum(s, blocks - 1), 0)
+    col = lambda s: (0, jnp.minimum(s, blocks - 1))
+    one = pl.Buffered(1)
+    return pl.pallas_call(
+        functools.partial(feed_kernel, blocks=blocks),
+        grid=(blocks + 4,),
+        in_specs=[
+            pl.BlockSpec(memory_space=pltpu.SMEM),
+            pl.BlockSpec((BLOCK, width), blk),
+            pl.BlockSpec((BLOCK, width), blk),
+            pl.BlockSpec((width, BLOCK), col),
+            pl.BlockSpec((4, 4, 48, width), lambda s: (0, 0, 3, 0), pipeline_mode=one),
+            pl.BlockSpec((4, 8, 192, width), lambda s: (0, 0, 0, 0), pipeline_mode=one),
+            pl.BlockSpec((4, 8, 1024), lambda s: (0, 0, 0), pipeline_mode=one),
+            pl.BlockSpec((8, width), lambda s: (0, 0), pipeline_mode=one),
+        ],
+        out_specs=[
+            pl.BlockSpec((BLOCK, width), blk),
+            pl.BlockSpec((BLOCK, width), blk),
+            pl.BlockSpec((width, BLOCK), col),
+            pl.BlockSpec((1, 8, 192, width), lambda s: (jnp.maximum(s - blocks, 0), 0, 0, 0)),
+            pl.BlockSpec((4, 4, 48, width), lambda s: (0, 0, 0, 0)),
+            pl.BlockSpec((8, width), lambda s: (0, 0)),
+        ],
+        out_shape=[
+            jax.ShapeDtypeStruct((rows, width), BF16),
+            jax.ShapeDtypeStruct((rows, width), F32),
+            jax.ShapeDtypeStruct((width, rows), BF16),
+            jax.ShapeDtypeStruct((4, 8, 192, width), BF16),
+            jax.ShapeDtypeStruct((4, 4, 48, width), BF16),
+            jax.ShapeDtypeStruct((8, width), F32),
+        ],
+        scratch_shapes=[
+            pltpu.VMEM((width + 16, rows), BF16),
+            pltpu.VMEM((width, rows), BF16),
+            pltpu.VMEM((4, rows, width), BF16),
+            pltpu.VMEM((4, rows, width), BF16),
+            pltpu.VMEM((width, width), F32),
+        ],
+        compiler_params=pltpu.CompilerParams(vmem_limit_bytes=60 << 20),
+        cost_estimate=pl.CostEstimate(flops=50_000_000_000, bytes_accessed=45_000_000, transcendentals=10_000_000),
+        name="feed",
+    )(live, tokens, out_grad, mixed, in_all, ff_all, bias_all, vectors)
 
 
 def local(
@@ -490,113 +1110,66 @@
     down_weight,
     down_bias,
 ):
-    mp = lax.axis_size("mp")
     width = tokens.shape[1]
     own_heads = project_in.shape[2] // HEAD_DIM
-    own_hidden = up_weight.shape[1]
     in_own = project_in.reshape(width, 3, own_heads, HEAD_DIM).transpose(2, 1, 3, 0)
-    in_own = in_own.reshape(own_heads, IN_ROWS, width)
+    in_own = jnp.concatenate(
+        [in_own.reshape(own_heads, IN_ROWS, width), project_out.reshape(own_heads, HEAD_DIM, width)],
+        axis=1,
+    )
     ff_own = jnp.concatenate(
-        [
-            up_weight.reshape(8, -1, width),
-            down_weight.reshape(8, -1, width),
-            project_out.reshape(8, -1, width),
-        ],
-        axis=1,
+        [up_weight.reshape(8, -1, width), down_weight.reshape(8, -1, width)], axis=1
     )
     pair_bias = query_value_bias.astype(F32).reshape(2, own_heads, HEAD_DIM)
     own_bias = jnp.concatenate([pair_bias[0], jnp.zeros_like(pair_bias[0]), pair_bias[1]], axis=1)
     bias_own = jnp.zeros((8, 1024), F32)
     bias_own = lax.dynamic_update_slice(bias_own, own_bias, (0, 0))
     bias_own = lax.dynamic_update_slice(bias_own, up_bias.astype(F32)[None], (0, 256))
-
-    inputs = tokens.astype(F32)
-    first_normed, first_pull = jax.vjp(layer_norm, inputs, first_gain, first_shift)
-    first = first_normed.astype(BF16)
+    blank = jnp.zeros_like(first_gain)
+    feed_vectors = jnp.stack([output_bias, second_gain, second_shift, down_bias] + [blank] * 4)
+    tail_vectors = jnp.stack([first_gain] + [blank] * 7)
+
+    first = layer_norm(tokens.astype(F32), first_gain, first_shift).astype(BF16)
     qkv, mixed, logsum, in_all, ff_all, bias_all = attend(first, in_own, ff_own, bias_own)
-    weight_in = in_all.reshape(-1, width)
-    weight_up = ff_all[:, :, 0:96].reshape(-1, width)
-    weight_down = ff_all[:, :, 96:192].reshape(-1, width)
-    weight_out = ff_all[:, :, 192:216].reshape(-1, width)
-    bias_up = bias_all[:, 0, 256:]
-    residual = inputs + tn(mixed, weight_out) + output_bias
-    second_normed, second_pull = jax.vjp(layer_norm, residual, second_gain, second_shift)
-    second = second_normed.astype(BF16)
-    is_live = live_mask(live_images, tokens.shape[0])
-    back_out = jnp.where(is_live, out_grad, jnp.zeros_like(out_grad))
-
-    feed = residual + down_bias
-    back_second = jnp.zeros_like(residual)
-    grads_up, grads_up_bias, grads_down = [], [], []
-    for j in range(mp):
-        up_j = weight_up[j * width : (j + 1) * width]
-        down_j = weight_down[j * own_hidden : (j + 1) * own_hidden]
-        hidden = nn(second, up_j) + bias_up[j]
-        activated, gelu_pull = jax.vjp(gelu_exact, hidden)
-        act_low = activated.astype(BF16)
-        feed = feed + nn(act_low, down_j)
-        grads_down.append(tn(act_low, back_out).astype(BF16))
-        back_hidden = gelu_pull(nt(back_out, down_j))[0].astype(BF16)
-        grads_up.append(tn(second, back_hidden).astype(BF16))
-        grads_up_bias.append(jnp.sum(back_hidden, axis=0, dtype=F32))
-        back_second = back_second + nt(back_hidden, up_j)
-    output = jnp.where(is_live, feed, 0.0).astype(BF16)
-    grad_down = reduce_rows(jnp.concatenate(grads_down, axis=0))
-    grad_up = reduce_rows(jnp.concatenate(grads_up, axis=0))
-    grad_down_bias = jnp.sum(back_out, axis=0, dtype=F32)
-
-    back_resid_norm, grad_second_gain, grad_second_shift = second_pull(back_second)
-    back_residual = back_out.astype(F32) + back_resid_norm
-    grad_output_bias = jnp.sum(back_residual, axis=0)
-    back_branch = back_residual.astype(BF16)
-    grad_out = reduce_rows(nn(mixed, back_branch).astype(BF16))
-    back_mixed = nt(weight_out, back_branch).astype(BF16)
-    back_qkv = attend_back(qkv, back_mixed, mixed, logsum)
-    grad_bias_in = jnp.sum(back_qkv, axis=1, dtype=F32)
-    grad_in = reduce_rows(nn(back_qkv, first).astype(BF16))
-    back_inputs, grad_first_gain, grad_first_shift = first_pull(tn(back_qkv, weight_in))
-    input_grad = back_residual + back_inputs
-
-    small = [
-        grad_first_gain,
-        grad_first_shift,
-        grad_output_bias,
-        grad_second_gain,
-        grad_second_shift,
-        grad_down_bias,
-    ]
-    packed = lax.psum(
-        jnp.concatenate(
-            small + [by_shard(grad_bias_in), by_shard(jnp.concatenate(grads_up_bias))]
-        ).reshape(-1, 128), ALL
-    ).reshape(-1)
-    sums = [packed[i * width : (i + 1) * width] for i in range(len(small))]
-    place = lax.axis_index("mp")
-    begin = len(small) * width
-    own_rows = 3 * own_heads * HEAD_DIM
-    own_in = lax.dynamic_slice_in_dim(packed, begin + place * own_rows, own_rows)
-    own_in = own_in.reshape(own_heads, 3, HEAD_DIM)
-    grad_pair = jnp.stack([own_in[:, 0].reshape(-1), own_in[:, 2].reshape(-1)])
-    begin = begin + mp * own_rows
-    grad_up_bias = lax.dynamic_slice_in_dim(packed, begin + place * own_hidden, own_hidden)
-    grad_in = (
-        grad_in.reshape(own_heads, 3, HEAD_DIM, width).transpose(3, 1, 0, 2).reshape(width, 3, -1)
+    output, resid, back_mixed, ff_grad, out_grads, feed_small = feed(
+        live_images, tokens, out_grad, mixed, in_all, ff_all, bias_all, feed_vectors
     )
+    back_qkv, in_grad, bias_sums, ff_sum = attend_back(
+        qkv, back_mixed, mixed, logsum, first, out_grads, ff_grad
+    )
+    input_grad, small, in_sum = tail(
+        back_qkv,
+        in_all,
+        tokens,
+        resid,
+        tail_vectors,
+        feed_small,
+        bias_sums,
+        in_grad.reshape(4, 2, 2, 2, 96, width),
+    )
+    grad_up = ff_sum[:, :96].reshape(width, width).astype(F32)
+    grad_down = ff_sum[:, 96:].reshape(width, width).astype(F32).T
+    in_sum = in_sum.reshape(own_heads, HEAD_ROWS, width)
+    grad_out = in_sum[:, IN_ROWS:].reshape(-1, width).astype(F32)
+    grad_in = in_sum[:, :IN_ROWS].reshape(own_heads, 3, HEAD_DIM, width).astype(F32)
+    grad_in = grad_in.transpose(3, 1, 0, 2).reshape(width, 3, -1)
+    pair_sum = small[8, : 4 * IN_ROWS].reshape(own_heads, 3, HEAD_DIM)
+    grad_pair = jnp.stack([pair_sum[:, 0].reshape(-1), pair_sum[:, 2].reshape(-1)])
     return (
         output,
         input_grad,
-        sums[0],
-        sums[1],
+        small[12],
+        small[13],
         grad_in,
         grad_pair,
         grad_out,
-        sums[2],
-        sums[3],
-        sums[4],
+        small[0],
+        small[1],
+        small[2],
         grad_up,
-        grad_up_bias,
+        small[4],
         grad_down,
-        sums[5],
+        small[3],
     )
 
 

time: 645 us -> 324 us (0.50); the launches traced: 634 us -> 323 us
  matrix products: 221 us -> 0 us
  Pallas kernels: 133 us -> 292 us
  waiting for transfers between devices: 105 us -> 0 us
  blocking collectives: 60 us -> 0 us
  other arithmetic: 51.9 us -> 9.8 us
  local copies, waits for them, and re-layouts: 47.7 us -> 21 us
  between operations: 15.5 us -> 0.96 us
    dot_general x29 -> x0, matrix products: 221 us -> none  [the longest x10 137 us: nn(): lax.dot_general(left, right, (((1,), (0,)), ((), ())), preferred_element_...]
    pallas_call x1 -> x3, Pallas kernels: 55.4 us -> 213 us  [the longest x1 91 us: attend_back(): pl.pallas_call(attend_back_kernel, grid=(16,), in_specs=[pl.BlockSpec((4...]
    reduce_scatter x8 -> x0, waiting for transfers between devices: 89.4 us -> none  [the longest x4 76 us: reduce_rows(): summed = lax.psum_scatter(blocks, 'dp', scatter_dimension=0, tiled=True)]
    psum x1 -> x0, blocking collectives: 39.2 us -> none  [local(): lax.psum(jnp.concatenate(small + [by_shard(grad_bias_in), by_shard(jnp.co...]
    all_gather x2 -> x0, blocking collectives: 20.8 us -> none  [reduce_rows(): return lax.all_gather(summed, 'dp', axis=0, tiled=True).astype(F32)]
    reduce_sum x4 -> x0, other arithmetic: 19.4 us -> none  [the longest x1 9.34 us: local(): grad_down_bias = jnp.sum(back_out, axis=0, dtype=F32)]
    all_gather x2 -> x0, waiting for transfers between devices: 15.1 us -> none  [reduce_rows(): return lax.all_gather(summed, 'dp', axis=0, tiled=True).astype(F32)]
    concatenate x8 -> x1, other arithmetic: 12.6 us -> 0.08 us  [local(): jnp.concatenate([in_own.reshape(own_heads, IN_ROWS, width), project_out.r...]
  transfers between devices with their start and end apart: 10 -> 0, of which waited for: 4 -> 0; matrix products, arithmetic and copies ran while one was open for 19% -> 0% of each run, Pallas kernels for 9% -> 0%
where the time goes in v3:
time: 324 us; the launch traced here: 323 us
  Pallas kernels  292 us (90%)
  local copies, waits for them, and re-layouts  21 us (6%)
  other arithmetic  9.8 us (3%)
    pallas_call x1, Pallas kernels, attend_back(): pl.pallas_call(attend_back_kernel, grid=(16,), in_specs=[pl.BlockSpec((4...  91 us
    pallas_call x1, Pallas kernels, attend(): pl.pallas_call(attend_kernel, grid=(heads,), in_specs=[pl.BlockSpec((rows...  78.8 us
    pallas_call x1, Pallas kernels, feed(): pl.pallas_call(functools.partial(feed_kernel, blocks=blocks), grid=(block...  68.1 us
    pallas_call x1, Pallas kernels, tail(): pl.pallas_call(functools.partial(tail_kernel, blocks=blocks), grid=(block...  53.8 us
    unnamed x47, local copies, waits for them, and re-layouts  11.3 us

profile of v3, /device:TPU:0, one launch (start us, length us, event | category | flops | bytes accessed | tf_op | source)
XLA Modules:
  0.0 323.4 jit_solution(9039896340550468331)
XLA Ops:
  0.6 0.0 copy-start
  0.7 2.2 convert_reduce_fusion
  2.9 0.1 copy-done
  3.0 0.8 fusion.2
  3.9 0.0 copy-start.22
  3.9 0.0 copy-start.21
  3.9 0.0 copy-start.11
  3.9 0.0 copy-start.12
  4.0 2.2 fusion.5.first_ref
  6.2 0.1 squeeze.27
  6.3 0.1 squeeze.28
  6.4 0.1 pad.8.clone
  6.4 0.1 pad_maximum_fusion.3
  6.5 0.3 dynamic_update_slice.7.bias_own
  6.9 0.2 pad_maximum_fusion.ff_own
  7.0 0.0 copy-start.3
  7.0 1.0 copy-done.13
  8.0 0.1 copy.32
  8.1 0.1 pad_maximum_fusion.1.in_own
  8.2 0.8 copy-done.3
  8.9 78.8 %attend.1 = (bf16[2304,1536]{1,0:T(8,128)(2,1)}, bf16[768,1536]{1,0:T(8,128)(2,1)S(1)}, f32[16,1,1536]{2,1,0:T(1,128)S(1)}, bf16[4,4,192,768]{3,2,1,0:T(8,128)(2...) custom-call(bf16[1536,768]{1,0:T(8,128)(2,1)S(1)} %copy-done.3, ...), custom_call_target="tpu_custom_call" | custom-call | flops 30000001024 | bytes 30000000 | tf_op jit(solution)/shard_map/attend/pallas_call | solution.py:354
  87.8 2.2 copy-done.2
  90.0 1.4 copy-done.7
  91.4 0.7 copy-done.8
  92.0 0.6 copy-done.9
  92.7 0.6 stack.29.vec_ref
  93.4 68.1 %feed.1 = (bf16[1536,768]{1,0:T(8,128)(2,1)}, f32[1536,768]{1,0:T(8,128)}, bf16[768,1536]{1,0:T(8,128)(2,1)}, bf16[4,8,192,768]{3,2,1,0:T(8,128)(2,1)}, bf16[4,4...) custom-call(s32[1,2]{1,0:T(1,128)} %live_ref.1, bf16[1536,768]{1,0:T(8,128)(2,1)} %tokens_ref.3, bf16[1536,768]{1,0:T(8,128)(2,1)} %grad_ref.1, ...), custom_call_target="tpu_custom_call" | custom-call | flops 49999998976 | bytes 45000000 | tf_op jit(solution)/shard_map/feed/pallas_call | solution.py:1054
  161.4 91.0 %attend_back.1 = (bf16[2304,1536]{1,0:T(8,128)(2,1)}, bf16[4,4,192,768]{3,2,1,0:T(8,128)(2,1)}, f32[4,8,576]{2,1,0:T(8,128)}, bf16[8,192,768]{2,1,0:T(8,128)(2,1)}) custom-call(bf16[2304,1536]{1,0:T(8,128)(2,1)} %get-tuple-element.38.qkv_ref, bf16[768,1536]{1,0:T(8,128)(2,1)} %get-tuple-element.39.back_ref, bf16[768,1536]{1,0:T(8,128)(2,1)} %copy-done.7, ...), custom_call_target="tpu_custom_call" | custom-call | flops 44999999488 | bytes 40000000 | tf_op jit(solution)/shard_map/attend_back/pallas_call | solution.py:727
  252.5 1.8 fusion.6
  254.2 2.7 bitcast_convert_fusion
  256.9 3.2 copy.34
  260.1 0.1 pad.5.clone
  260.2 0.1 pad.4.clone
  260.3 0.1 pad_maximum_fusion.2.vector_ref
  260.4 0.9 copy-done.4
  261.3 0.7 copy-done.5
  262.0 53.8 %tail.1 = (f32[1536,768]{1,0:T(8,128)}, f32[16,768]{1,0:T(8,128)S(1)}, bf16[8,96,768]{2,1,0:T(8,128)(2,1)S(1)}) custom-call(bf16[2304,1536]{1,0:T(8,128)(2,1)} %get-tuple-element.43.back_qkv_ref, bf16[4,4,192,768]{3,2,1,0:T(8,128)(2,1)} %copy-done.2, bf16[1536,768]{1,0:T(8,128)(2,1)S(1)} %copy-done.1, f32[1536,768]{1,0:T(8,128)} %get-tuple-element.44.resid_ref, ...), custom_call_target="tpu_custom_call" | custom-call | flops 6000000000 | bytes 30000000 | tf_op jit(solution)/shard_map/tail/pallas_call | solution.py:925
  315.8 0.0 copy-start.6
  315.8 0.6 copy-done.6
  316.4 0.1 reshape_squeeze.3
  316.6 0.1 stack_reshape_squeeze.6
  316.6 0.1 stack_reshape_squeeze.7
  316.7 0.6 pad_maximum_fusion.4
  317.3 0.1 slice.68
  317.4 1.4 copy.33
  318.8 0.9 bitcast_convert_fusion.2
  319.7 1.6 slice_reduce_fusion
  321.3 2.2 copy.37
  (46 shorter events, 0.2 us)
Async XLA Ops:
  0.6 2.4 copy-start
  0.7 3.2 copy-start.15
  0.7 3.2 copy-start.16
  3.9 2.2 copy-start.22
  3.9 2.6 copy-start.21
  3.9 2.9 copy-start.11
  3.9 2.9 copy-start.12
  6.8 1.2 copy-start.13
  6.8 1.2 copy-start.14
  7.0 1.9 copy-start.3
  8.9 83.8 %copy-start.17 = (f32[768]{0:T(1024)S(1)}, f32[768]{0:T(1024)}, u32[]{:S(2)}) copy-start(f32[768]{0:T(1024)} %param.23) | copy-start | bytes 9220
  8.9 83.8 %copy-start.18 = (f32[768]{0:T(1024)S(1)}, f32[768]{0:T(1024)}, u32[]{:S(2)}) copy-start(f32[768]{0:T(1024)} %param.24) | copy-start | bytes 9220
  8.9 83.8 %copy-start.19 = (f32[768]{0:T(1024)S(1)}, f32[768]{0:T(1024)}, u32[]{:S(2)}) copy-start(f32[768]{0:T(1024)} %param.25) | copy-start | bytes 9220
  8.9 83.8 %copy-start.20 = (f32[768]{0:T(1024)S(1)}, f32[768]{0:T(1024)}, u32[]{:S(2)}) copy-start(f32[768]{0:T(1024)} %param.29) | copy-start | bytes 9220
  87.8 2.2 copy-start.2
  90.0 1.4 copy-start.7
  91.4 0.7 copy-start.8
  92.0 0.7 copy-start.9
  256.9 3.4 %copy-start.1 = (bf16[1536,768]{1,0:T(8,128)(2,1)S(1)}, bf16[1536,768]{1,0:T(8,128)(2,1)}, u32[]{:S(2)}) copy-start(bf16[1536,768]{1,0:T(8,128)(2,1)} %tokens_ref.3) | copy-start | bytes 7077892
  260.4 0.9 copy-start.4
  261.3 0.7 copy-start.5
  315.8 0.6 copy-start.6
  317.3 3.9 %copy-start.10 = (f32[1536,768]{1,0:T(8,128)S(1)}, f32[1536,768]{1,0:T(8,128)}, u32[]{:S(2)}) copy-start(f32[1536,768]{1,0:T(8,128)} %get-tuple-element.82) | copy-start | bytes 14155780

commit v4 on v3

v4 whole, which is shorter than its diff:
```python
import functools
import math

import jax
import jax.numpy as jnp
from jax import lax
from jax.experimental import pallas as pl
from jax.experimental.pallas import tpu as pltpu
from jax.sharding import PartitionSpec as P

HEAD_DIM = 48
SHORT_LEN = 256
LONG_LEN = 1024
SHORT_SLOTS = 2
LONG_SLOTS = 1
SHORT_ROWS = SHORT_SLOTS * SHORT_LEN
IMAGES = tuple((SHORT_LEN * i, SHORT_LEN) for i in range(SHORT_SLOTS)) + tuple(
    (SHORT_ROWS + LONG_LEN * i, LONG_LEN) for i in range(LONG_SLOTS)
)
SCALE = HEAD_DIM**-0.5
SCALE_LOG2 = SCALE * math.log2(math.e)
BF16 = jnp.bfloat16
F32 = jnp.float32
CHUNK = 512
BACK_CHUNK = 256

epsilon = 1e-05


def layer_norm(rows_in, norm_gain, norm_shift):
    average = jnp.mean(rows_in, axis=-1, keepdims=True)
    centred = rows_in - average
    variance = jnp.mean(centred * centred, axis=-1, keepdims=True)
    return centred * lax.rsqrt(variance + epsilon) * norm_gain + norm_shift


def nn(left, right):
    return lax.dot_general(
        left, right, (((1,), (0,)), ((), ())), preferred_element_type=F32
    )


def nt(left, right):
    return lax.dot_general(
        left, right, (((1,), (1,)), ((), ())), preferred_element_type=F32
    )


def tn(left, right):
    return lax.dot_general(
        left, right, (((0,), (0,)), ((), ())), preferred_element_type=F32
    )


GROUP = 8
MESH = pl.DeviceIdType.MESH
IN_ROWS = 144
HEAD_ROWS = 192


def place():
    dp, mp = lax.axis_index("dp"), lax.axis_index("mp")
    g = lax.rem(dp, GROUP)
    return dp, dp - g, g // 4, lax.rem(g // 2, 2), lax.rem(g, 2), mp


def flip(bit):
    return 1 - bit


class Gather:
    def __init__(self, own, buffers, piece, split, send, recv):
        self.own, self.buffers, self.piece, self.split = own, buffers, piece, split
        self.send, self.recv = send, recv
        self.dp, self.base, self.y, self.x, self.core, self.mp = place()

    def device(self, y, x, core):
        return (self.base + 4 * y + 2 * x + core, self.mp)

    def view(self, ref, y, x, core, part=None):
        view = self.piece(ref, 2 * y + x, core)
        if part is None:
            return view
        rows = view.shape[0]
        return view.at[pl.ds(0, self.split)] if part == 0 else view.at[pl.ds(self.split, rows - self.split)]

    def copy(self, kind, slot):
        y, x, core = self.y, self.x, self.core
        mine = (y, x, core)
        buffer = self.buffers[slot]
        if kind == 0:
            ways = lax.axis_size("mp")
            hop = 1 if slot == 2 else slot
            src = self.view(self.buffers[1] if slot == 2 else self.own, *mine)
            dst = self.view(buffer, *mine)
            device = (self.dp, lax.rem(self.mp + ways - hop, ways))
        else:
            return self.shared(kind, buffer, kind * 4 + slot)
        return self.remote(src, dst, device, kind * 4 + slot)

    def shared(self, kind, buffer, index):
        y, x, core = self.y, self.x, self.core
        mine, near_x, near_y = (y, x, core), (y, flip(x), core), (flip(y), x, core)
        moved, device = {
            1: lambda: (self.view(buffer, *mine), near_x),
            2: lambda: (self.view(buffer, *mine), near_y),
            3: lambda: (self.view(buffer, *near_x, 0), near_y),
            4: lambda: (self.view(buffer, *near_y, 1), near_x),
            5: lambda: (self.view(buffer, *mine), (y, x, flip(core))),
            6: lambda: (self.view(buffer, *near_x), (y, x, flip(core))),
            7: lambda: (self.view(buffer, *near_y), (y, x, flip(core))),
            8: lambda: (self.view(buffer, flip(y), flip(x), core), (y, x, flip(core))),
        }[kind]()
        return self.remote(moved, moved, self.device(*device), index)

    def remote(self, src, dst, device, index):
        return pltpu.make_async_remote_copy(
            src_ref=src,
            dst_ref=dst,
            send_sem=self.send.at[index],
            recv_sem=self.recv.at[index],
            device_id=device,
            device_id_type=MESH,
        )

    def start(self, slot, *kinds):
        for kind in kinds:
            self.copy(kind, slot).start()

    def arrived(self, slot, *kinds):
        for kind in kinds:
            self.copy(kind, slot).wait_recv()

    def along(self, slot):
        self.start(slot, 0)

    def spread(self, slot):
        self.arrived(slot, 0)
        self.start(slot, 1, 2, 5)

    def forward(self, slot):
        self.arrived(slot, 1)
        self.start(slot, 3, 6)
        self.arrived(slot, 2)
        self.start(slot, 4, 7)

    def last(self, slot):
        self.arrived(slot, 3, 4)
        self.start(slot, 8)

    def complete(self, slot):
        self.arrived(slot, 5, 6, 7, 8)

    def finish(self, *slots):
        for slot in slots:
            for kind in range(GATHER_KINDS):
                self.copy(kind, slot).wait_send()


GATHER_KINDS = 9


def in_piece(ref, chip, core):
    return ref.at[chip, :, pl.ds(pl.multiple_of(core * 384, 128), 384)]


def ff_piece(ref, chip, core):
    return ref.at[2 * chip + core]


def greet(partners):
    barrier = pltpu.get_barrier_semaphore()
    for partner in partners:
        pl.semaphore_signal(barrier, inc=1, device_id=partner, device_id_type=MESH)
    pl.semaphore_wait(barrier, len(partners))


def chunks_of(images, size):
    return [
        (start, length, first, min(size, length))
        for start, length in images
        for first in range(start, start + length, min(size, length))
    ]


def attend_head(qkv_ref, mixed_ref, logsum_ref):
    held = {}

    def score(start, length, first, chunk):
        if start not in held:
            whole = slice(start, start + length)
            value_t = qkv_ref[96:144, whole]
            held[start] = (
                qkv_ref[48:96, whole].T,
                jnp.concatenate([value_t, jnp.ones((16, length), BF16)], axis=0),
            )
        return nn(held[start][0], qkv_ref[0:48, first : first + chunk])

    def soften(scores):
        top = jnp.max(scores, axis=0, keepdims=True)
        return top, jnp.exp2((scores - top) * SCALE_LOG2).astype(BF16)

    def mix(item, top, weights):
        start, length, first, chunk = item
        cols = slice(first, first + chunk)
        sums = nn(held[start][1], weights)
        total = sums[48:49]
        mixed_ref[:, cols] = (sums[:48] / total).astype(BF16)
        logsum_ref[:, cols] = top * SCALE_LOG2 + jnp.log2(total)

    items = chunks_of(IMAGES, CHUNK)
    early, late = {0: score(*items[0])}, {}
    for i in range(len(items) + 1):
        if i + 1 < len(items):
            early[i + 1] = score(*items[i + 1])
        if i < len(items):
            late[i] = soften(early.pop(i))
        if i > 0:
            mix(items[i - 1], *late.pop(i - 1))


def hooks_of(table, step):
    def hook(name):
        for (at, where), actions in table.items():
            if where == name:

                @pl.when(step == at)
                def _(actions=actions):
                    for action in actions:
                        action()

    return hook


def group_partners(wide=False):
    dp, base, y, x, core, mp = place()
    ways = lax.axis_size("mp")
    return (
        [(dp, lax.rem(mp + k, ways)) for k in (1, 2, 3)]
        + [
            (base + 4 * y + 2 * flip(x) + core, mp),
            (base + 4 * flip(y) + 2 * x + core, mp),
            (base + 4 * y + 2 * x + flip(core), mp),
        ]
        + [(other_bit(dp, bit), mp) for bit in wider_bits() if wide]
    )


def attend_kernel(
    tokens_ref,
    vector_ref,
    in_own,
    out_own,
    ff_own,
    bias_own,
    qkv_ref,
    mixed_ref,
    logsum_ref,
    first_ref,
    in_out,
    ff_near,
    bias_out,
    in_all,
    bias_all,
    in_send,
    in_recv,
    ff_send,
    ff_recv,
    bias_send,
    bias_recv,
    own_sem,
    local_sem,
):
    step = pl.program_id(0)
    dp, base, y, x, core, mp = place()
    ways = lax.axis_size("mp")
    gin = Gather(in_all.at[0], [in_all.at[k] for k in range(4)], in_piece, 96, in_send, in_recv)
    gff = Gather(ff_own, [None, ff_near], ff_piece, 96, ff_send, ff_recv)
    own_copies = [
        pltpu.make_async_copy(
            in_own.at[part, pl.ds(head * 48, 48)] if part < 3 else out_own.at[pl.ds(head * 48, 48)],
            in_all.at[0, head, pl.ds(part * 48, 48)],
            own_sem.at[part * 4 + head],
        )
        for part in range(4)
        for head in range(4)
    ]
    local_bias = pltpu.make_async_copy(bias_own, bias_all.at[0], local_sem.at[1])
    out_in = pltpu.make_async_copy(in_all, in_out, local_sem.at[2])
    out_bias = pltpu.make_async_copy(bias_all, bias_out, local_sem.at[3])

    def bias_copy(slot):
        return pltpu.make_async_remote_copy(
            src_ref=bias_own,
            dst_ref=bias_all.at[slot],
            send_sem=bias_send.at[slot],
            recv_sem=bias_recv.at[slot],
            device_id=(dp, lax.rem(mp + ways - slot, ways)),
            device_id_type=MESH,
        )

    def begin():
        for copy in own_copies:
            copy.start()
        local_bias.start()
        greet(group_partners())
        for copy in own_copies:
            copy.wait()
        gin.along(1)
        gin.along(3)
        for slot in (1, 2, 3):
            bias_copy(slot).start()
        for rows in range(0, tokens_ref.shape[0], BLOCK):
            block = slice(rows, rows + BLOCK)
            first_ref[block] = layer_norm(
                tokens_ref[block].astype(F32), vector_ref[4:5], vector_ref[5:6]
            ).astype(BF16)
        local_bias.wait()

    def end():
        gff.complete(1)
        out_in.wait()
        out_bias.wait()
        for slot in (1, 2, 3):
            bias_copy(slot).wait_send()
        gin.finish(1, 2, 3)
        gff.finish(1)

    hook = hooks_of(
        {
            (0, "begin"): [begin],
            (0, "heads"): [lambda: gin.spread(1), lambda: gin.along(2), lambda: gff.along(1)],
            (0, 2): [lambda: gin.forward(1)],
            (0, 3): [lambda: gin.spread(3)],
            (0, "end"): [lambda: gin.last(1), lambda: gin.spread(2)],
            (1, "begin"): [
                lambda: [bias_copy(slot).wait_recv() for slot in (1, 2, 3)],
                lambda: gin.complete(1),
            ],
            (1, "heads"): [lambda: gin.forward(3)],
            (1, 2): [lambda: gin.last(3), lambda: gin.forward(2), lambda: gff.spread(1)],
            (1, "end"): [lambda: gin.last(2)],
            (2, "begin"): [lambda: gin.complete(3)],
            (2, 2): [lambda: gff.forward(1)],
            (2, "end"): [lambda: gff.last(1)],
            (3, "begin"): [lambda: gin.complete(2), out_in.start, out_bias.start],
            (3, "end"): [end],
        },
        step,
    )
    slot = slot_order(step)
    hook("begin")
    bias_t = bias_all[slot, :, 0:256].T
    for part in range(4):
        product = nt(in_all[slot, part, :IN_ROWS], first_ref[...])
        qkv_ref[part * IN_ROWS : (part + 1) * IN_ROWS, :] = (
            product + bias_t[:IN_ROWS, part : part + 1]
        ).astype(BF16)
    hook("heads")
    for head in range(4):
        if head:
            hook(head)
        attend_head(
            qkv_ref.at[pl.ds(head * IN_ROWS, IN_ROWS)],
            mixed_ref.at[pl.ds(head * 48, 48)],
            logsum_ref.at[head],
        )
    hook("end")


def slot_order(turn):
    return turn + (turn // 2) * (1 - 2 * (turn % 2))


def attend(tokens, vectors, in_own, out_own, ff_own, bias_own):
    rows, width = tokens.shape
    heads = 16
    anywhere = pl.BlockSpec(memory_space=pl.ANY)
    dma = pltpu.SemaphoreType.DMA
    return pl.pallas_call(
        attend_kernel,
        grid=(4,),
        in_specs=[
            pl.BlockSpec((rows, width), lambda s: (0, 0), pipeline_mode=pl.Buffered(1)),
            pl.BlockSpec((8, width), lambda s: (0, 0)),
            anywhere,
            anywhere,
            anywhere,
            anywhere,
        ],
        out_specs=[
            pl.BlockSpec((4 * IN_ROWS, rows), lambda s: (slot_order(s), 0)),
            pl.BlockSpec((4 * 48, rows), lambda s: (slot_order(s), 0)),
            pl.BlockSpec((4, 1, rows), lambda s: (slot_order(s), 0, 0)),
            pl.BlockSpec((rows, width), lambda s: (0, 0)),
            anywhere,
            anywhere,
            anywhere,
        ],
        out_shape=[
            jax.ShapeDtypeStruct((heads * IN_ROWS, rows), BF16),
            jax.ShapeDtypeStruct((heads * 48, rows), BF16),
            jax.ShapeDtypeStruct((heads, 1, rows), F32),
            jax.ShapeDtypeStruct((rows, width), BF16),
            jax.ShapeDtypeStruct((4, 4, HEAD_ROWS, width), BF16),
            jax.ShapeDtypeStruct((8, 192, width), BF16),
            jax.ShapeDtypeStruct((4, 8, 1024), F32),
        ],
        scratch_shapes=[
            pltpu.VMEM((4, 4, HEAD_ROWS, width), BF16),
            pltpu.VMEM((4, 8, 1024), F32),
            dma((4 * GATHER_KINDS,)),
            dma((4 * GATHER_KINDS,)),
            dma((4 * GATHER_KINDS,)),
            dma((4 * GATHER_KINDS,)),
            dma((4,)),
            dma((4,)),
            dma((16,)),
            dma((4,)),
        ],
        compiler_params=pltpu.CompilerParams(
            vmem_limit_bytes=62 << 20, collective_id=0, has_side_effects=True
        ),
        cost_estimate=pl.CostEstimate(
            flops=30_000_000_000, bytes_accessed=30_000_000, transcendentals=19_000_000
        ),
        name="attend",
    )(tokens, vectors, in_own, out_own, ff_own, bias_own)


class Reduce:
    def __init__(self, slot, other, total, got, split, send, recv):
        self.slot, self.other, self.total, self.got, self.split = slot, other, total, got, split
        self.send, self.recv = send, recv
        self.dp, self.base, self.y, self.x, self.core, self.mp = place()

    def copy(self, kind):
        y, x, core = self.y, self.x, self.core
        first, late = pl.ds(0, self.split), pl.ds(self.split, self.total.shape[2] - self.split)
        got = self.got
        near = lambda y, x, core: (self.base + 4 * y + 2 * x + core, self.mp)
        to_x, to_y = near(y, flip(x), core), near(flip(y), x, core)
        src, dst, device = {
            0: lambda: (self.other, got[0], near(y, x, flip(core))),
            1: lambda: (self.total.at[:, flip(x), first], got[1], to_x),
            2: lambda: (self.total.at[flip(y), :, late], got[2], to_y),
            3: lambda: (self.total.at[flip(y), x, first], got[3], to_y),
            4: lambda: (self.total.at[y, flip(x), late], got[4], to_x),
            5: lambda: (
                self.total.at[y, x],
                got[5],
                (self.dp, lax.rem(self.mp + self.slot, lax.axis_size("mp"))),
            ),
        }[kind]()
        index = kind * 4 + self.slot
        return pltpu.make_async_remote_copy(
            src_ref=src,
            dst_ref=dst,
            send_sem=self.send.at[index],
            recv_sem=self.recv.at[index],
            device_id=device,
            device_id_type=MESH,
        )

    def cores(self):
        self.copy(0).start()

    def chips(self):
        self.copy(0).wait_recv()
        for y in range(2):
            for x in range(2):
                self.total[y, x] = add(self.total[y, x], self.got[0][y, x])
        self.copy(1).start()
        self.copy(2).start()

    def chips_again(self):
        x, y, split = self.x, self.y, self.split
        self.copy(1).wait_recv()
        for i in range(2):
            self.total[i, x, :split] = add(self.total[i, x, :split], self.got[1][i])
        self.copy(2).wait_recv()
        for i in range(2):
            self.total[y, i, split:] = add(self.total[y, i, split:], self.got[2][i])
        self.copy(3).start()
        self.copy(4).start()

    def settle(self):
        x, y, split = self.x, self.y, self.split
        self.copy(3).wait_recv()
        self.total[y, x, :split] = add(self.total[y, x, :split], self.got[3][...])
        self.copy(4).wait_recv()
        self.total[y, x, split:] = add(self.total[y, x, split:], self.got[4][...])

    def along(self):
        self.settle()
        if self.slot:
            self.copy(5).start()

    def finish(self, kinds=6):
        for kind in range(kinds if self.slot else 5):
            self.copy(kind).wait_send()

    def result(self):
        if self.slot:
            self.copy(5).wait_recv()
            return self.got[5][...].astype(F32)
        return self.total[self.y, self.x].astype(F32)


REDUCE_KINDS = 6


def add(left, right):
    return (left.astype(F32) + right.astype(F32)).astype(BF16)


def other_bit(index, bit):
    return index + bit * (1 - 2 * lax.rem(index // bit, 2))


def wider_bits():
    bits, bit = [], GROUP
    while bit < lax.axis_size("dp"):
        bits.append(bit)
        bit *= 2
    return bits


class Share:
    def __init__(self, pieces, split, send, recv):
        self.inner = Gather(None, None, ff_piece, split, send, recv)
        self.pieces = pieces

    def copy(self, kind):
        return self.inner.shared(kind, self.pieces, kind)

    def start(self, *kinds):
        for kind in kinds:
            self.copy(kind).start()

    def arrived(self, *kinds):
        for kind in kinds:
            self.copy(kind).wait_recv()

    def spread(self):
        self.start(1, 2, 5)

    def forward(self):
        self.arrived(1)
        self.start(3, 6)
        self.arrived(2)
        self.start(4, 7)

    def last(self):
        self.arrived(3, 4)
        self.start(8)

    def finish(self):
        self.arrived(5, 6, 7, 8)
        for kind in range(1, 9):
            self.copy(kind).wait_send()


class Wide:
    def __init__(self, held, send, recv):
        self.held, self.send, self.recv = held, send, recv

    def copy(self, i, bit):
        dp, mp = lax.axis_index("dp"), lax.axis_index("mp")
        return pltpu.make_async_remote_copy(
            src_ref=self.held.at[2 * i],
            dst_ref=self.held.at[2 * i + 1],
            send_sem=self.send.at[i],
            recv_sem=self.recv.at[i],
            device_id=(other_bit(dp, bit), mp),
            device_id_type=MESH,
        )

    def sum(self, total):
        for i, bit in enumerate(wider_bits()):
            self.held[2 * i] = total.astype(BF16)
            self.copy(i, bit).start()
            self.copy(i, bit).wait()
            total = total + self.held[2 * i + 1].astype(F32)
        return total


def reduce_scratch(slots, rows, split, width):
    dma = pltpu.SemaphoreType.DMA
    late = rows - split
    return [
        pltpu.VMEM((slots, 2, 2, rows, width), BF16),
        pltpu.VMEM((slots, 2, split, width), BF16),
        pltpu.VMEM((slots, 2, late, width), BF16),
        pltpu.VMEM((slots, split, width), BF16),
        pltpu.VMEM((slots, late, width), BF16),
        pltpu.VMEM((slots, rows, width), BF16),
        dma((4 * REDUCE_KINDS,)),
        dma((4 * REDUCE_KINDS,)),
    ]


REDUCE_REFS = 8


def reduces_of(slots, other, total, scratch, split):
    *got, send, recv = scratch
    return {
        slot: Reduce(slot, other(i), total(i), [ref.at[i] for ref in got], split, send, recv)
        for i, slot in enumerate(slots)
    }


def share_scratch(rows, width):
    dma = pltpu.SemaphoreType.DMA
    wide = max(len(wider_bits()), 1)
    return [
        pltpu.VMEM((8, rows, width), BF16),
        pltpu.VMEM((2 * wide, rows, width), BF16),
        dma((GATHER_KINDS,)),
        dma((GATHER_KINDS,)),
        dma((wide,)),
        dma((wide,)),
    ]


SHARE_REFS = 6


def attend_back_head(qkv_ref, back_ref, mixed_ref, logsum_ref, out_ref, held):
    rows = {}

    def score(start, length, first, chunk):
        if start not in rows:
            whole = slice(start, start + length)
            key_t = qkv_ref[48:96, whole]
            rows[start] = (key_t, key_t.T, qkv_ref[96:144, whole].T)
        cols = slice(first, first + chunk)
        return (
            nn(rows[start][1], qkv_ref[0:48, cols]),
            nn(rows[start][2], back_ref[:, cols]),
        )

    def soften(item, scores, back_probs):
        cols = slice(item[2], item[2] + item[3])
        inner = jnp.sum(
            back_ref[:, cols].astype(F32) * mixed_ref[:, cols].astype(F32), axis=0, keepdims=True
        )
        probs = jnp.exp2(scores * SCALE_LOG2 - logsum_ref[:, cols])
        return probs.astype(BF16), (probs * (back_probs - inner)).astype(BF16)

    def pull(item, probs, back_scores):
        start, length, first, chunk = item
        cols, whole = slice(first, first + chunk), slice(start, start + length)
        query_t, back_t = qkv_ref[0:48, cols], back_ref[:, cols]
        out_ref[0:48, cols] = (nn(rows[start][0], back_scores) * SCALE).astype(BF16)
        back_key = nt(query_t, back_scores)
        back_value = nt(back_t, probs)
        if first > start:
            back_key = back_key + held[0:48, 0:length]
            back_value = back_value + held[48:96, 0:length]
        if first + chunk < start + length:
            held[0:48, 0:length] = back_key
            held[48:96, 0:length] = back_value
        else:
            out_ref[48:96, whole] = (back_key * SCALE).astype(BF16)
            out_ref[96:144, whole] = back_value.astype(BF16)

    items = chunks_of(IMAGES, BACK_CHUNK)
    early = {0: score(*items[0])}
    for i in range(len(items)):
        if i + 1 < len(items):
            early[i + 1] = score(*items[i + 1])
        pull(items[i], *soften(items[i], *early.pop(i)))


def attend_back_kernel(
    qkv_ref,
    back_ref,
    mixed_ref,
    logsum_ref,
    first_ref,
    out_grad_ref,
    ff_part_ref,
    ff_grad,
    out_ref,
    sums_ref,
    part_ref,
    piece_ref,
    ff_out,
    in_grad,
    held,
    ff_total,
    grads,
    local,
    *scratch,
):
    step = pl.program_id(0)
    dp, base, y, x, core, mp = place()
    ff_scratch, scratch = scratch[:REDUCE_REFS], scratch[REDUCE_REFS:]
    in_scratch, scratch = scratch[:REDUCE_REFS], scratch[REDUCE_REFS:]
    final, wide, share_send, share_recv, wide_send, wide_recv = scratch
    ff = reduces_of(
        (2, 3),
        lambda i: ff_grad.at[i, :, :, flip(core)],
        lambda i: ff_total.at[i],
        ff_scratch,
        96,
    )
    ins = reduces_of(
        (1, 2, 3),
        lambda i: grads.at[i + 1, :, :, flip(core)],
        lambda i: grads.at[i + 1, :, :, core],
        in_scratch,
        48,
    )
    share = Share(final, 96, share_send, share_recv)
    written = pltpu.make_async_copy(final, ff_out, local.at[2])
    in_written = pltpu.make_async_copy(grads.at[0], in_grad, local.at[3])

    def own(i):
        return pltpu.make_async_copy(
            ff_grad.at[i, :, :, core], ff_total.at[i], local.at[i]
        )

    def begin():
        own(0).start()
        own(1).start()
        greet(group_partners(True))
        ff[2].cores()
        ff[3].cores()

    def chips(slot):
        own(slot - 2).wait()
        ff[slot].chips()

    def finish_ff():
        total = ff_part_ref[...] + ff[2].result() + ff[3].result()
        total = Wide(wide, wide_send, wide_recv).sum(total)
        final[4 * y + 2 * x + core] = total.astype(BF16)
        share.spread()

    def end():
        in_written.start()
        share.finish()
        written.start()
        part_ref[...] = ins[1].result() + ins[2].result()
        ins[3].settle()
        piece_ref[...] = ins[3].total[y, x]
        for reduce in [*ff.values(), ins[1], ins[2]]:
            reduce.finish()
        ins[3].finish(5)
        written.wait()
        in_written.wait()

    hook = hooks_of(
        {
            (0, 0): [begin],
            (0, 1): [lambda: chips(2)],
            (0, 3): [ff[2].chips_again, lambda: chips(3)],
            (1, 0): [ins[2].cores],
            (1, 2): [ff[2].along],
            (1, 3): [ff[3].chips_again, ins[2].chips],
            (2, 0): [ff[3].along, ins[1].cores],
            (2, 1): [ins[2].chips_again, ins[1].chips],
            (2, 3): [finish_ff, ins[2].along, ins[1].chips_again],
            (3, 0): [ins[1].along, ins[3].cores],
            (3, 1): [share.forward, ins[3].chips],
            (3, 3): [share.last, ins[3].chips_again],
            (3, "end"): [end],
        },
        step,
    )
    for head in range(4):
        hook(head)
        attend_back_head(
            qkv_ref.at[pl.ds(head * IN_ROWS, IN_ROWS)],
            back_ref.at[pl.ds(head * 48, 48)],
            mixed_ref.at[pl.ds(head * 48, 48)],
            logsum_ref.at[head],
            out_ref.at[pl.ds(head * IN_ROWS, IN_ROWS)],
            held,
        )
    slot = back_order(step)
    for head in range(4):
        rows = out_ref[head * IN_ROWS : (head + 1) * IN_ROWS, :]
        grad = nn(rows, first_ref[...]).astype(BF16)
        grads[slot, head // 2, head % 2, 0] = grad[:96]
        grads[slot, head // 2, head % 2, 1, 0:48] = grad[96:]
        grads[slot, head // 2, head % 2, 1, 48:96] = out_grad_ref[0, head]
    sums_ref[0] = nt(jnp.ones((8, out_ref.shape[1]), BF16), out_ref[...])
    hook("end")


def back_order(turn):
    return 2 - turn + (turn // 2) * (3 - 2 * (turn // 3))


def attend_back(qkv, back_mixed, mixed, logsum, first, out_grad, ff_part, ff_grad):
    rows, width = first.shape
    anywhere = pl.BlockSpec(memory_space=pl.ANY)
    return pl.pallas_call(
        attend_back_kernel,
        grid=(4,),
        in_specs=[
            pl.BlockSpec((4 * IN_ROWS, rows), lambda s: (back_order(s), 0)),
            pl.BlockSpec((4 * 48, rows), lambda s: (back_order(s), 0)),
            pl.BlockSpec((4 * 48, rows), lambda s: (back_order(s), 0)),
            pl.BlockSpec((4, 1, rows), lambda s: (back_order(s), 0, 0)),
            pl.BlockSpec((rows, width), lambda s: (0, 0), pipeline_mode=pl.Buffered(1)),
            pl.BlockSpec((1, 4, 48, width), lambda s: (back_order(s), 0, 0, 0)),
            pl.BlockSpec((192, width), lambda s: (0, 0), pipeline_mode=pl.Buffered(1)),
            anywhere,
        ],
        out_specs=[
            pl.BlockSpec((4 * IN_ROWS, rows), lambda s: (back_order(s), 0)),
            pl.BlockSpec((1, 8, 4 * IN_ROWS), lambda s: (back_order(s), 0, 0)),
            pl.BlockSpec((96, width), lambda s: (0, 0)),
            pl.BlockSpec((96, width), lambda s: (0, 0)),
            anywhere,
            anywhere,
        ],
        out_shape=[
            jax.ShapeDtypeStruct((16 * IN_ROWS, rows), BF16),
            jax.ShapeDtypeStruct((4, 8, 4 * IN_ROWS), F32),
            jax.ShapeDtypeStruct((96, width), F32),
            jax.ShapeDtypeStruct((96, width), BF16),
            jax.ShapeDtypeStruct((8, 192, width), BF16),
            jax.ShapeDtypeStruct((2, 2, 2, 96, width), BF16),
        ],
        scratch_shapes=[
            pltpu.VMEM((96, LONG_LEN), F32),
            pltpu.VMEM((2, 2, 2, 192, width), BF16),
            pltpu.VMEM((4, 2, 2, 2, 96, width), BF16),
            pltpu.SemaphoreType.DMA((4,)),
        ]
        + reduce_scratch(2, 192, 96, width)
        + reduce_scratch(3, 96, 48, width)
        + share_scratch(192, width),
        compiler_params=pltpu.CompilerParams(
            vmem_limit_bytes=62 << 20, collective_id=1, has_side_effects=True
        ),
        cost_estimate=pl.CostEstimate(
            flops=45_000_000_000, bytes_accessed=40_000_000, transcendentals=19_000_000
        ),
        name="attend_back",
    )(qkv, back_mixed, mixed, logsum, first, out_grad, ff_part, ff_grad)


BLOCK = 256


def tail_kernel(
    back_qkv_ref,
    in_ref,
    tokens_ref,
    resid_ref,
    vector_ref,
    feed_small_ref,
    up_sums_ref,
    bias_sums_ref,
    part_ref,
    piece_ref,
    ff_ref,
    in_grad,
    input_ref,
    small_ref,
    up_ref,
    down_ref,
    in_ref_out,
    out_ref_out,
    total,
    piece_got,
    sums,
    sum_got,
    wide_got,
    along_got,
    sum_send,
    sum_recv,
    along_send,
    along_recv,
    piece_sem,
    local,
    *scratch,
    blocks,
):
    step = pl.program_id(0)
    width = tokens_ref.shape[1]
    dp, base, y, x, core, mp = place()
    ways = lax.axis_size("mp")
    final, wide, share_send, share_recv, wide_send, wide_recv = scratch[REDUCE_REFS:]
    reduce = reduces_of(
        (0,),
        lambda i: in_grad.at[:, :, flip(core)],
        lambda i: total,
        scratch[:REDUCE_REFS],
        48,
    )[0]
    share = Share(final, 48, share_send, share_recv)
    own = pltpu.make_async_copy(in_grad.at[:, :, core], total, local.at[0])

    piece = pltpu.make_async_remote_copy(
        src_ref=piece_ref,
        dst_ref=piece_got,
        send_sem=piece_sem.at[0],
        recv_sem=piece_sem.at[1],
        device_id=(dp, lax.rem(mp + 3, ways)),
        device_id_type=MESH,
    )

    def begin():
        own.start()
        greet(every_partner())
        reduce.cores()
        piece.start()
        sums[0] = jnp.zeros_like(sums[0])
        sums[0, 0:8, :] = feed_small_ref[...]
        sums[0, 4:6, :] = up_sums_ref[0:2, :]
        for slot in range(4):
            sums[0, 8 + slot : 9 + slot, 0 : 4 * IN_ROWS] = bias_sums_ref[slot, 0:1]
        own.wait()
        reduce.chips()

    def finish_in():
        piece.wait_recv()
        whole = part_ref[...] + reduce.result() + piece_got[...].astype(F32)
        whole = Wide(wide, wide_send, wide_recv).sum(whole)
        final[4 * y + 2 * x + core] = whole.astype(BF16)
        share.spread()

    def along():
        reduce.along()
        finish_in()

    def write_up():
        up_ref[...] = ff_ref[:, :96].reshape(width, width).astype(F32)

    def write_down():
        down_ref[...] = ff_ref[:, 96:].reshape(width, width).astype(F32).T

    hook = hooks_of(
        {
            (0, "begin"): [begin],
            (1, "end"): [reduce.chips_again],
            (2, "begin"): [write_up],
            (2, "end"): [along],
            (3, "begin"): [write_down],
            (4, "end"): [share.forward],
        },
        step,
    )
    hook("begin")
    inputs = tokens_ref[...].astype(F32)
    average = jnp.mean(inputs, axis=-1, keepdims=True)
    centred = inputs - average
    inverse = lax.rsqrt(jnp.mean(centred * centred, axis=-1, keepdims=True) + epsilon)
    scaled = centred * inverse
    back_first = None
    for slot in range(4):
        weight = in_ref[slot, :, :IN_ROWS].reshape(4 * IN_ROWS, width)
        part = tn(back_qkv_ref[slot * 4 * IN_ROWS : (slot + 1) * 4 * IN_ROWS, :], weight)
        back_first = part if slot == 0 else back_first + part
    sums[0, 12:13, :] += jnp.sum(back_first * scaled, axis=0, keepdims=True)
    sums[0, 13:14, :] += jnp.sum(back_first, axis=0, keepdims=True)
    back_norm = back_first * vector_ref[4:5, :]
    input_ref[...] = resid_ref[...] + inverse * (
        back_norm
        - jnp.mean(back_norm, axis=-1, keepdims=True)
        - scaled * jnp.mean(back_norm * scaled, axis=-1, keepdims=True)
    )

    hook("end")

    @pl.when(step == blocks - 1)
    def _():
        wide = wider_bits()
        near = range(1, GROUP)

        def near_copy(k):
            return pltpu.make_async_remote_copy(
                src_ref=sums.at[0],
                dst_ref=sum_got.at[k - 1],
                send_sem=sum_send.at[k - 1],
                recv_sem=sum_recv.at[k - 1],
                device_id=(base + near_index(y, x, core, k), mp),
                device_id_type=MESH,
            )

        def wide_copy(i):
            return pltpu.make_async_remote_copy(
                src_ref=sums.at[i + 1],
                dst_ref=wide_got.at[i],
                send_sem=sum_send.at[GROUP - 1 + i],
                recv_sem=sum_recv.at[GROUP - 1 + i],
                device_id=(other_bit(dp, wide[i]), mp),
                device_id_type=MESH,
            )

        def along_copy(slot):
            return pltpu.make_async_remote_copy(
                src_ref=sums.at[len(wide) + 1],
                dst_ref=along_got.at[slot - 1],
                send_sem=along_send.at[slot - 1],
                recv_sem=along_recv.at[slot - 1],
                device_id=(dp, lax.rem(mp + slot, ways)),
                device_id_type=MESH,
            )

        for k in near:
            near_copy(k).start()
        share.last()
        result = sums[0]
        for k in near:
            near_copy(k).wait_recv()
            result = result + sum_got[k - 1]
        sums[1] = result
        for i in range(len(wide)):
            wide_copy(i).start()
            wide_copy(i).wait_recv()
            sums[i + 2] = sums[i + 1] + wide_got[i]
        for slot in (1, 2, 3):
            along_copy(slot).start()
        share.finish()
        for head in range(4):
            low, high = final[2 * head].astype(F32), final[2 * head + 1].astype(F32)
            rows = slice(48 * head, 48 * head + 48)
            in_ref_out[0, rows], in_ref_out[1, rows] = low[:48], low[48:]
            in_ref_out[2, rows], out_ref_out[rows] = high[:48], high[48:]
        small_ref[...] = sums[len(wide) + 1]
        for slot in (1, 2, 3):
            along_copy(slot).wait_recv()
            more = along_got[slot - 1]
            small_ref[0:4, :] += more[0:4]
            small_ref[12:14, :] += more[12:14]
            small_ref[4:5, :] += more[4 + slot : 5 + slot]
            small_ref[8:9, :] += more[8 + slot : 9 + slot]
        for k in near:
            near_copy(k).wait_send()
        for i in range(len(wide)):
            wide_copy(i).wait_send()
        for slot in (1, 2, 3):
            along_copy(slot).wait_send()
        reduce.finish()
        piece.wait_send()


def near_index(y, x, core, k):
    y = flip(y) if k & 4 else y
    x = flip(x) if k & 2 else x
    core = flip(core) if k & 1 else core
    return 4 * y + 2 * x + core


def every_partner():
    dp, base, y, x, core, mp = place()
    ways = lax.axis_size("mp")
    return (
        [(dp, lax.rem(mp + k, ways)) for k in (1, 2, 3)]
        + [(base + near_index(y, x, core, k), mp) for k in range(1, GROUP)]
        + [(other_bit(dp, bit), mp) for bit in wider_bits()]
    )


def tail(
    back_qkv, in_all, tokens, resid, vectors, small_sums, bias_sums, in_part, piece, ff_sum, in_grad
):
    rows, width = tokens.shape
    blocks = rows // BLOCK
    bits = len(wider_bits())
    anywhere = pl.BlockSpec(memory_space=pl.ANY)
    one = pl.Buffered(1)
    dma = pltpu.SemaphoreType.DMA
    return pl.pallas_call(
        functools.partial(tail_kernel, blocks=blocks),
        grid=(blocks,),
        in_specs=[
            pl.BlockSpec((16 * IN_ROWS, BLOCK), lambda s: (0, s)),
            pl.BlockSpec((4, 4, HEAD_ROWS, width), lambda s: (0, 0, 0, 0), pipeline_mode=one),
            pl.BlockSpec((BLOCK, width), lambda s: (s, 0)),
            pl.BlockSpec((BLOCK, width), lambda s: (s, 0)),
            pl.BlockSpec((8, width), lambda s: (0, 0)),
            pl.BlockSpec((8, width), lambda s: (0, 0)),
            pl.BlockSpec((8, width), lambda s: (0, 0)),
            pl.BlockSpec((4, 8, 4 * IN_ROWS), lambda s: (0, 0, 0)),
            pl.BlockSpec((96, width), lambda s: (0, 0)),
            pl.BlockSpec((96, width), lambda s: (0, 0)),
            pl.BlockSpec((8, 192, width), lambda s: (0, 0, 0), pipeline_mode=one),
            anywhere,
        ],
        out_specs=[
            pl.BlockSpec((BLOCK, width), lambda s: (s, 0)),
            pl.BlockSpec((16, width), lambda s: (0, 0)),
            pl.BlockSpec((width, width), lambda s: (0, 0)),
            pl.BlockSpec((width, width), lambda s: (0, 0)),
            pl.BlockSpec((3, 192, width), lambda s: (0, 0, 0)),
            pl.BlockSpec((192, width), lambda s: (0, 0)),
        ],
        out_shape=[
            jax.ShapeDtypeStruct((rows, width), F32),
            jax.ShapeDtypeStruct((16, width), F32),
            jax.ShapeDtypeStruct((width, width), F32),
            jax.ShapeDtypeStruct((width, width), F32),
            jax.ShapeDtypeStruct((3, 192, width), F32),
            jax.ShapeDtypeStruct((192, width), F32),
        ],
        scratch_shapes=[
            pltpu.VMEM((2, 2, 96, width), BF16),
            pltpu.VMEM((96, width), BF16),
            pltpu.VMEM((bits + 2, 16, width), F32),
            pltpu.VMEM((GROUP - 1, 16, width), F32),
            pltpu.VMEM((max(bits, 1), 16, width), F32),
            pltpu.VMEM((3, 16, width), F32),
            dma((GROUP - 1 + bits,)),
            dma((GROUP - 1 + bits,)),
            dma((3,)),
            dma((3,)),
            dma((2,)),
            dma((1,)),
        ]
        + reduce_scratch(1, 96, 48, width)
        + share_scratch(96, width),
        compiler_params=pltpu.CompilerParams(
            vmem_limit_bytes=62 << 20, collective_id=2, has_side_effects=True
        ),
        cost_estimate=pl.CostEstimate(
            flops=6_000_000_000, bytes_accessed=30_000_000, transcendentals=2000
        ),
        name="tail",
    )(
        back_qkv,
        in_all,
        tokens,
        resid,
        vectors,
        *small_sums,
        bias_sums,
        in_part,
        piece,
        ff_sum,
        in_grad,
    )


FEED_BLOCKS = 6


def feed_rows(
    second, back_low, slots, ff_refs, bias_ref, act_s, hid_s, rows, width, feed, back_second
):
    for i, slot in enumerate(slots):
        up = ff_refs[i][:, 0:96, :].reshape(width, width)
        down = ff_refs[i][:, 96:192, :].reshape(width, width)
        hidden = nn(second, up) + bias_ref[slot, 0:1, 256:]
        half = 0.5 + 0.5 * lax.erf(hidden * (0.5**0.5))
        act = (hidden * half).astype(BF16)
        slope = half + hidden * (jnp.exp(hidden * hidden * -0.5) * (1.0 / math.sqrt(2 * math.pi)))
        back_hid = (nt(back_low, down) * slope).astype(BF16)
        act_s[i, rows, :] = act
        hid_s[i, rows, :] = back_hid
        fed, pulled = nn(act, down), nt(back_hid, up)
        feed = fed if feed is None else feed + fed
        back_second = pulled if back_second is None else back_second + pulled
    return feed, back_second


def normed(rows_in):
    average = jnp.mean(rows_in, axis=-1, keepdims=True)
    centred = rows_in - average
    inverse = lax.rsqrt(jnp.mean(centred * centred, axis=-1, keepdims=True) + epsilon)
    return centred * inverse, inverse


def live_back(live_ref, grad_ref, step):
    row = step * BLOCK + lax.broadcasted_iota(jnp.int32, (BLOCK, 1), 0)
    limit = jnp.where(
        row < SHORT_ROWS, live_ref[0, 0] * SHORT_LEN, SHORT_ROWS + live_ref[0, 1] * LONG_LEN
    )
    is_live = row < limit
    return is_live, jnp.where(is_live, grad_ref[...].astype(F32), 0.0)


def feed_grads(i, second_t, back_t, act_s, hid_s, ff_grad_ref, up_sum_ref, row, width):
    up = nn(second_t[...], hid_s[i])
    ff_grad_ref[0, :, 0:96, :] = up[:width].astype(BF16).reshape(8, 96, width)
    up_sum_ref[pl.ds(row, 1), :] = up[width : width + 1]
    down = nn(back_t[...], act_s[i])
    ff_grad_ref[0, :, 96:192, :] = down.astype(BF16).reshape(8, 96, width)


def feed_first_kernel(
    live_ref,
    tokens_ref,
    grad_ref,
    mixed_ref,
    out_w_ref,
    own_ref,
    near_ref,
    bias_ref,
    vec_ref,
    ff_own,
    ff_near,
    residual_ref,
    feed_ref,
    back_second_ref,
    ff_grad_ref,
    up_sum_ref,
    ff_late,
    second_t,
    back_t,
    act_s,
    hid_s,
    send,
    recv,
):
    step = pl.program_id(0)
    width = tokens_ref.shape[1]
    late = [None, ff_near, ff_late.at[0], ff_late.at[1]]
    gff = Gather(ff_own, late, ff_piece, 96, send, recv)

    def begin():
        greet(group_partners())
        gff.along(3)
        gff.along(2)
        up_sum_ref[...] = jnp.zeros_like(up_sum_ref)
        second_t[width:, :] = jnp.ones((16, second_t.shape[1]), BF16)

    def end():
        gff.complete(3)
        gff.complete(2)
        gff.finish(2, 3)

    hook = hooks_of(
        {
            (0, "begin"): [begin],
            (2, "begin"): [lambda: gff.spread(3)],
            (3, "begin"): [lambda: gff.spread(2)],
            (5, "begin"): [lambda: gff.forward(3)],
            (6, "begin"): [lambda: gff.last(3), lambda: gff.forward(2)],
            (7, "begin"): [lambda: gff.last(2)],
            (7, "end"): [end],
        },
        step,
    )
    hook("begin")

    @pl.when(step < FEED_BLOCKS)
    def _():
        out_w = out_w_ref[...].reshape(width, width)
        residual = tokens_ref[...].astype(F32) + tn(mixed_ref[...], out_w) + vec_ref[0:1, :]
        residual_ref[...] = residual
        scaled, _ = normed(residual)
        second = (scaled * vec_ref[1:2, :] + vec_ref[2:3, :]).astype(BF16)
        _, back = live_back(live_ref, grad_ref, step)
        back_low = back.astype(BF16)
        rows = pl.ds(pl.multiple_of(step * BLOCK, BLOCK), BLOCK)
        second_t[0:width, rows] = second.T
        back_t[:, rows] = back_low.T
        feed_ref[...], back_second_ref[...] = feed_rows(
            second,
            back_low,
            (0, 1),
            (own_ref, near_ref),
            bias_ref,
            act_s,
            hid_s,
            rows,
            width,
            None,
            None,
        )

    @pl.when(step >= FEED_BLOCKS)
    def _():
        i = step - FEED_BLOCKS
        feed_grads(i, second_t, back_t, act_s, hid_s, ff_grad_ref, up_sum_ref, i, width)

    hook("end")


def feed_last_kernel(
    live_ref,
    residual_ref,
    feed_ref,
    back_second_ref,
    grad_ref,
    mixed_ref,
    out_w_ref,
    ff_ref,
    bias_ref,
    vec_ref,
    ff_near_grad,
    output_ref,
    resid_ref,
    back_mixed_ref,
    ff_grad_ref,
    out_grad_ref,
    small_ref,
    part_ref,
    second_t,
    back_t,
    act_s,
    hid_s,
    out_acc,
    ff_total,
    local,
    *scratch,
):
    step = pl.program_id(0)
    width = residual_ref.shape[1]
    dp, base, y, x, core, mp = place()
    ff = reduces_of(
        (0, 1),
        lambda i: ff_near_grad.at[i, :, :, flip(core)],
        lambda i: ff_total.at[i],
        scratch,
        96,
    )

    def own(i):
        return pltpu.make_async_copy(ff_near_grad.at[i, :, :, core], ff_total.at[i], local.at[i])

    def begin():
        own(1).start()
        own(0).start()
        greet(group_partners())
        ff[1].cores()
        ff[0].cores()
        small_ref[...] = jnp.zeros_like(small_ref)
        second_t[width:, :] = jnp.ones((16, second_t.shape[1]), BF16)

    def chips(slot):
        own(slot).wait()
        ff[slot].chips()

    def end():
        part_ref[...] = ff[0].result() + ff[1].result()
        ff[0].finish()
        ff[1].finish()

    hook = hooks_of(
        {
            (0, "begin"): [begin],
            (1, "begin"): [lambda: chips(1)],
            (3, "begin"): [ff[1].chips_again, lambda: chips(0)],
            (5, "begin"): [ff[1].along],
            (6, "begin"): [ff[0].chips_again],
            (7, "begin"): [ff[0].along],
            (7, "end"): [end],
        },
        step,
    )
    hook("begin")

    @pl.when(step < FEED_BLOCKS)
    def _():
        out_w = out_w_ref[...].reshape(width, width)
        residual = residual_ref[...]
        scaled, inverse = normed(residual)
        gain = vec_ref[1:2, :]
        second = (scaled * gain + vec_ref[2:3, :]).astype(BF16)
        is_live, back = live_back(live_ref, grad_ref, step)
        back_low = back.astype(BF16)
        rows = pl.ds(pl.multiple_of(step * BLOCK, BLOCK), BLOCK)
        second_t[0:width, rows] = second.T
        back_t[:, rows] = back_low.T
        feed, back_second = feed_rows(
            second,
            back_low,
            (2, 3),
            (ff_ref.at[0], ff_ref.at[1]),
            bias_ref,
            act_s,
            hid_s,
            rows,
            width,
            feed_ref[...],
            back_second_ref[...],
        )
        output_ref[...] = jnp.where(is_live, residual + feed + vec_ref[3:4, :], 0.0).astype(BF16)
        small_ref[1:2, :] += jnp.sum(back_second * scaled, axis=0, keepdims=True)
        small_ref[2:3, :] += jnp.sum(back_second, axis=0, keepdims=True)
        small_ref[3:4, :] += jnp.sum(back, axis=0, keepdims=True)
        back_norm = back_second * gain
        back_resid = back + inverse * (
            back_norm
            - jnp.mean(back_norm, axis=-1, keepdims=True)
            - scaled * jnp.mean(back_norm * scaled, axis=-1, keepdims=True)
        )
        small_ref[0:1, :] += jnp.sum(back_resid, axis=0, keepdims=True)
        resid_ref[...] = back_resid
        branch = back_resid.astype(BF16)
        back_mixed_ref[...] = nt(out_w, branch).astype(BF16)
        part = nn(mixed_ref[...], branch)

        @pl.when(step == 0)
        def _():
            out_acc[...] = part

        @pl.when(step > 0)
        def _():
            out_acc[...] += part

        @pl.when(step == FEED_BLOCKS - 1)
        def _():
            out_grad_ref[...] = out_acc[...].astype(BF16).reshape(out_grad_ref.shape)

    @pl.when(step >= FEED_BLOCKS)
    def _():
        i = step - FEED_BLOCKS
        feed_grads(i, second_t, back_t, act_s, hid_s, ff_grad_ref, small_ref, 6 + i, width)

    hook("end")


def feed_first(live, tokens, out_grad, mixed, in_all, ff_near, bias_all, vectors, ff_own):
    rows, width = tokens.shape
    anywhere = pl.BlockSpec(memory_space=pl.ANY)
    one = pl.Buffered(1)
    last = FEED_BLOCKS - 1
    row = pl.BlockSpec((BLOCK, width), lambda s: (jnp.minimum(s, last), 0))
    return pl.pallas_call(
        feed_first_kernel,
        grid=(FEED_BLOCKS + 2,),
        in_specs=[
            pl.BlockSpec(memory_space=pltpu.SMEM),
            row,
            row,
            pl.BlockSpec((width, BLOCK), lambda s: (0, jnp.minimum(s, last))),
            pl.BlockSpec((4, 4, 48, width), lambda s: (0, 0, 3, 0), pipeline_mode=one),
            pl.BlockSpec((8, 192, width), lambda s: (0, 0, 0), pipeline_mode=one),
            pl.BlockSpec((8, 192, width), lambda s: (0, 0, 0), pipeline_mode=one),
            pl.BlockSpec((4, 8, 1024), lambda s: (0, 0, 0), pipeline_mode=one),
            pl.BlockSpec((8, width), lambda s: (0, 0), pipeline_mode=one),
            anywhere,
            anywhere,
        ],
        out_specs=[
            row,
            row,
            row,
            pl.BlockSpec(
                (1, 8, 192, width), lambda s: (jnp.maximum(s - FEED_BLOCKS, 0), 0, 0, 0)
            ),
            pl.BlockSpec((8, width), lambda s: (0, 0)),
            anywhere,
        ],
        out_shape=[
            jax.ShapeDtypeStruct((rows, width), F32),
            jax.ShapeDtypeStruct((rows, width), F32),
            jax.ShapeDtypeStruct((rows, width), F32),
            jax.ShapeDtypeStruct((2, 8, 192, width), BF16),
            jax.ShapeDtypeStruct((8, width), F32),
            jax.ShapeDtypeStruct((2, 8, 192, width), BF16),
        ],
        scratch_shapes=[
            pltpu.VMEM((width + 16, rows), BF16),
            pltpu.VMEM((width, rows), BF16),
            pltpu.VMEM((2, rows, width), BF16),
            pltpu.VMEM((2, rows, width), BF16),
            pltpu.SemaphoreType.DMA((4 * GATHER_KINDS,)),
            pltpu.SemaphoreType.DMA((4 * GATHER_KINDS,)),
        ],
        compiler_params=pltpu.CompilerParams(
            vmem_limit_bytes=62 << 20, collective_id=3, has_side_effects=True
        ),
        cost_estimate=pl.CostEstimate(
            flops=24_000_000_000, bytes_accessed=45_000_000, transcendentals=5_000_000
        ),
        name="feed_first",
    )(live, tokens, out_grad, mixed, in_all, ff_own, ff_near, bias_all, vectors, ff_own, ff_near)


def feed_last(
    live,
    residual,
    feed,
    back_second,
    out_grad,
    mixed,
    in_all,
    ff_late,
    bias_all,
    vectors,
    ff_near_grad,
):
    rows, width = out_grad.shape
    anywhere = pl.BlockSpec(memory_space=pl.ANY)
    one = pl.Buffered(1)
    last = FEED_BLOCKS - 1
    row = pl.BlockSpec((BLOCK, width), lambda s: (jnp.minimum(s, last), 0))
    column = pl.BlockSpec((width, BLOCK), lambda s: (0, jnp.minimum(s, last)))
    return pl.pallas_call(
        feed_last_kernel,
        grid=(FEED_BLOCKS + 2,),
        in_specs=[
            pl.BlockSpec(memory_space=pltpu.SMEM),
            row,
            row,
            row,
            row,
            column,
            pl.BlockSpec((4, 4, 48, width), lambda s: (0, 0, 3, 0), pipeline_mode=one),
            pl.BlockSpec((2, 8, 192, width), lambda s: (0, 0, 0, 0), pipeline_mode=one),
            pl.BlockSpec((4, 8, 1024), lambda s: (0, 0, 0), pipeline_mode=one),
            pl.BlockSpec((8, width), lambda s: (0, 0), pipeline_mode=one),
            anywhere,
        ],
        out_specs=[
            row,
            row,
            column,
            pl.BlockSpec(
                (1, 8, 192, width), lambda s: (jnp.maximum(s - FEED_BLOCKS, 0), 0, 0, 0)
            ),
            pl.BlockSpec((4, 4, 48, width), lambda s: (0, 0, 0, 0)),
            pl.BlockSpec((8, width), lambda s: (0, 0)),
            pl.BlockSpec((192, width), lambda s: (0, 0)),
        ],
        out_shape=[
            jax.ShapeDtypeStruct((rows, width), BF16),
            jax.ShapeDtypeStruct((rows, width), F32),
            jax.ShapeDtypeStruct((width, rows), BF16),
            jax.ShapeDtypeStruct((2, 8, 192, width), BF16),
            jax.ShapeDtypeStruct((4, 4, 48, width), BF16),
            jax.ShapeDtypeStruct((8, width), F32),
            jax.ShapeDtypeStruct((192, width), F32),
        ],
        scratch_shapes=[
            pltpu.VMEM((width + 16, rows), BF16),
            pltpu.VMEM((width, rows), BF16),
            pltpu.VMEM((2, rows, width), BF16),
            pltpu.VMEM((2, rows, width), BF16),
            pltpu.VMEM((width, width), F32),
            pltpu.VMEM((2, 2, 2, 192, width), BF16),
            pltpu.SemaphoreType.DMA((2,)),
        ]
        + reduce_scratch(2, 192, 96, width),
        compiler_params=pltpu.CompilerParams(
            vmem_limit_bytes=62 << 20, collective_id=4, has_side_effects=True
        ),
        cost_estimate=pl.CostEstimate(
            flops=28_000_000_000, bytes_accessed=55_000_000, transcendentals=5_000_000
        ),
        name="feed_last",
    )(
        live,
        residual,
        feed,
        back_second,
        out_grad,
        mixed,
        in_all,
        ff_late,
        bias_all,
        vectors,
        ff_near_grad.reshape(2, 2, 2, 2, 192, width),
    )


def local(
    tokens,
    out_grad,
    live_images,
    first_gain,
    first_shift,
    project_in,
    query_value_bias,
    project_out,
    output_bias,
    second_gain,
    second_shift,
    up_weight,
    up_bias,
    down_weight,
    down_bias,
):
    width = tokens.shape[1]
    own_heads = project_in.shape[2] // HEAD_DIM
    ff_own = jnp.concatenate(
        [up_weight.reshape(8, -1, width), down_weight.reshape(8, -1, width)], axis=1
    )
    pair_bias = query_value_bias.astype(F32).reshape(2, own_heads, HEAD_DIM)
    own_bias = jnp.concatenate([pair_bias[0], jnp.zeros_like(pair_bias[0]), pair_bias[1]], axis=1)
    bias_own = jnp.concatenate(
        [
            jnp.pad(own_bias, ((0, 8 - own_heads), (0, 256 - own_bias.shape[1]))),
            jnp.pad(up_bias.astype(F32)[None], ((0, 7), (0, 0))),
        ],
        axis=1,
    )
    row = lax.broadcasted_iota(jnp.int32, (8, width), 0)
    vectors = jnp.zeros((8, width), F32)
    for i, vector in enumerate(
        (output_bias, second_gain, second_shift, down_bias, first_gain, first_shift)
    ):
        vectors = jnp.where(row == i, vector[None], vectors)
    qkv, mixed, logsum, first, in_all, ff_near, bias_all = attend(
        tokens, vectors, project_in.transpose(1, 2, 0), project_out, ff_own, bias_own
    )
    residual, feed, back_second, near_grad, up_sums, ff_late = feed_first(
        live_images, tokens, out_grad, mixed, in_all, ff_near, bias_all, vectors, ff_own
    )
    output, resid, back_mixed, late_grad, out_grads, feed_small, ff_part = feed_last(
        live_images,
        residual,
        feed,
        back_second,
        out_grad,
        mixed,
        in_all,
        ff_late,
        bias_all,
        vectors,
        near_grad,
    )
    back_qkv, bias_sums, in_part, piece, ff_sum, in_grad = attend_back(
        qkv,
        back_mixed,
        mixed,
        logsum,
        first,
        out_grads,
        ff_part,
        late_grad.reshape(2, 2, 2, 2, 192, width),
    )
    input_grad, small, grad_up, grad_down, grad_in, grad_out = tail(
        back_qkv,
        in_all,
        tokens,
        resid,
        vectors,
        (feed_small, up_sums),
        bias_sums,
        in_part,
        piece,
        ff_sum,
        in_grad,
    )
    grad_in = grad_in.transpose(2, 0, 1)
    pair_sum = small[8, : 4 * IN_ROWS].reshape(own_heads, 3, HEAD_DIM)
    grad_pair = jnp.stack([pair_sum[:, 0].reshape(-1), pair_sum[:, 2].reshape(-1)])
    return (
        output,
        input_grad,
        small[12],
        small[13],
        grad_in,
        grad_pair,
        grad_out,
        small[0],
        small[1],
        small[2],
        grad_up,
        small[4],
        grad_down,
        small[3],
    )


def solution(mesh):
    rows = P(("dp", "mp"), None)
    return jax.shard_map(
        local,
        mesh=mesh,
        in_specs=(
            rows,
            rows,
            rows,
            P(),
            P(),
            P(None, None, "mp"),
            P(None, "mp"),
            P("mp", None),
            P(),
            P(),
            P(),
            P(None, "mp"),
            P("mp"),
            P("mp", None),
            P(),
        ),
        out_specs=(
            rows,
            rows,
            P(),
            P(),
            P(None, None, "mp"),
            P(None, "mp"),
            P("mp", None),
            P(),
            P(),
            P(),
            P(None, "mp"),
            P("mp"),
            P("mp", None),
            P(),
        ),
        check_vma=False,
    )
```

time: 324 us -> 302 us (0.932)
  Pallas kernels: 292 us -> 275 us
  local copies, waits for them, and re-layouts: 21 us -> 16.3 us
    pallas_call x1, Pallas kernels: 53.8 us -> 37.2 us  [tail(): pl.pallas_call(functools.partial(tail_kernel, blocks=blocks), grid=(block...]
    unnamed x47 -> x16, local copies, waits for them, and re-layouts: 11.3 us -> 12.7 us
    pallas_call x3 -> x4, Pallas kernels: 238 us -> 237 us  [the longest x1 88.7 us: attend_back(): pl.pallas_call(attend_back_kernel, grid=(4,), in_specs=[pl.BlockSpec((4 *...]
where the time goes in v4:
time: 302 us; the launch traced here: 298 us
  Pallas kernels  275 us (91%)
  local copies, waits for them, and re-layouts  16.3 us (5%)
  other arithmetic  6.63 us (2%)
    pallas_call x1, Pallas kernels, attend_back(): pl.pallas_call(attend_back_kernel, grid=(4,), in_specs=[pl.BlockSpec((4 *...  88.7 us
    pallas_call x1, Pallas kernels, attend(): pl.pallas_call(attend_kernel, grid=(4,), in_specs=[pl.BlockSpec((rows, wi...  59 us
    pallas_call x1, Pallas kernels, feed_last(): pl.pallas_call(feed_last_kernel, grid=(FEED_BLOCKS + 2,), in_specs=[pl.Bl...  45.4 us
    pallas_call x1, Pallas kernels, feed_first(): pl.pallas_call(feed_first_kernel, grid=(FEED_BLOCKS + 2,), in_specs=[pl.B...  44.3 us
    pallas_call x1, Pallas kernels, tail(): pl.pallas_call(functools.partial(tail_kernel, blocks=blocks), grid=(block...  37.2 us
    unnamed x16, local copies, waits for them, and re-layouts  12.7 us

profile of v4, /device:TPU:0, one launch (start us, length us, event | category | flops | bytes accessed | tf_op | source)
XLA Modules:
  0.0 298.4 jit_solution(9815354766604042637)
XLA Ops:
  0.7 0.1 pad.19.clone
  0.7 0.7 convert_element_type.8
  1.5 0.1 squeeze.27
  1.5 0.1 squeeze.28
  1.6 0.1 pad_maximum_fusion.1
  1.7 0.7 broadcast_in_dim.57
  2.4 1.5 select_select_fusion.vector_ref.vec_ref
  3.8 0.6 select_maximum_fusion.bias_own
  4.5 3.2 %pad_maximum_fusion.ff_own.own_ref = bf16[8,192,768]{2,1,0:T(8,128)(2,1)} fusion(bf16[8,96,768]{2,1,0:T(8,128)(2,1)} %bitcast.7, bf16[8,96,768]{2,1,0:T(8,128)(2,1)} %bitcast.8), kind=kLoop, calls=%fused_computation | loop fusion | flops 4718592 | bytes 4718592 | tf_op jit(solution)/shard_map/concatenate | solution.py:1579
  7.7 59.0 %attend.1 = (bf16[2304,1536]{1,0:T(8,128)(2,1)}, bf16[768,1536]{1,0:T(8,128)(2,1)}, f32[16,1,1536]{2,1,0:T(1,128)}, bf16[1536,768]{1,0:T(8,128)(2,1)}, bf16[4,4,...) custom-call(bf16[1536,768]{1,0:T(8,128)(2,1)} %tokens_ref.5, ...), custom_call_target="tpu_custom_call" | custom-call | flops 30000001024 | bytes 30000000 | tf_op jit(solution)/shard_map/attend/pallas_call | solution.py:380
  66.6 44.3 %feed_first.1 = (f32[1536,768]{1,0:T(8,128)}, f32[1536,768]{1,0:T(8,128)}, f32[1536,768]{1,0:T(8,128)}, bf16[2,8,192,768]{3,2,1,0:T(8,128)(2,1)}, f32[8,768]{1,0:T(8,128)}, /*index=5*/bf16[2,8,192,768]{3,2,1,0:T(8,128)(2,1)}) custom-call(s32[1,2]{1,0:T(1,128)} %live_ref.3, bf16[1536,768]{1,0:T(8,128)(2,1)} %tokens_ref.5, bf16[1536,768]{1,0:T(8,128)(2,1)} %grad_ref.3, ...), custom_call_target="tpu_custom_call" | custom-call | flops 24000000000 | bytes 45000000 | tf_op jit(solution)/shard_map/feed_first/pallas_call | solution.py:1421
  110.9 45.4 %feed_last.1 = (bf16[1536,768]{1,0:T(8,128)(2,1)}, f32[1536,768]{1,0:T(8,128)}, bf16[768,1536]{1,0:T(8,128)(2,1)}, bf16[2,8,192,768]{3,2,1,0:T(8,128)(2,1)}, bf1...) custom-call(s32[1,2]{1,0:T(1,128)} %live_ref.3, f32[1536,768]{1,0:T(8,128)} %get-tuple-element.50.residual_ref, ...), custom_call_target="tpu_custom_call" | custom-call | flops 28000000000 | bytes 55000000 | tf_op jit(solution)/shard_map/feed_last/pallas_call | solution.py:1492
  156.4 88.7 %attend_back.1 = (bf16[2304,1536]{1,0:T(8,128)(2,1)}, f32[4,8,576]{2,1,0:T(8,128)}, f32[96,768]{1,0:T(8,128)}, bf16[96,768]{1,0:T(8,128)(2,1)}, bf16[8,192,768]{...) custom-call(bf16[2304,1536]{1,0:T(8,128)(2,1)} %get-tuple-element.56.qkv_ref, ...), custom_call_target="tpu_custom_call" | custom-call | flops 44999999488 | bytes 40000000 | tf_op jit(solution)/shard_map/attend_back/pallas_call | solution.py:802
  245.1 37.2 %tail.1 = (f32[1536,768]{1,0:T(8,128)}, f32[16,768]{1,0:T(8,128)}, f32[768,768]{1,0:T(8,128)}, f32[768,768]{1,0:T(8,128)}, f32[3,192,768]{2,1,0:T(8,128)}, /*index=5*/f32[192,768]{1,0:T(8,128)}) custom-call(bf16[2304,1536]{1,0:T(8,128)(2,1)} %get-tuple-element.63.back_qkv_ref, bf16[4,4,192,768]{3,2,1,0:T(8,128)(2,1)} %get-tuple-element.47.out_w_ref.in_ref, ...), custom_call_target="tpu_custom_call" | custom-call | flops 6000000000 | bytes 30000000 | tf_op jit(solution)/shard_map/tail/pallas_call | solution.py:1073
  282.3 0.7 slice_reduce_fusion.7
  283.0 1.6 slice_reduce_fusion
  284.6 0.1 reshape_squeeze.3
  284.7 0.1 stack_reshape_squeeze.6
  284.8 0.1 stack_reshape_squeeze.7
  284.9 0.6 pad_maximum_fusion.2
  285.5 0.0 copy-start
  285.5 3.4 %copy.35 = bf16[1536,768]{1,0:T(8,128)(2,1)} copy(bf16[1536,768]{1,0:T(8,128)(2,1)} %get-tuple-element.109) | data formatting | bytes 4718592
  288.9 0.0 copy-done
  288.9 0.0 copy-start.3
  288.9 2.2 copy.36
  291.1 0.6 copy-done.3
  291.6 0.0 copy-start.4
  291.6 0.0 copy-start.2
  291.6 1.2 copy.37
  292.8 0.2 copy-done.4
  293.1 0.8 copy.38
  293.9 0.4 copy-done.2
  294.3 0.0 copy-start.1
  294.3 1.4 copy.39
  295.7 1.1 copy-done.1
  296.8 1.4 copy.40
  (7 shorter events, 0.1 us)
Async XLA Ops:
  285.5 3.4 %copy-start = (f32[1536,768]{1,0:T(8,128)S(1)}, f32[1536,768]{1,0:T(8,128)}, u32[]{:S(2)}) copy-start(f32[1536,768]{1,0:T(8,128)} %get-tuple-element.110) | copy-start | bytes 14155780
  288.9 2.8 copy-start.3
  291.6 1.4 copy-start.4
  291.6 2.7 copy-start.2
  294.3 2.5 copy-start.1

commit v5 on v4

--- a/solution.py
+++ b/solution.py
@@ -220,11 +220,11 @@
 
 
 def hooks_of(table, step):
-    def hook(name):
+    def hook(name, head=None):
         for (at, where), actions in table.items():
-            if where == name:
-
-                @pl.when(step == at)
+            if where == name if head is None else isinstance(where, int):
+
+                @pl.when(step == at if head is None else (step == at) & (head == where))
                 def _(actions=actions):
                     for action in actions:
                         action()
@@ -357,14 +357,17 @@
             product + bias_t[:IN_ROWS, part : part + 1]
         ).astype(BF16)
     hook("heads")
-    for head in range(4):
-        if head:
-            hook(head)
+
+    def one_head(head, carry):
+        hook(None, head)
         attend_head(
-            qkv_ref.at[pl.ds(head * IN_ROWS, IN_ROWS)],
-            mixed_ref.at[pl.ds(head * 48, 48)],
+            qkv_ref.at[pl.ds(pl.multiple_of(head * IN_ROWS, 16), IN_ROWS)],
+            mixed_ref.at[pl.ds(pl.multiple_of(head * 48, 16), 48)],
             logsum_ref.at[head],
         )
+        return carry
+
+    lax.fori_loop(0, 4, one_head, 0)
     hook("end")
 
 
@@ -682,195 +685,24 @@
     first_ref,
     out_grad_ref,
     ff_part_ref,
-    ff_grad,
-    out_ref,
-    sums_ref,
-    part_ref,
-    piece_ref,
-    ff_out,
-    in_grad,
-    held,
-    ff_total,
-    grads,
-    local,
-    *scratch,
-):
-    step = pl.program_id(0)
-    dp, base, y, x, core, mp = place()
-    ff_scratch, scratch = scratch[:REDUCE_REFS], scratch[REDUCE_REFS:]
-    in_scratch, scratch = scratch[:REDUCE_REFS], scratch[REDUCE_REFS:]
-    final, wide, share_send, share_recv, wide_send, wide_recv = scratch
-    ff = reduces_of(
-        (2, 3),
-        lambda i: ff_grad.at[i, :, :, flip(core)],
-        lambda i: ff_total.at[i],
-        ff_scratch,
-        96,
-    )
-    ins = reduces_of(
-        (1, 2, 3),
-        lambda i: grads.at[i + 1, :, :, flip(core)],
-        lambda i: grads.at[i + 1, :, :, core],
-        in_scratch,
-        48,
-    )
-    share = Share(final, 96, share_send, share_recv)
-    written = pltpu.make_async_copy(final, ff_out, local.at[2])
-    in_written = pltpu.make_async_copy(grads.at[0], in_grad, local.at[3])
-
-    def own(i):
-        return pltpu.make_async_copy(
-            ff_grad.at[i, :, :, core], ff_total.at[i], local.at[i]
-        )
-
-    def begin():
-        own(0).start()
-        own(1).start()
-        greet(group_partners(True))
-        ff[2].cores()
-        ff[3].cores()
-
-    def chips(slot):
-        own(slot - 2).wait()
-        ff[slot].chips()
-
-    def finish_ff():
-        total = ff_part_ref[...] + ff[2].result() + ff[3].result()
-        total = Wide(wide, wide_send, wide_recv).sum(total)
-        final[4 * y + 2 * x + core] = total.astype(BF16)
-        share.spread()
-
-    def end():
-        in_written.start()
-        share.finish()
-        written.start()
-        part_ref[...] = ins[1].result() + ins[2].result()
-        ins[3].settle()
-        piece_ref[...] = ins[3].total[y, x]
-        for reduce in [*ff.values(), ins[1], ins[2]]:
-            reduce.finish()
-        ins[3].finish(5)
-        written.wait()
-        in_written.wait()
-
-    hook = hooks_of(
-        {
-            (0, 0): [begin],
-            (0, 1): [lambda: chips(2)],
-            (0, 3): [ff[2].chips_again, lambda: chips(3)],
-            (1, 0): [ins[2].cores],
-            (1, 2): [ff[2].along],
-            (1, 3): [ff[3].chips_again, ins[2].chips],
-            (2, 0): [ff[3].along, ins[1].cores],
-            (2, 1): [ins[2].chips_again, ins[1].chips],
-            (2, 3): [finish_ff, ins[2].along, ins[1].chips_again],
-            (3, 0): [ins[1].along, ins[3].cores],
-            (3, 1): [share.forward, ins[3].chips],
-            (3, 3): [share.last, ins[3].chips_again],
-            (3, "end"): [end],
-        },
-        step,
-    )
-    for head in range(4):
-        hook(head)
-        attend_back_head(
-            qkv_ref.at[pl.ds(head * IN_ROWS, IN_ROWS)],
-            back_ref.at[pl.ds(head * 48, 48)],
-            mixed_ref.at[pl.ds(head * 48, 48)],
-            logsum_ref.at[head],
-            out_ref.at[pl.ds(head * IN_ROWS, IN_ROWS)],
-            held,
-        )
-    slot = back_order(step)
-    for head in range(4):
-        rows = out_ref[head * IN_ROWS : (head + 1) * IN_ROWS, :]
-        grad = nn(rows, first_ref[...]).astype(BF16)
-        grads[slot, head // 2, head % 2, 0] = grad[:96]
-        grads[slot, head // 2, head % 2, 1, 0:48] = grad[96:]
-        grads[slot, head // 2, head % 2, 1, 48:96] = out_grad_ref[0, head]
-    sums_ref[0] = nt(jnp.ones((8, out_ref.shape[1]), BF16), out_ref[...])
-    hook("end")
-
-
-def back_order(turn):
-    return 2 - turn + (turn // 2) * (3 - 2 * (turn // 3))
-
-
-def attend_back(qkv, back_mixed, mixed, logsum, first, out_grad, ff_part, ff_grad):
-    rows, width = first.shape
-    anywhere = pl.BlockSpec(memory_space=pl.ANY)
-    return pl.pallas_call(
-        attend_back_kernel,
-        grid=(4,),
-        in_specs=[
-            pl.BlockSpec((4 * IN_ROWS, rows), lambda s: (back_order(s), 0)),
-            pl.BlockSpec((4 * 48, rows), lambda s: (back_order(s), 0)),
-            pl.BlockSpec((4 * 48, rows), lambda s: (back_order(s), 0)),
-            pl.BlockSpec((4, 1, rows), lambda s: (back_order(s), 0, 0)),
-            pl.BlockSpec((rows, width), lambda s: (0, 0), pipeline_mode=pl.Buffered(1)),
-            pl.BlockSpec((1, 4, 48, width), lambda s: (back_order(s), 0, 0, 0)),
-            pl.BlockSpec((192, width), lambda s: (0, 0), pipeline_mode=pl.Buffered(1)),
-            anywhere,
-        ],
-        out_specs=[
-            pl.BlockSpec((4 * IN_ROWS, rows), lambda s: (back_order(s), 0)),
-            pl.BlockSpec((1, 8, 4 * IN_ROWS), lambda s: (back_order(s), 0, 0)),
-            pl.BlockSpec((96, width), lambda s: (0, 0)),
-            pl.BlockSpec((96, width), lambda s: (0, 0)),
-            anywhere,
-            anywhere,
-        ],
-        out_shape=[
-            jax.ShapeDtypeStruct((16 * IN_ROWS, rows), BF16),
-            jax.ShapeDtypeStruct((4, 8, 4 * IN_ROWS), F32),
-            jax.ShapeDtypeStruct((96, width), F32),
-            jax.ShapeDtypeStruct((96, width), BF16),
-            jax.ShapeDtypeStruct((8, 192, width), BF16),
-            jax.ShapeDtypeStruct((2, 2, 2, 96, width), BF16),
-        ],
-        scratch_shapes=[
-            pltpu.VMEM((96, LONG_LEN), F32),
-            pltpu.VMEM((2, 2, 2, 192, width), BF16),
-            pltpu.VMEM((4, 2, 2, 2, 96, width), BF16),
-            pltpu.SemaphoreType.DMA((4,)),
-        ]
-        + reduce_scratch(2, 192, 96, width)
-        + reduce_scratch(3, 96, 48, width)
-        + share_scratch(192, width),
-        compiler_params=pltpu.CompilerParams(
-            vmem_limit_bytes=62 << 20, collective_id=1, has_side_effects=True
-        ),
-        cost_estimate=pl.CostEstimate(
-            flops=45_000_000_000, bytes_accessed=40_000_000, transcendentals=19_000_000
-        ),
-        name="attend_back",
-    )(qkv, back_mixed, mixed, logsum, first, out_grad, ff_part, ff_grad)
-
-
-BLOCK = 256
-
-
-def tail_kernel(
-    back_qkv_ref,
     in_ref,
     tokens_ref,
     resid_ref,
     vector_ref,
     feed_small_ref,
     up_sums_ref,
-    bias_sums_ref,
-    part_ref,
-    piece_ref,
-    ff_ref,
-    in_grad,
+    ff_grad,
     input_ref,
     small_ref,
-    up_ref,
-    down_ref,
-    in_ref_out,
-    out_ref_out,
-    total,
-    piece_got,
+    up_out,
+    down_out,
+    in_out,
+    out_out,
+    held,
+    ff_total,
+    grads,
+    back_qkv,
+    turned,
     sums,
     sum_got,
     wide_got,
@@ -879,7 +711,6 @@
     sum_recv,
     along_send,
     along_recv,
-    piece_sem,
     local,
     *scratch,
     blocks,
@@ -888,127 +719,112 @@
     width = tokens_ref.shape[1]
     dp, base, y, x, core, mp = place()
     ways = lax.axis_size("mp")
-    final, wide, share_send, share_recv, wide_send, wide_recv = scratch[REDUCE_REFS:]
-    reduce = reduces_of(
-        (0,),
-        lambda i: in_grad.at[:, :, flip(core)],
-        lambda i: total,
-        scratch[:REDUCE_REFS],
+    ff_scratch, scratch = scratch[:REDUCE_REFS], scratch[REDUCE_REFS:]
+    in_scratch, scratch = scratch[:REDUCE_REFS], scratch[REDUCE_REFS:]
+    ff_final, ff_wide, *ff_sems = scratch[:SHARE_REFS]
+    in_final, in_wide, *in_sems = scratch[SHARE_REFS:]
+    ff = reduces_of(
+        (2, 3),
+        lambda i: ff_grad.at[i, :, :, flip(core)],
+        lambda i: ff_total.at[i],
+        ff_scratch,
+        96,
+    )
+    ins = reduces_of(
+        (0, 1, 2, 3),
+        lambda i: grads.at[i, :, :, flip(core)],
+        lambda i: grads.at[i, :, :, core],
+        in_scratch,
         48,
-    )[0]
-    share = Share(final, 48, share_send, share_recv)
-    own = pltpu.make_async_copy(in_grad.at[:, :, core], total, local.at[0])
-
-    piece = pltpu.make_async_remote_copy(
-        src_ref=piece_ref,
-        dst_ref=piece_got,
-        send_sem=piece_sem.at[0],
-        recv_sem=piece_sem.at[1],
-        device_id=(dp, lax.rem(mp + 3, ways)),
-        device_id_type=MESH,
-    )
+    )
+    ff_share = Share(ff_final, 96, *ff_sems[:2])
+    in_share = Share(in_final, 48, *in_sems[:2])
+    me = 4 * y + 2 * x + core
+
+    def own(i):
+        return pltpu.make_async_copy(ff_grad.at[i, :, :, core], ff_total.at[i], local.at[i])
+
+    up_written = pltpu.make_async_copy(ff_final.at[:, pl.ds(0, 96)], up_out, local.at[2])
+    down_written = pltpu.make_async_copy(turned, down_out, local.at[3])
+
+    def in_written():
+        copies = []
+        for head in range(4):
+            rows = pl.ds(48 * head, 48)
+            for part in range(4):
+                src = in_final.at[2 * head + part // 2, pl.ds(48 * (part % 2), 48)]
+                dst = in_out.at[part, rows] if part < 3 else out_out.at[rows]
+                copies.append(pltpu.make_async_copy(src, dst, local.at[4 + 4 * head + part]))
+        return copies
 
     def begin():
-        own.start()
+        own(0).start()
+        own(1).start()
         greet(every_partner())
-        reduce.cores()
-        piece.start()
+        ff[2].cores()
+        ff[3].cores()
         sums[0] = jnp.zeros_like(sums[0])
         sums[0, 0:8, :] = feed_small_ref[...]
         sums[0, 4:6, :] = up_sums_ref[0:2, :]
-        for slot in range(4):
-            sums[0, 8 + slot : 9 + slot, 0 : 4 * IN_ROWS] = bias_sums_ref[slot, 0:1]
-        own.wait()
-        reduce.chips()
+
+    def chips(slot):
+        own(slot - 2).wait()
+        ff[slot].chips()
+
+    def finish_ff():
+        total = ff_part_ref[...] + ff[2].result() + ff[3].result()
+        ff_final[me] = Wide(ff_wide, *ff_sems[2:]).sum(total).astype(BF16)
+        ff_share.spread()
+
+    def write_ff():
+        ff_share.finish()
+        up_written.start()
+        turned[...] = ff_final[:, 96:].reshape(width, width).T
+        down_written.start()
 
     def finish_in():
-        piece.wait_recv()
-        whole = part_ref[...] + reduce.result() + piece_got[...].astype(F32)
-        whole = Wide(wide, wide_send, wide_recv).sum(whole)
-        final[4 * y + 2 * x + core] = whole.astype(BF16)
-        share.spread()
-
-    def along():
-        reduce.along()
-        finish_in()
-
-    def write_up():
-        up_ref[...] = ff_ref[:, :96].reshape(width, width).astype(F32)
-
-    def write_down():
-        down_ref[...] = ff_ref[:, 96:].reshape(width, width).astype(F32).T
-
-    hook = hooks_of(
-        {
-            (0, "begin"): [begin],
-            (1, "end"): [reduce.chips_again],
-            (2, "begin"): [write_up],
-            (2, "end"): [along],
-            (3, "begin"): [write_down],
-            (4, "end"): [share.forward],
-        },
-        step,
-    )
-    hook("begin")
-    inputs = tokens_ref[...].astype(F32)
-    average = jnp.mean(inputs, axis=-1, keepdims=True)
-    centred = inputs - average
-    inverse = lax.rsqrt(jnp.mean(centred * centred, axis=-1, keepdims=True) + epsilon)
-    scaled = centred * inverse
-    back_first = None
-    for slot in range(4):
-        weight = in_ref[slot, :, :IN_ROWS].reshape(4 * IN_ROWS, width)
-        part = tn(back_qkv_ref[slot * 4 * IN_ROWS : (slot + 1) * 4 * IN_ROWS, :], weight)
-        back_first = part if slot == 0 else back_first + part
-    sums[0, 12:13, :] += jnp.sum(back_first * scaled, axis=0, keepdims=True)
-    sums[0, 13:14, :] += jnp.sum(back_first, axis=0, keepdims=True)
-    back_norm = back_first * vector_ref[4:5, :]
-    input_ref[...] = resid_ref[...] + inverse * (
-        back_norm
-        - jnp.mean(back_norm, axis=-1, keepdims=True)
-        - scaled * jnp.mean(back_norm * scaled, axis=-1, keepdims=True)
-    )
-
-    hook("end")
-
-    @pl.when(step == blocks - 1)
-    def _():
-        wide = wider_bits()
-        near = range(1, GROUP)
-
-        def near_copy(k):
-            return pltpu.make_async_remote_copy(
-                src_ref=sums.at[0],
-                dst_ref=sum_got.at[k - 1],
-                send_sem=sum_send.at[k - 1],
-                recv_sem=sum_recv.at[k - 1],
-                device_id=(base + near_index(y, x, core, k), mp),
-                device_id_type=MESH,
-            )
-
-        def wide_copy(i):
-            return pltpu.make_async_remote_copy(
-                src_ref=sums.at[i + 1],
-                dst_ref=wide_got.at[i],
-                send_sem=sum_send.at[GROUP - 1 + i],
-                recv_sem=sum_recv.at[GROUP - 1 + i],
-                device_id=(other_bit(dp, wide[i]), mp),
-                device_id_type=MESH,
-            )
-
-        def along_copy(slot):
-            return pltpu.make_async_remote_copy(
-                src_ref=sums.at[len(wide) + 1],
-                dst_ref=along_got.at[slot - 1],
-                send_sem=along_send.at[slot - 1],
-                recv_sem=along_recv.at[slot - 1],
-                device_id=(dp, lax.rem(mp + slot, ways)),
-                device_id_type=MESH,
-            )
-
+        ins[0].along()
+        total = ins[0].result() + ins[1].result() + ins[2].result() + ins[3].result()
+        in_final[me] = Wide(in_wide, *in_sems[2:]).sum(total).astype(BF16)
+        in_share.spread()
+
+    wide = wider_bits()
+    near = range(1, GROUP)
+
+    def near_copy(k):
+        return pltpu.make_async_remote_copy(
+            src_ref=sums.at[0],
+            dst_ref=sum_got.at[k - 1],
+            send_sem=sum_send.at[k - 1],
+            recv_sem=sum_recv.at[k - 1],
+            device_id=(base + near_index(y, x, core, k), mp),
+            device_id_type=MESH,
+        )
+
+    def wide_copy(i):
+        return pltpu.make_async_remote_copy(
+            src_ref=sums.at[i + 1],
+            dst_ref=wide_got.at[i],
+            send_sem=sum_send.at[GROUP - 1 + i],
+            recv_sem=sum_recv.at[GROUP - 1 + i],
+            device_id=(other_bit(dp, wide[i]), mp),
+            device_id_type=MESH,
+        )
+
+    def along_copy(slot):
+        return pltpu.make_async_remote_copy(
+            src_ref=sums.at[len(wide) + 1],
+            dst_ref=along_got.at[slot - 1],
+            send_sem=along_send.at[slot - 1],
+            recv_sem=along_recv.at[slot - 1],
+            device_id=(dp, lax.rem(mp + slot, ways)),
+            device_id_type=MESH,
+        )
+
+    def end():
         for k in near:
             near_copy(k).start()
-        share.last()
+        in_share.forward()
         result = sums[0]
         for k in near:
             near_copy(k).wait_recv()
@@ -1020,12 +836,10 @@
             sums[i + 2] = sums[i + 1] + wide_got[i]
         for slot in (1, 2, 3):
             along_copy(slot).start()
-        share.finish()
-        for head in range(4):
-            low, high = final[2 * head].astype(F32), final[2 * head + 1].astype(F32)
-            rows = slice(48 * head, 48 * head + 48)
-            in_ref_out[0, rows], in_ref_out[1, rows] = low[:48], low[48:]
-            in_ref_out[2, rows], out_ref_out[rows] = high[:48], high[48:]
+        in_share.last()
+        in_share.finish()
+        for copy in in_written():
+            copy.start()
         small_ref[...] = sums[len(wide) + 1]
         for slot in (1, 2, 3):
             along_copy(slot).wait_recv()
@@ -1040,8 +854,88 @@
             wide_copy(i).wait_send()
         for slot in (1, 2, 3):
             along_copy(slot).wait_send()
-        reduce.finish()
-        piece.wait_send()
+        for reduce in [*ff.values(), *ins.values()]:
+            reduce.finish()
+        up_written.wait()
+        down_written.wait()
+        for copy in in_written():
+            copy.wait()
+
+    hook = hooks_of(
+        {
+            (0, 0): [begin],
+            (0, 1): [lambda: chips(2)],
+            (0, 3): [ff[2].chips_again, lambda: chips(3)],
+            (1, 0): [ins[2].cores],
+            (1, 2): [ff[2].along],
+            (1, 3): [ff[3].chips_again, ins[2].chips],
+            (2, 0): [ff[3].along, ins[1].cores],
+            (2, 1): [ins[2].chips_again, ins[1].chips],
+            (2, 3): [ins[2].along, ins[1].chips_again],
+            (3, 0): [finish_ff, ins[1].along, ins[3].cores],
+            (3, 1): [ins[3].chips],
+            (3, 3): [ff_share.forward, ins[3].chips_again],
+            (4, "begin"): [ins[0].cores, ins[3].along],
+            (5, "begin"): [ins[0].chips, ff_share.last],
+            (6, "begin"): [write_ff],
+            (6, "end"): [ins[0].chips_again],
+            (7, "end"): [finish_in],
+            (9, "end"): [end],
+        },
+        step,
+    )
+
+    @pl.when(step < 4)
+    def _():
+        slot = back_order(step)
+
+        def one_head(head, carry):
+            hook(None, head)
+            of_head = pl.ds(pl.multiple_of(head * IN_ROWS, 16), IN_ROWS)
+            own_head = pl.ds(pl.multiple_of(head * 48, 16), 48)
+            out_rows = pl.ds(pl.multiple_of((4 * slot + head) * IN_ROWS, 16), IN_ROWS)
+            attend_back_head(
+                qkv_ref.at[of_head],
+                back_ref.at[own_head],
+                mixed_ref.at[own_head],
+                logsum_ref.at[head],
+                back_qkv.at[out_rows],
+                held,
+            )
+            return carry
+
+        lax.fori_loop(0, 4, one_head, 0)
+
+        for head in range(4):
+            rows = back_qkv[pl.ds(pl.multiple_of((4 * slot + head) * IN_ROWS, 16), IN_ROWS), :]
+            grad = nn(rows, first_ref[...]).astype(BF16)
+            grads[slot, head // 2, head % 2, 0] = grad[:96]
+            grads[slot, head // 2, head % 2, 1, 0:48] = grad[96:]
+            grads[slot, head // 2, head % 2, 1, 48:96] = out_grad_ref[0, head]
+        rows = back_qkv[pl.ds(pl.multiple_of(4 * slot * IN_ROWS, 16), 4 * IN_ROWS), :]
+        row_sums = nt(jnp.ones((8, rows.shape[1]), BF16), rows)
+        sums[0, pl.ds(8 + slot, 1), 0 : 4 * IN_ROWS] = row_sums[0:1]
+
+    @pl.when(step >= 4)
+    def _():
+        hook("begin")
+        inputs = tokens_ref[...].astype(F32)
+        scaled, inverse = normed(inputs)
+        cols = pl.ds(pl.multiple_of((step - 4) * BLOCK, BLOCK), BLOCK)
+        back_first = None
+        for slot in range(4):
+            weight = in_ref[slot, :, :IN_ROWS].reshape(4 * IN_ROWS, width)
+            part = tn(back_qkv[slot * 4 * IN_ROWS : (slot + 1) * 4 * IN_ROWS, cols], weight)
+            back_first = part if slot == 0 else back_first + part
+        sums[0, 12:13, :] += jnp.sum(back_first * scaled, axis=0, keepdims=True)
+        sums[0, 13:14, :] += jnp.sum(back_first, axis=0, keepdims=True)
+        back_norm = back_first * vector_ref[4:5, :]
+        input_ref[...] = resid_ref[...] + inverse * (
+            back_norm
+            - jnp.mean(back_norm, axis=-1, keepdims=True)
+            - scaled * jnp.mean(back_norm * scaled, axis=-1, keepdims=True)
+        )
+        hook("end")
 
 
 def near_index(y, x, core, k):
@@ -1061,51 +955,79 @@
     )
 
 
-def tail(
-    back_qkv, in_all, tokens, resid, vectors, small_sums, bias_sums, in_part, piece, ff_sum, in_grad
+def back_order(turn):
+    turn = jnp.minimum(turn, 3)
+    return 2 - turn + (turn // 2) * (3 - 2 * (turn // 3))
+
+
+BLOCK = 256
+
+
+def attend_back(
+    qkv,
+    back_mixed,
+    mixed,
+    logsum,
+    first,
+    out_grad,
+    ff_part,
+    in_all,
+    tokens,
+    resid,
+    vectors,
+    feed_small,
+    up_sums,
+    ff_grad,
 ):
-    rows, width = tokens.shape
+    rows, width = first.shape
     blocks = rows // BLOCK
     bits = len(wider_bits())
     anywhere = pl.BlockSpec(memory_space=pl.ANY)
     one = pl.Buffered(1)
     dma = pltpu.SemaphoreType.DMA
+    row = pl.BlockSpec((BLOCK, width), lambda s: (jnp.maximum(s - 4, 0), 0))
+    small = pl.BlockSpec((8, width), lambda s: (0, 0))
     return pl.pallas_call(
-        functools.partial(tail_kernel, blocks=blocks),
-        grid=(blocks,),
+        functools.partial(attend_back_kernel, blocks=blocks),
+        grid=(4 + blocks,),
         in_specs=[
-            pl.BlockSpec((16 * IN_ROWS, BLOCK), lambda s: (0, s)),
+            pl.BlockSpec((4 * IN_ROWS, rows), lambda s: (back_order(s), 0)),
+            pl.BlockSpec((4 * 48, rows), lambda s: (back_order(s), 0)),
+            pl.BlockSpec((4 * 48, rows), lambda s: (back_order(s), 0)),
+            pl.BlockSpec((4, 1, rows), lambda s: (back_order(s), 0, 0)),
+            pl.BlockSpec((rows, width), lambda s: (0, 0), pipeline_mode=one),
+            pl.BlockSpec((1, 4, 48, width), lambda s: (back_order(s), 0, 0, 0)),
+            pl.BlockSpec((192, width), lambda s: (0, 0), pipeline_mode=one),
             pl.BlockSpec((4, 4, HEAD_ROWS, width), lambda s: (0, 0, 0, 0), pipeline_mode=one),
-            pl.BlockSpec((BLOCK, width), lambda s: (s, 0)),
-            pl.BlockSpec((BLOCK, width), lambda s: (s, 0)),
-            pl.BlockSpec((8, width), lambda s: (0, 0)),
-            pl.BlockSpec((8, width), lambda s: (0, 0)),
-            pl.BlockSpec((8, width), lambda s: (0, 0)),
-            pl.BlockSpec((4, 8, 4 * IN_ROWS), lambda s: (0, 0, 0)),
-            pl.BlockSpec((96, width), lambda s: (0, 0)),
-            pl.BlockSpec((96, width), lambda s: (0, 0)),
-            pl.BlockSpec((8, 192, width), lambda s: (0, 0, 0), pipeline_mode=one),
+            row,
+            row,
+            small,
+            small,
+            small,
             anywhere,
         ],
         out_specs=[
-            pl.BlockSpec((BLOCK, width), lambda s: (s, 0)),
+            row,
             pl.BlockSpec((16, width), lambda s: (0, 0)),
-            pl.BlockSpec((width, width), lambda s: (0, 0)),
-            pl.BlockSpec((width, width), lambda s: (0, 0)),
-            pl.BlockSpec((3, 192, width), lambda s: (0, 0, 0)),
-            pl.BlockSpec((192, width), lambda s: (0, 0)),
+            anywhere,
+            anywhere,
+            anywhere,
+            anywhere,
         ],
         out_shape=[
             jax.ShapeDtypeStruct((rows, width), F32),
             jax.ShapeDtypeStruct((16, width), F32),
-            jax.ShapeDtypeStruct((width, width), F32),
-            jax.ShapeDtypeStruct((width, width), F32),
-            jax.ShapeDtypeStruct((3, 192, width), F32),
-            jax.ShapeDtypeStruct((192, width), F32),
+            jax.ShapeDtypeStruct((8, 96, width), BF16),
+            jax.ShapeDtypeStruct((width, width), BF16),
+            jax.ShapeDtypeStruct((3, 192, width), BF16),
+            jax.ShapeDtypeStruct((192, width), BF16),
         ],
         scratch_shapes=[
-            pltpu.VMEM((2, 2, 96, width), BF16),
-            pltpu.VMEM((96, width), BF16),
+            pltpu.VMEM((96, LONG_LEN), F32),
+            pltpu.VMEM((2, 2, 2, 192, width), BF16),
+            pltpu.VMEM((4, 2, 2, 2, 96, width), BF16),
+            pltpu.VMEM((16 * IN_ROWS, rows), BF16),
+            pltpu.VMEM((width, width), BF16),
             pltpu.VMEM((bits + 2, 16, width), F32),
             pltpu.VMEM((GROUP - 1, 16, width), F32),
             pltpu.VMEM((max(bits, 1), 16, width), F32),
@@ -1114,30 +1036,34 @@
             dma((GROUP - 1 + bits,)),
             dma((3,)),
             dma((3,)),
-            dma((2,)),
-            dma((1,)),
+            dma((20,)),
         ]
-        + reduce_scratch(1, 96, 48, width)
+        + reduce_scratch(2, 192, 96, width)
+        + reduce_scratch(4, 96, 48, width)
+        + share_scratch(192, width)
         + share_scratch(96, width),
         compiler_params=pltpu.CompilerParams(
-            vmem_limit_bytes=62 << 20, collective_id=2, has_side_effects=True
+            vmem_limit_bytes=62 << 20, collective_id=1, has_side_effects=True
         ),
         cost_estimate=pl.CostEstimate(
-            flops=6_000_000_000, bytes_accessed=30_000_000, transcendentals=2000
+            flops=50_000_000_000, bytes_accessed=50_000_000, transcendentals=19_000_000
         ),
-        name="tail",
+        name="attend_back",
     )(
-        back_qkv,
+        qkv,
+        back_mixed,
+        mixed,
+        logsum,
+        first,
+        out_grad,
+        ff_part,
         in_all,
         tokens,
         resid,
         vectors,
-        *small_sums,
-        bias_sums,
-        in_part,
-        piece,
-        ff_sum,
-        in_grad,
+        feed_small,
+        up_sums,
+        ff_grad,
     )
 
 
@@ -1613,7 +1539,7 @@
         vectors,
         near_grad,
     )
-    back_qkv, bias_sums, in_part, piece, ff_sum, in_grad = attend_back(
+    input_grad, small, grad_up, grad_down, grad_in, grad_out = attend_back(
         qkv,
         back_mixed,
         mixed,
@@ -1621,22 +1547,17 @@
         first,
         out_grads,
         ff_part,
-        late_grad.reshape(2, 2, 2, 2, 192, width),
-    )
-    input_grad, small, grad_up, grad_down, grad_in, grad_out = tail(
-        back_qkv,
         in_all,
         tokens,
         resid,
         vectors,
-        (feed_small, up_sums),
-        bias_sums,
-        in_part,
-        piece,
-        ff_sum,
-        in_grad,
-    )
-    grad_in = grad_in.transpose(2, 0, 1)
+        feed_small,
+        up_sums,
+        late_grad.reshape(2, 2, 2, 2, 192, width),
+    )
+    grad_up = grad_up.reshape(width, width).astype(F32)
+    grad_down, grad_out = grad_down.astype(F32), grad_out.astype(F32)
+    grad_in = grad_in.astype(F32).transpose(2, 0, 1)
     pair_sum = small[8, : 4 * IN_ROWS].reshape(own_heads, 3, HEAD_DIM)
     grad_pair = jnp.stack([pair_sum[:, 0].reshape(-1), pair_sum[:, 2].reshape(-1)])
     return (

time: 302 us -> 272 us (0.901); the launches traced: 298 us -> 272 us
  Pallas kernels: 275 us -> 248 us
  other arithmetic: 6.63 us -> 14.3 us
  local copies, waits for them, and re-layouts: 16.3 us -> 8.66 us
    pallas_call x2 -> x1, Pallas kernels: 126 us -> 98.4 us  [attend_back(): pl.pallas_call(functools.partial(attend_back_kernel, blocks=blocks), grid...]
    unnamed x16 -> x12, local copies, waits for them, and re-layouts: 12.7 us -> 5 us
    convert_element_type x0 -> x3, other arithmetic: none -> 5.04 us  [the longest x2 3.39 us: local(): grad_down, grad_out = (grad_down.astype(F32), grad_out.astype(F32))]
where the time goes in v5:
time: 272 us
  Pallas kernels  248 us (91%)
  other arithmetic  14.3 us (5%)
  local copies, waits for them, and re-layouts  8.66 us (3%)
    pallas_call x1, Pallas kernels, attend_back(): pl.pallas_call(functools.partial(attend_back_kernel, blocks=blocks), grid...  98.4 us
    pallas_call x1, Pallas kernels, attend(): pl.pallas_call(attend_kernel, grid=(4,), in_specs=[pl.BlockSpec((rows, wi...  59.5 us
    pallas_call x1, Pallas kernels, feed_last(): pl.pallas_call(feed_last_kernel, grid=(FEED_BLOCKS + 2,), in_specs=[pl.Bl...  45.8 us
    pallas_call x1, Pallas kernels, feed_first(): pl.pallas_call(feed_first_kernel, grid=(FEED_BLOCKS + 2,), in_specs=[pl.B...  44.3 us

profile of v5, /device:TPU:0, one launch (start us, length us, event | category | flops | bytes accessed | tf_op | source)
XLA Modules:
  0.0 271.6 jit_solution(7495890315537535038)
XLA Ops:
  0.7 0.1 pad.19.clone
  0.7 0.7 convert_element_type.21
  1.5 0.1 squeeze.27
  1.5 0.1 squeeze.28
  1.6 0.1 pad_maximum_fusion.1
  1.7 0.7 broadcast_in_dim.57
  2.4 1.5 select_select_fusion.vector_ref.vec_ref
  3.8 0.6 select_maximum_fusion.bias_own
  4.5 3.2 %pad_maximum_fusion.ff_own.own_ref = bf16[8,192,768]{2,1,0:T(8,128)(2,1)} fusion(bf16[8,96,768]{2,1,0:T(8,128)(2,1)} %bitcast.12, bf16[8,96,768]{2,1,0:T(8,128)(2,1)} %bitcast.13), kind=kLoop, calls=%fused_computation | loop fusion | flops 4718592 | bytes 4718592 | tf_op jit(solution)/shard_map/concatenate | solution.py:1505
  7.7 59.5 %attend.1 = (bf16[2304,1536]{1,0:T(8,128)(2,1)}, bf16[768,1536]{1,0:T(8,128)(2,1)}, f32[16,1,1536]{2,1,0:T(1,128)}, bf16[1536,768]{1,0:T(8,128)(2,1)}, bf16[4,4,...) custom-call(bf16[1536,768]{1,0:T(8,128)(2,1)} %tokens_ref.5, ...), custom_call_target="tpu_custom_call" | custom-call | flops 30000001024 | bytes 30000000 | tf_op jit(solution)/shard_map/attend/pallas_call | solution.py:383
  67.1 44.3 %feed_first.1 = (f32[1536,768]{1,0:T(8,128)}, f32[1536,768]{1,0:T(8,128)}, f32[1536,768]{1,0:T(8,128)}, bf16[2,8,192,768]{3,2,1,0:T(8,128)(2,1)}, f32[8,768]{1,0:T(8,128)}, /*index=5*/bf16[2,8,192,768]{3,2,1,0:T(8,128)(2,1)}) custom-call(s32[1,2]{1,0:T(1,128)} %live_ref.3, bf16[1536,768]{1,0:T(8,128)(2,1)} %tokens_ref.5, bf16[1536,768]{1,0:T(8,128)(2,1)} %grad_ref.3, ...), custom_call_target="tpu_custom_call" | custom-call | flops 24000000000 | bytes 45000000 | tf_op jit(solution)/shard_map/feed_first/pallas_call | solution.py:1347
  111.4 45.8 %feed_last.1 = (bf16[1536,768]{1,0:T(8,128)(2,1)}, f32[1536,768]{1,0:T(8,128)}, bf16[768,1536]{1,0:T(8,128)(2,1)}, bf16[2,8,192,768]{3,2,1,0:T(8,128)(2,1)}, bf1...) custom-call(s32[1,2]{1,0:T(1,128)} %live_ref.3, f32[1536,768]{1,0:T(8,128)} %get-tuple-element.44.residual_ref, ...), custom_call_target="tpu_custom_call" | custom-call | flops 28000000000 | bytes 55000000 | tf_op jit(solution)/shard_map/feed_last/pallas_call | solution.py:1418
  157.3 98.4 %attend_back.1 = (f32[1536,768]{1,0:T(8,128)}, f32[16,768]{1,0:T(8,128)}, bf16[8,96,768]{2,1,0:T(8,128)(2,1)}, bf16[768,768]{1,0:T(8,128)(2,1)}, bf16[3,192,768]{2,1,0:T(8,128)(2,1)}, /*index=5*/bf16[192,768]{1,0:T(8,128)(2,1)}) custom-call(bf16[2304,1536]{1,0:T(8,128)(2,1)} %get-tuple-element.50.qkv_ref, bf16[768,1536]{1,0:T(8,128)(2,1)} %get-tuple-element.51.back_ref, ...), custom_call_target="tpu_custom_call" | custom-call | flops 49999998976 | bytes 50000000 | tf_op jit(solution)/shard_map/attend_back/pallas_call | solution.py:990
  255.6 0.0 copy-start.2
  255.6 0.8 slice_reduce_fusion.7
  256.5 1.6 slice_reduce_fusion
  258.1 0.1 reshape_squeeze.3
  258.2 0.1 stack_reshape_squeeze.6
  258.3 0.1 stack_reshape_squeeze.7
  258.4 0.6 pad_maximum_fusion.2
  259.0 1.8 convert_element_type.22
  260.8 0.0 copy-start.1
  260.8 2.6 convert_bitcast_fusion
  263.4 0.0 copy-done.2
  263.4 0.0 slice-start
  263.4 1.7 bitcast_convert_fusion
  265.0 0.0 copy-done.1
  265.0 0.0 copy-start
  265.0 0.0 slice-start.1
  265.1 1.6 convert_element_type.25
  266.6 1.4 copy-done
  268.0 1.4 copy.31
  269.4 0.0 slice-done
  269.4 0.0 slice-done.1
  269.4 2.2 copy.32
  (8 shorter events, 0.1 us)
Async XLA Ops:
  255.6 7.8 %copy-start.2 = (bf16[8,96,768]{2,1,0:T(8,128)(2,1)S(1)}, bf16[8,96,768]{2,1,0:T(8,128)(2,1)}, u32[]{:S(2)}) copy-start(bf16[8,96,768]{2,1,0:T(8,128)(2,1)} %get-tuple-element.64) | copy-start | bytes 3538948
  260.8 4.3 %copy-start.1 = (bf16[768,768]{1,0:T(8,128)(2,1)S(1)}, bf16[768,768]{1,0:T(8,128)(2,1)}, u32[]{:S(2)}) copy-start(bf16[768,768]{1,0:T(8,128)(2,1)} %get-tuple-element.65) | copy-start | bytes 3538948
  263.4 6.0 %slice-start = ((s8[4718592]{0:T(1024)(128)(4,1)}), s8[4194304]{0:T(1024)(128)(4,1)S(1)}, s32[]{:S(2)}) async-start(s8[4718592]{0:T(1024)(128)(4,1)} %bitcast.10), calls=%async_computation | async-start | bytes 8388608
  265.0 3.0 %copy-start = (bf16[1536,768]{1,0:T(8,128)(2,1)S(1)}, bf16[1536,768]{1,0:T(8,128)(2,1)}, u32[]{:S(2)}) copy-start(bf16[1536,768]{1,0:T(8,128)(2,1)} %get-tuple-element.97) | copy-start | bytes 7077892
  265.0 4.4 %slice-start.1 = ((s8[4718592]{0:T(1024)(128)(4,1)}), s8[524288]{0:T(1024)(128)(4,1)S(1)}, s32[]{:S(2)}) async-start(s8[4718592]{0:T(1024)(128)(4,1)} %bitcast.10), calls=%async_computation.1 | async-start | bytes 1048576

commit v6 on v5

--- a/solution.py
+++ b/solution.py
@@ -69,8 +69,9 @@
 
 
 class Gather:
-    def __init__(self, own, buffers, piece, split, send, recv):
+    def __init__(self, own, buffers, piece, split, send, recv, pieces=None):
         self.own, self.buffers, self.piece, self.split = own, buffers, piece, split
+        self.pieces = pieces or {}
         self.send, self.recv = send, recv
         self.dp, self.base, self.y, self.x, self.core, self.mp = place()
 
@@ -92,13 +93,13 @@
             ways = lax.axis_size("mp")
             hop = 1 if slot == 2 else slot
             src = self.view(self.buffers[1] if slot == 2 else self.own, *mine)
-            dst = self.view(buffer, *mine)
+            dst = self.pieces[slot] if slot in self.pieces else self.view(buffer, *mine)
             device = (self.dp, lax.rem(self.mp + ways - hop, ways))
         else:
-            return self.shared(kind, buffer, kind * 4 + slot)
+            return self.shared(kind, buffer, kind * 4 + slot, self.pieces.get(slot))
         return self.remote(src, dst, device, kind * 4 + slot)
 
-    def shared(self, kind, buffer, index):
+    def shared(self, kind, buffer, index, piece=None):
         y, x, core = self.y, self.x, self.core
         mine, near_x, near_y = (y, x, core), (y, flip(x), core), (flip(y), x, core)
         moved, device = {
@@ -111,7 +112,8 @@
             7: lambda: (self.view(buffer, *near_y), (y, x, flip(core))),
             8: lambda: (self.view(buffer, flip(y), flip(x), core), (y, x, flip(core))),
         }[kind]()
-        return self.remote(moved, moved, self.device(*device), index)
+        src = moved if piece is None or kind not in (1, 2, 5) else piece
+        return self.remote(src, moved, self.device(*device), index)
 
     def remote(self, src, dst, device, index):
         return pltpu.make_async_remote_copy(
@@ -135,7 +137,8 @@
         self.start(slot, 0)
 
     def spread(self, slot):
-        self.arrived(slot, 0)
+        if slot not in self.pieces:
+            self.arrived(slot, 0)
         self.start(slot, 1, 2, 5)
 
     def forward(self, slot):
@@ -151,9 +154,9 @@
     def complete(self, slot):
         self.arrived(slot, 5, 6, 7, 8)
 
-    def finish(self, *slots):
+    def finish(self, slots, kinds=range(9)):
         for slot in slots:
-            for kind in range(GATHER_KINDS):
+            for kind in kinds:
                 self.copy(kind, slot).wait_send()
 
 
@@ -259,6 +262,7 @@
     first_ref,
     in_out,
     ff_near,
+    ff_pieces,
     bias_out,
     in_all,
     bias_all,
@@ -275,7 +279,15 @@
     dp, base, y, x, core, mp = place()
     ways = lax.axis_size("mp")
     gin = Gather(in_all.at[0], [in_all.at[k] for k in range(4)], in_piece, 96, in_send, in_recv)
-    gff = Gather(ff_own, [None, ff_near], ff_piece, 96, ff_send, ff_recv)
+    gff = Gather(
+        ff_own,
+        [None, ff_near, None, None],
+        ff_piece,
+        96,
+        ff_send,
+        ff_recv,
+        {2: ff_pieces.at[0], 3: ff_pieces.at[1]},
+    )
     own_copies = [
         pltpu.make_async_copy(
             in_own.at[part, pl.ds(head * 48, 48)] if part < 3 else out_own.at[pl.ds(head * 48, 48)],
@@ -307,9 +319,6 @@
         for copy in own_copies:
             copy.wait()
         gin.along(1)
-        gin.along(3)
-        for slot in (1, 2, 3):
-            bias_copy(slot).start()
         for rows in range(0, tokens_ref.shape[0], BLOCK):
             block = slice(rows, rows + BLOCK)
             first_ref[block] = layer_norm(
@@ -319,31 +328,43 @@
 
     def end():
         gff.complete(1)
+        gff.arrived(2, 0)
+        gff.arrived(3, 0)
         out_in.wait()
         out_bias.wait()
         for slot in (1, 2, 3):
             bias_copy(slot).wait_send()
-        gin.finish(1, 2, 3)
-        gff.finish(1)
+        gin.finish((1, 2, 3))
+        gff.finish((1,))
+        gff.finish((2, 3), (0,))
 
     hook = hooks_of(
         {
             (0, "begin"): [begin],
-            (0, "heads"): [lambda: gin.spread(1), lambda: gin.along(2), lambda: gff.along(1)],
+            (0, "heads"): [
+                lambda: gin.spread(1),
+                lambda: gin.along(3),
+                lambda: gin.along(2),
+                lambda: [bias_copy(slot).start() for slot in (1, 2, 3)],
+            ],
             (0, 2): [lambda: gin.forward(1)],
-            (0, 3): [lambda: gin.spread(3)],
-            (0, "end"): [lambda: gin.last(1), lambda: gin.spread(2)],
+            (0, "end"): [lambda: gin.last(1), lambda: gin.spread(3)],
             (1, "begin"): [
                 lambda: [bias_copy(slot).wait_recv() for slot in (1, 2, 3)],
                 lambda: gin.complete(1),
             ],
-            (1, "heads"): [lambda: gin.forward(3)],
-            (1, 2): [lambda: gin.last(3), lambda: gin.forward(2), lambda: gff.spread(1)],
-            (1, "end"): [lambda: gin.last(2)],
-            (2, "begin"): [lambda: gin.complete(3)],
-            (2, 2): [lambda: gff.forward(1)],
-            (2, "end"): [lambda: gff.last(1)],
-            (3, "begin"): [lambda: gin.complete(2), out_in.start, out_bias.start],
+            (1, "heads"): [lambda: gin.spread(2), lambda: gff.along(1)],
+            (1, 1): [lambda: gin.forward(3)],
+            (1, 3): [lambda: gin.last(3), lambda: gin.forward(2)],
+            (2, "begin"): [lambda: gin.last(2), lambda: gin.complete(3)],
+            (2, "heads"): [lambda: gff.spread(1), lambda: gff.along(3), lambda: gff.along(2)],
+            (3, "begin"): [
+                lambda: gin.complete(2),
+                out_in.start,
+                out_bias.start,
+                lambda: gff.forward(1),
+            ],
+            (3, 2): [lambda: gff.last(1)],
             (3, "end"): [end],
         },
         step,
@@ -399,6 +420,7 @@
             anywhere,
             anywhere,
             anywhere,
+            anywhere,
         ],
         out_shape=[
             jax.ShapeDtypeStruct((heads * IN_ROWS, rows), BF16),
@@ -407,6 +429,7 @@
             jax.ShapeDtypeStruct((rows, width), BF16),
             jax.ShapeDtypeStruct((4, 4, HEAD_ROWS, width), BF16),
             jax.ShapeDtypeStruct((8, 192, width), BF16),
+            jax.ShapeDtypeStruct((2, 192, width), BF16),
             jax.ShapeDtypeStruct((4, 8, 1024), F32),
         ],
         scratch_shapes=[
@@ -630,6 +653,105 @@
 SHARE_REFS = 6
 
 
+class Sums:
+    def __init__(self, direct, held, got, along_got, send, recv, along_send, along_recv):
+        self.direct, self.held, self.got, self.along_got = direct, held, got, along_got
+        self.send, self.recv, self.along_send, self.along_recv = send, recv, along_send, along_recv
+        self.dp, self.base, self.y, self.x, self.core, self.mp = place()
+        self.bits = ([] if direct else [1, 2, 4]) + wider_bits()
+        self.near = GROUP - 1 if direct else 0
+
+    def copy(self, src, index, device):
+        return pltpu.make_async_remote_copy(
+            src_ref=self.held.at[src],
+            dst_ref=self.got.at[index],
+            send_sem=self.send.at[index],
+            recv_sem=self.recv.at[index],
+            device_id=(device, self.mp),
+            device_id_type=MESH,
+        )
+
+    def near_copy(self, k):
+        return self.copy(0, k, self.base + near_index(self.y, self.x, self.core, k + 1))
+
+    def bit_copy(self, i):
+        first = 1 if self.direct else 0
+        return self.copy(first + i, self.near + i, other_bit(self.dp, self.bits[i]))
+
+    def along_copy(self, slot):
+        return pltpu.make_async_remote_copy(
+            src_ref=self.held.at[self.last()],
+            dst_ref=self.along_got.at[slot - 1],
+            send_sem=self.along_send.at[slot - 1],
+            recv_sem=self.along_recv.at[slot - 1],
+            device_id=(self.dp, lax.rem(self.mp + slot, lax.axis_size("mp"))),
+            device_id_type=MESH,
+        )
+
+    def last(self):
+        return len(self.bits) + (1 if self.direct else 0)
+
+    def start(self):
+        if self.direct:
+            for k in range(self.near):
+                self.near_copy(k).start()
+        else:
+            self.bit_copy(0).start()
+
+    def step(self, i):
+        first = 1 if self.direct else 0
+        self.bit_copy(i).wait_recv()
+        self.held[first + i + 1] = self.held[first + i] + self.got[self.near + i]
+        if i + 1 < len(self.bits):
+            self.bit_copy(i + 1).start()
+
+    def join(self, begin=0):
+        if self.direct:
+            total = self.held[0]
+            for k in range(self.near):
+                self.near_copy(k).wait_recv()
+                total = total + self.got[k]
+            self.held[1] = total
+            if self.bits:
+                self.bit_copy(0).start()
+        for i in range(begin, len(self.bits)):
+            self.step(i)
+        for slot in (1, 2, 3):
+            self.along_copy(slot).start()
+
+    def result(self):
+        return self.held[self.last()]
+
+    def arrived(self, slot):
+        self.along_copy(slot).wait_recv()
+        return self.along_got[slot - 1]
+
+    def finish(self):
+        for k in range(self.near):
+            self.near_copy(k).wait_send()
+        for i in range(len(self.bits)):
+            self.bit_copy(i).wait_send()
+        for slot in (1, 2, 3):
+            self.along_copy(slot).wait_send()
+
+
+SUMS_REFS = 7
+
+
+def sums_scratch(direct, rows, width):
+    dma = pltpu.SemaphoreType.DMA
+    stages = (GROUP - 1 if direct else 3) + len(wider_bits())
+    return [
+        pltpu.VMEM(((1 if direct else 3) + len(wider_bits()) + 1, rows, width), F32),
+        pltpu.VMEM((stages, rows, width), F32),
+        pltpu.VMEM((3, rows, width), F32),
+        dma((stages,)),
+        dma((stages,)),
+        dma((3,)),
+        dma((3,)),
+    ]
+
+
 def attend_back_head(qkv_ref, back_ref, mixed_ref, logsum_ref, out_ref, held):
     rows = {}
 
@@ -682,10 +804,10 @@
     back_ref,
     mixed_ref,
     logsum_ref,
-    first_ref,
+    first_any,
     out_grad_ref,
     ff_part_ref,
-    in_ref,
+    in_any,
     tokens_ref,
     resid_ref,
     vector_ref,
@@ -703,14 +825,8 @@
     grads,
     back_qkv,
     turned,
-    sums,
-    sum_got,
-    wide_got,
-    along_got,
-    sum_send,
-    sum_recv,
-    along_send,
-    along_recv,
+    first_ref,
+    in_ref,
     local,
     *scratch,
     blocks,
@@ -718,7 +834,9 @@
     step = pl.program_id(0)
     width = tokens_ref.shape[1]
     dp, base, y, x, core, mp = place()
-    ways = lax.axis_size("mp")
+    early, scratch = Sums(False, *scratch[:SUMS_REFS]), scratch[SUMS_REFS:]
+    late, scratch = Sums(True, *scratch[:SUMS_REFS]), scratch[SUMS_REFS:]
+    sums, late_sums = early.held, late.held
     ff_scratch, scratch = scratch[:REDUCE_REFS], scratch[REDUCE_REFS:]
     in_scratch, scratch = scratch[:REDUCE_REFS], scratch[REDUCE_REFS:]
     ff_final, ff_wide, *ff_sems = scratch[:SHARE_REFS]
@@ -757,13 +875,19 @@
                 copies.append(pltpu.make_async_copy(src, dst, local.at[4 + 4 * head + part]))
         return copies
 
+    first_read = pltpu.make_async_copy(first_any, first_ref, local.at[20])
+    in_read = pltpu.make_async_copy(in_any, in_ref, local.at[21])
+
     def begin():
         own(0).start()
         own(1).start()
+        first_read.start()
+        in_read.start()
         greet(every_partner())
         ff[2].cores()
         ff[3].cores()
         sums[0] = jnp.zeros_like(sums[0])
+        late_sums[0] = jnp.zeros_like(late_sums[0])
         sums[0, 0:8, :] = feed_small_ref[...]
         sums[0, 4:6, :] = up_sums_ref[0:2, :]
 
@@ -788,72 +912,33 @@
         in_final[me] = Wide(in_wide, *in_sems[2:]).sum(total).astype(BF16)
         in_share.spread()
 
-    wide = wider_bits()
-    near = range(1, GROUP)
-
-    def near_copy(k):
-        return pltpu.make_async_remote_copy(
-            src_ref=sums.at[0],
-            dst_ref=sum_got.at[k - 1],
-            send_sem=sum_send.at[k - 1],
-            recv_sem=sum_recv.at[k - 1],
-            device_id=(base + near_index(y, x, core, k), mp),
-            device_id_type=MESH,
-        )
-
-    def wide_copy(i):
-        return pltpu.make_async_remote_copy(
-            src_ref=sums.at[i + 1],
-            dst_ref=wide_got.at[i],
-            send_sem=sum_send.at[GROUP - 1 + i],
-            recv_sem=sum_recv.at[GROUP - 1 + i],
-            device_id=(other_bit(dp, wide[i]), mp),
-            device_id_type=MESH,
-        )
-
-    def along_copy(slot):
-        return pltpu.make_async_remote_copy(
-            src_ref=sums.at[len(wide) + 1],
-            dst_ref=along_got.at[slot - 1],
-            send_sem=along_send.at[slot - 1],
-            recv_sem=along_recv.at[slot - 1],
-            device_id=(dp, lax.rem(mp + slot, ways)),
-            device_id_type=MESH,
-        )
+    def late_start():
+        late.start()
+        in_share.forward()
+
+    def end_early():
+        small_ref[0:12] = early.result()[0:12]
+        for slot in (1, 2, 3):
+            more = early.arrived(slot)
+            small_ref[0:4] += more[0:4]
+            small_ref[4:5] += more[4 + slot : 5 + slot]
+            small_ref[8:9] += more[8 + slot : 9 + slot]
 
     def end():
-        for k in near:
-            near_copy(k).start()
-        in_share.forward()
-        result = sums[0]
-        for k in near:
-            near_copy(k).wait_recv()
-            result = result + sum_got[k - 1]
-        sums[1] = result
-        for i in range(len(wide)):
-            wide_copy(i).start()
-            wide_copy(i).wait_recv()
-            sums[i + 2] = sums[i + 1] + wide_got[i]
-        for slot in (1, 2, 3):
-            along_copy(slot).start()
+        late_start()
+        late.join()
         in_share.last()
         in_share.finish()
         for copy in in_written():
             copy.start()
-        small_ref[...] = sums[len(wide) + 1]
-        for slot in (1, 2, 3):
-            along_copy(slot).wait_recv()
-            more = along_got[slot - 1]
-            small_ref[0:4, :] += more[0:4]
-            small_ref[12:14, :] += more[12:14]
-            small_ref[4:5, :] += more[4 + slot : 5 + slot]
-            small_ref[8:9, :] += more[8 + slot : 9 + slot]
-        for k in near:
-            near_copy(k).wait_send()
-        for i in range(len(wide)):
-            wide_copy(i).wait_send()
-        for slot in (1, 2, 3):
-            along_copy(slot).wait_send()
+        total = late.result() + late.arrived(1) + late.arrived(2) + late.arrived(3)
+        third = width // 3
+        for i in range(3):
+            part = slice(third * i, third * (i + 1))
+            small_ref[12:13, part] = total[i : i + 1]
+            small_ref[13:14, part] = total[3 + i : 4 + i]
+        early.finish()
+        late.finish()
         for reduce in [*ff.values(), *ins.values()]:
             reduce.finish()
         up_written.wait()
@@ -864,6 +949,7 @@
     hook = hooks_of(
         {
             (0, 0): [begin],
+            (0, "grads"): [first_read.wait],
             (0, 1): [lambda: chips(2)],
             (0, 3): [ff[2].chips_again, lambda: chips(3)],
             (1, 0): [ins[2].cores],
@@ -875,11 +961,13 @@
             (3, 0): [finish_ff, ins[1].along, ins[3].cores],
             (3, 1): [ins[3].chips],
             (3, 3): [ff_share.forward, ins[3].chips_again],
-            (4, "begin"): [ins[0].cores, ins[3].along],
-            (5, "begin"): [ins[0].chips, ff_share.last],
-            (6, "begin"): [write_ff],
+            (4, "begin"): [in_read.wait, ins[0].cores, early.start, ins[3].along],
+            (5, "begin"): [ins[0].chips, ff_share.last, lambda: early.step(0)],
+            (6, "begin"): [write_ff, lambda: early.step(1)],
             (6, "end"): [ins[0].chips_again],
+            (7, "begin"): [lambda: early.join(2)],
             (7, "end"): [finish_in],
+            (9, "begin"): [end_early],
             (9, "end"): [end],
         },
         step,
@@ -905,7 +993,7 @@
             return carry
 
         lax.fori_loop(0, 4, one_head, 0)
-
+        hook("grads")
         for head in range(4):
             rows = back_qkv[pl.ds(pl.multiple_of((4 * slot + head) * IN_ROWS, 16), IN_ROWS), :]
             grad = nn(rows, first_ref[...]).astype(BF16)
@@ -927,8 +1015,13 @@
             weight = in_ref[slot, :, :IN_ROWS].reshape(4 * IN_ROWS, width)
             part = tn(back_qkv[slot * 4 * IN_ROWS : (slot + 1) * 4 * IN_ROWS, cols], weight)
             back_first = part if slot == 0 else back_first + part
-        sums[0, 12:13, :] += jnp.sum(back_first * scaled, axis=0, keepdims=True)
-        sums[0, 13:14, :] += jnp.sum(back_first, axis=0, keepdims=True)
+        gain_sum = jnp.sum(back_first * scaled, axis=0, keepdims=True)
+        shift_sum = jnp.sum(back_first, axis=0, keepdims=True)
+        third = width // 3
+        for i in range(3):
+            part = slice(third * i, third * (i + 1))
+            late_sums[0, i : i + 1] += gain_sum[:, part]
+            late_sums[0, 3 + i : 4 + i] += shift_sum[:, part]
         back_norm = back_first * vector_ref[4:5, :]
         input_ref[...] = resid_ref[...] + inverse * (
             back_norm
@@ -981,7 +1074,6 @@
 ):
     rows, width = first.shape
     blocks = rows // BLOCK
-    bits = len(wider_bits())
     anywhere = pl.BlockSpec(memory_space=pl.ANY)
     one = pl.Buffered(1)
     dma = pltpu.SemaphoreType.DMA
@@ -995,10 +1087,10 @@
             pl.BlockSpec((4 * 48, rows), lambda s: (back_order(s), 0)),
             pl.BlockSpec((4 * 48, rows), lambda s: (back_order(s), 0)),
             pl.BlockSpec((4, 1, rows), lambda s: (back_order(s), 0, 0)),
-            pl.BlockSpec((rows, width), lambda s: (0, 0), pipeline_mode=one),
+            anywhere,
             pl.BlockSpec((1, 4, 48, width), lambda s: (back_order(s), 0, 0, 0)),
             pl.BlockSpec((192, width), lambda s: (0, 0), pipeline_mode=one),
-            pl.BlockSpec((4, 4, HEAD_ROWS, width), lambda s: (0, 0, 0, 0), pipeline_mode=one),
+            anywhere,
             row,
             row,
             small,
@@ -1028,16 +1120,12 @@
             pltpu.VMEM((4, 2, 2, 2, 96, width), BF16),
             pltpu.VMEM((16 * IN_ROWS, rows), BF16),
             pltpu.VMEM((width, width), BF16),
-            pltpu.VMEM((bits + 2, 16, width), F32),
-            pltpu.VMEM((GROUP - 1, 16, width), F32),
-            pltpu.VMEM((max(bits, 1), 16, width), F32),
-            pltpu.VMEM((3, 16, width), F32),
-            dma((GROUP - 1 + bits,)),
-            dma((GROUP - 1 + bits,)),
-            dma((3,)),
-            dma((3,)),
-            dma((20,)),
+            pltpu.VMEM((rows, width), BF16),
+            pltpu.VMEM((4, 4, HEAD_ROWS, width), BF16),
+            dma((22,)),
         ]
+        + sums_scratch(False, 16, width)
+        + sums_scratch(True, 8, width // 3)
         + reduce_scratch(2, 192, 96, width)
         + reduce_scratch(4, 96, 48, width)
         + share_scratch(192, width)
@@ -1123,8 +1211,7 @@
     near_ref,
     bias_ref,
     vec_ref,
-    ff_own,
-    ff_near,
+    pieces_ref,
     residual_ref,
     feed_ref,
     back_second_ref,
@@ -1137,31 +1224,42 @@
     hid_s,
     send,
     recv,
+    local,
 ):
     step = pl.program_id(0)
     width = tokens_ref.shape[1]
-    late = [None, ff_near, ff_late.at[0], ff_late.at[1]]
-    gff = Gather(ff_own, late, ff_piece, 96, send, recv)
+    gff = Gather(
+        None,
+        [None, None, ff_late.at[0], ff_late.at[1]],
+        ff_piece,
+        96,
+        send,
+        recv,
+        {2: pieces_ref.at[0], 3: pieces_ref.at[1]},
+    )
+    mine = pltpu.make_async_copy(
+        pieces_ref, ff_late.at[:, 4 * gff.y + 2 * gff.x + gff.core], local.at[0]
+    )
 
     def begin():
         greet(group_partners())
-        gff.along(3)
-        gff.along(2)
+        gff.spread(3)
+        mine.start()
         up_sum_ref[...] = jnp.zeros_like(up_sum_ref)
         second_t[width:, :] = jnp.ones((16, second_t.shape[1]), BF16)
 
     def end():
         gff.complete(3)
         gff.complete(2)
-        gff.finish(2, 3)
+        gff.finish((2, 3), range(1, 9))
+        mine.wait()
 
     hook = hooks_of(
         {
             (0, "begin"): [begin],
-            (2, "begin"): [lambda: gff.spread(3)],
-            (3, "begin"): [lambda: gff.spread(2)],
-            (5, "begin"): [lambda: gff.forward(3)],
-            (6, "begin"): [lambda: gff.last(3), lambda: gff.forward(2)],
+            (2, "begin"): [lambda: gff.forward(3), lambda: gff.spread(2)],
+            (4, "begin"): [lambda: gff.last(3)],
+            (5, "begin"): [lambda: gff.forward(2)],
             (7, "begin"): [lambda: gff.last(2)],
             (7, "end"): [end],
         },
@@ -1338,7 +1436,9 @@
     hook("end")
 
 
-def feed_first(live, tokens, out_grad, mixed, in_all, ff_near, bias_all, vectors, ff_own):
+def feed_first(
+    live, tokens, out_grad, mixed, in_all, ff_own, ff_near, bias_all, vectors, ff_pieces
+):
     rows, width = tokens.shape
     anywhere = pl.BlockSpec(memory_space=pl.ANY)
     one = pl.Buffered(1)
@@ -1357,8 +1457,7 @@
             pl.BlockSpec((8, 192, width), lambda s: (0, 0, 0), pipeline_mode=one),
             pl.BlockSpec((4, 8, 1024), lambda s: (0, 0, 0), pipeline_mode=one),
             pl.BlockSpec((8, width), lambda s: (0, 0), pipeline_mode=one),
-            anywhere,
-            anywhere,
+            pl.BlockSpec((2, 192, width), lambda s: (0, 0, 0), pipeline_mode=one),
         ],
         out_specs=[
             row,
@@ -1385,6 +1484,7 @@
             pltpu.VMEM((2, rows, width), BF16),
             pltpu.SemaphoreType.DMA((4 * GATHER_KINDS,)),
             pltpu.SemaphoreType.DMA((4 * GATHER_KINDS,)),
+            pltpu.SemaphoreType.DMA((1,)),
         ],
         compiler_params=pltpu.CompilerParams(
             vmem_limit_bytes=62 << 20, collective_id=3, has_side_effects=True
@@ -1393,7 +1493,7 @@
             flops=24_000_000_000, bytes_accessed=45_000_000, transcendentals=5_000_000
         ),
         name="feed_first",
-    )(live, tokens, out_grad, mixed, in_all, ff_own, ff_near, bias_all, vectors, ff_own, ff_near)
+    )(live, tokens, out_grad, mixed, in_all, ff_own, ff_near, bias_all, vectors, ff_pieces)
 
 
 def feed_last(
@@ -1520,11 +1620,20 @@
         (output_bias, second_gain, second_shift, down_bias, first_gain, first_shift)
     ):
         vectors = jnp.where(row == i, vector[None], vectors)
-    qkv, mixed, logsum, first, in_all, ff_near, bias_all = attend(
+    qkv, mixed, logsum, first, in_all, ff_near, ff_pieces, bias_all = attend(
         tokens, vectors, project_in.transpose(1, 2, 0), project_out, ff_own, bias_own
     )
     residual, feed, back_second, near_grad, up_sums, ff_late = feed_first(
-        live_images, tokens, out_grad, mixed, in_all, ff_near, bias_all, vectors, ff_own
+        live_images,
+        tokens,
+        out_grad,
+        mixed,
+        in_all,
+        ff_own,
+        ff_near,
+        bias_all,
+        vectors,
+        ff_pieces,
     )
     output, resid, back_mixed, late_grad, out_grads, feed_small, ff_part = feed_last(
         live_images,

time: 272 us -> 263 us (0.967)
  Pallas kernels: 248 us -> 239 us
    pallas_call x1, Pallas kernels: 44.3 us -> 38.3 us  [feed_first(): pl.pallas_call(feed_first_kernel, grid=(FEED_BLOCKS + 2,), in_specs=[pl.B...]
where the time goes in v6:
time: 263 us; the launch traced here: 262 us
  Pallas kernels  239 us (91%)
  other arithmetic  14.3 us (5%)
  local copies, waits for them, and re-layouts  8.66 us (3%)
    pallas_call x1, Pallas kernels, attend_back(): pl.pallas_call(functools.partial(attend_back_kernel, blocks=blocks), grid...  95.9 us
    pallas_call x1, Pallas kernels, attend(): pl.pallas_call(attend_kernel, grid=(4,), in_specs=[pl.BlockSpec((rows, wi...  60.3 us
    pallas_call x1, Pallas kernels, feed_last(): pl.pallas_call(feed_last_kernel, grid=(FEED_BLOCKS + 2,), in_specs=[pl.Bl...  44.4 us
    pallas_call x1, Pallas kernels, feed_first(): pl.pallas_call(feed_first_kernel, grid=(FEED_BLOCKS + 2,), in_specs=[pl.B...  38.3 us

profile of v6, /device:TPU:0, one launch (start us, length us, event | category | flops | bytes accessed | tf_op | source)
XLA Modules:
  0.0 262.5 jit_solution(10441557658646956506)
XLA Ops:
  0.7 0.1 pad.19.clone
  0.7 0.7 convert_element_type.21
  1.5 0.1 squeeze.27
  1.5 0.1 squeeze.28
  1.6 0.1 pad_maximum_fusion.1
  1.7 0.7 broadcast_in_dim.57
  2.4 1.5 select_select_fusion.vector_ref.vec_ref
  3.8 0.6 select_maximum_fusion.bias_own
  4.5 3.2 %pad_maximum_fusion.ff_own.own_ref = bf16[8,192,768]{2,1,0:T(8,128)(2,1)} fusion(bf16[8,96,768]{2,1,0:T(8,128)(2,1)} %bitcast.12, bf16[8,96,768]{2,1,0:T(8,128)(2,1)} %bitcast.13), kind=kLoop, calls=%fused_computation | loop fusion | flops 4718592 | bytes 4718592 | tf_op jit(solution)/shard_map/concatenate | solution.py:1605
  7.7 60.3 %attend.1 = (bf16[2304,1536]{1,0:T(8,128)(2,1)}, bf16[768,1536]{1,0:T(8,128)(2,1)}, f32[16,1,1536]{2,1,0:T(1,128)}, bf16[1536,768]{1,0:T(8,128)(2,1)}, bf16[4,4,...) custom-call(bf16[1536,768]{1,0:T(8,128)(2,1)} %tokens_ref.5, ...), custom_call_target="tpu_custom_call" | custom-call | flops 30000001024 | bytes 30000000 | tf_op jit(solution)/shard_map/attend/pallas_call | solution.py:404
  68.0 38.3 %feed_first.1 = (f32[1536,768]{1,0:T(8,128)}, f32[1536,768]{1,0:T(8,128)}, f32[1536,768]{1,0:T(8,128)}, bf16[2,8,192,768]{3,2,1,0:T(8,128)(2,1)}, f32[8,768]{1,0:T(8,128)}, /*index=5*/bf16[2,8,192,768]{3,2,1,0:T(8,128)(2,1)}) custom-call(s32[1,2]{1,0:T(1,128)} %live_ref.3, bf16[1536,768]{1,0:T(8,128)(2,1)} %tokens_ref.5, bf16[1536,768]{1,0:T(8,128)(2,1)} %grad_ref.3, ...), custom_call_target="tpu_custom_call" | custom-call | flops 24000000000 | bytes 45000000 | tf_op jit(solution)/shard_map/feed_first/pallas_call | solution.py:1447
  106.2 44.4 %feed_last.1 = (bf16[1536,768]{1,0:T(8,128)(2,1)}, f32[1536,768]{1,0:T(8,128)}, bf16[768,1536]{1,0:T(8,128)(2,1)}, bf16[2,8,192,768]{3,2,1,0:T(8,128)(2,1)}, bf1...) custom-call(s32[1,2]{1,0:T(1,128)} %live_ref.3, f32[1536,768]{1,0:T(8,128)} %get-tuple-element.46.residual_ref, ...), custom_call_target="tpu_custom_call" | custom-call | flops 28000000000 | bytes 55000000 | tf_op jit(solution)/shard_map/feed_last/pallas_call | solution.py:1518
  150.6 95.9 %attend_back.1 = (f32[1536,768]{1,0:T(8,128)}, f32[16,768]{1,0:T(8,128)}, bf16[8,96,768]{2,1,0:T(8,128)(2,1)}, bf16[768,768]{1,0:T(8,128)(2,1)}, bf16[3,192,768]{2,1,0:T(8,128)(2,1)}, /*index=5*/bf16[192,768]{1,0:T(8,128)(2,1)}) custom-call(bf16[2304,1536]{1,0:T(8,128)(2,1)} %get-tuple-element.52.qkv_ref, bf16[768,1536]{1,0:T(8,128)(2,1)} %get-tuple-element.53.back_ref, ...), custom_call_target="tpu_custom_call" | custom-call | flops 49999998976 | bytes 50000000 | tf_op jit(solution)/shard_map/attend_back/pallas_call | solution.py:1082
  246.5 0.0 copy-start.2
  246.5 0.8 slice_reduce_fusion.7
  247.4 1.6 slice_reduce_fusion
  249.0 0.1 reshape_squeeze.3
  249.1 0.1 stack_reshape_squeeze.6
  249.2 0.1 stack_reshape_squeeze.7
  249.2 0.6 pad_maximum_fusion.2
  249.8 1.8 convert_element_type.22
  251.6 0.0 copy-start.1
  251.6 2.6 convert_bitcast_fusion
  254.3 0.0 copy-done.2
  254.3 0.0 slice-start
  254.3 1.7 bitcast_convert_fusion
  255.9 0.0 copy-done.1
  255.9 0.0 copy-start
  255.9 0.0 slice-start.1
  255.9 1.6 convert_element_type.25
  257.5 1.4 copy-done
  258.9 1.4 copy.31
  260.3 0.0 slice-done
  260.3 0.0 slice-done.1
  260.3 2.2 copy.32
  (8 shorter events, 0.1 us)
Async XLA Ops:
  246.5 7.8 %copy-start.2 = (bf16[8,96,768]{2,1,0:T(8,128)(2,1)S(1)}, bf16[8,96,768]{2,1,0:T(8,128)(2,1)}, u32[]{:S(2)}) copy-start(bf16[8,96,768]{2,1,0:T(8,128)(2,1)} %get-tuple-element.66) | copy-start | bytes 3538948
  251.6 4.3 %copy-start.1 = (bf16[768,768]{1,0:T(8,128)(2,1)S(1)}, bf16[768,768]{1,0:T(8,128)(2,1)}, u32[]{:S(2)}) copy-start(bf16[768,768]{1,0:T(8,128)(2,1)} %get-tuple-element.67) | copy-start | bytes 3538948
  254.3 6.0 %slice-start = ((s8[4718592]{0:T(1024)(128)(4,1)}), s8[4194304]{0:T(1024)(128)(4,1)S(1)}, s32[]{:S(2)}) async-start(s8[4718592]{0:T(1024)(128)(4,1)} %bitcast.10), calls=%async_computation | async-start | bytes 8388608
  255.9 3.0 %copy-start = (bf16[1536,768]{1,0:T(8,128)(2,1)S(1)}, bf16[1536,768]{1,0:T(8,128)(2,1)}, u32[]{:S(2)}) copy-start(bf16[1536,768]{1,0:T(8,128)(2,1)} %get-tuple-element.99) | copy-start | bytes 7077892
  255.9 4.4 %slice-start.1 = ((s8[4718592]{0:T(1024)(128)(4,1)}), s8[524288]{0:T(1024)(128)(4,1)S(1)}, s32[]{:S(2)}) async-start(s8[4718592]{0:T(1024)(128)(4,1)} %bitcast.10), calls=%async_computation.1 | async-start | bytes 1048576

commit v7 on v6

--- a/solution.py
+++ b/solution.py
@@ -89,11 +89,17 @@
         y, x, core = self.y, self.x, self.core
         mine = (y, x, core)
         buffer = self.buffers[slot]
-        if kind == 0:
+        if kind in (0, 9):
             ways = lax.axis_size("mp")
             hop = 1 if slot == 2 else slot
-            src = self.view(self.buffers[1] if slot == 2 else self.own, *mine)
             dst = self.pieces[slot] if slot in self.pieces else self.view(buffer, *mine)
+            if slot == 2:
+                src = self.view(self.buffers[1], *mine)
+            elif isinstance(self.own, tuple):
+                src = self.view(self.own[kind // 9], *mine)
+                dst = dst.at[pl.ds(96 * (kind // 9), 96)]
+            else:
+                src = self.view(self.own, *mine)
             device = (self.dp, lax.rem(self.mp + ways - hop, ways))
         else:
             return self.shared(kind, buffer, kind * 4 + slot, self.pieces.get(slot))
@@ -133,12 +139,15 @@
         for kind in kinds:
             self.copy(kind, slot).wait_recv()
 
+    def along_kinds(self, slot):
+        return (0, 9) if isinstance(self.own, tuple) and slot != 2 else (0,)
+
     def along(self, slot):
-        self.start(slot, 0)
+        self.start(slot, *self.along_kinds(slot))
 
     def spread(self, slot):
         if slot not in self.pieces:
-            self.arrived(slot, 0)
+            self.arrived(slot, *self.along_kinds(slot))
         self.start(slot, 1, 2, 5)
 
     def forward(self, slot):
@@ -160,7 +169,7 @@
                 self.copy(kind, slot).wait_send()
 
 
-GATHER_KINDS = 9
+GATHER_KINDS = 10
 
 
 def in_piece(ref, chip, core):
@@ -171,11 +180,14 @@
     return ref.at[2 * chip + core]
 
 
-def greet(partners):
+def signal(partners):
     barrier = pltpu.get_barrier_semaphore()
     for partner in partners:
         pl.semaphore_signal(barrier, inc=1, device_id=partner, device_id_type=MESH)
-    pl.semaphore_wait(barrier, len(partners))
+
+
+def meet(partners):
+    pl.semaphore_wait(pltpu.get_barrier_semaphore(), len(partners))
 
 
 def chunks_of(images, size):
@@ -254,7 +266,8 @@
     vector_ref,
     in_own,
     out_own,
-    ff_own,
+    up_own,
+    down_own,
     bias_own,
     qkv_ref,
     mixed_ref,
@@ -280,7 +293,7 @@
     ways = lax.axis_size("mp")
     gin = Gather(in_all.at[0], [in_all.at[k] for k in range(4)], in_piece, 96, in_send, in_recv)
     gff = Gather(
-        ff_own,
+        (up_own, down_own),
         [None, ff_near, None, None],
         ff_piece,
         96,
@@ -315,11 +328,13 @@
         for copy in own_copies:
             copy.start()
         local_bias.start()
-        greet(group_partners())
-        for copy in own_copies:
-            copy.wait()
-        gin.along(1)
-        for rows in range(0, tokens_ref.shape[0], BLOCK):
+        signal(group_partners())
+        for i, rows in enumerate(range(0, tokens_ref.shape[0], BLOCK)):
+            if i == 2:
+                meet(group_partners())
+                for copy in own_copies:
+                    copy.wait()
+                gin.along(1)
             block = slice(rows, rows + BLOCK)
             first_ref[block] = layer_norm(
                 tokens_ref[block].astype(F32), vector_ref[4:5], vector_ref[5:6]
@@ -329,14 +344,15 @@
     def end():
         gff.complete(1)
         gff.arrived(2, 0)
-        gff.arrived(3, 0)
+        gff.arrived(3, 0, 9)
         out_in.wait()
         out_bias.wait()
         for slot in (1, 2, 3):
             bias_copy(slot).wait_send()
         gin.finish((1, 2, 3))
-        gff.finish((1,))
-        gff.finish((2, 3), (0,))
+        gff.finish((1,), range(10))
+        gff.finish((2,), (0,))
+        gff.finish((3,), (0, 9))
 
     hook = hooks_of(
         {
@@ -396,7 +412,7 @@
     return turn + (turn // 2) * (1 - 2 * (turn % 2))
 
 
-def attend(tokens, vectors, in_own, out_own, ff_own, bias_own):
+def attend(tokens, vectors, in_own, out_own, up_own, down_own, bias_own):
     rows, width = tokens.shape
     heads = 16
     anywhere = pl.BlockSpec(memory_space=pl.ANY)
@@ -407,6 +423,7 @@
         in_specs=[
             pl.BlockSpec((rows, width), lambda s: (0, 0), pipeline_mode=pl.Buffered(1)),
             pl.BlockSpec((8, width), lambda s: (0, 0)),
+            anywhere,
             anywhere,
             anywhere,
             anywhere,
@@ -451,7 +468,7 @@
             flops=30_000_000_000, bytes_accessed=30_000_000, transcendentals=19_000_000
         ),
         name="attend",
-    )(tokens, vectors, in_own, out_own, ff_own, bias_own)
+    )(tokens, vectors, in_own, out_own, up_own, down_own, bias_own)
 
 
 class Reduce:
@@ -883,9 +900,7 @@
         own(1).start()
         first_read.start()
         in_read.start()
-        greet(every_partner())
-        ff[2].cores()
-        ff[3].cores()
+        signal(every_partner())
         sums[0] = jnp.zeros_like(sums[0])
         late_sums[0] = jnp.zeros_like(late_sums[0])
         sums[0, 0:8, :] = feed_small_ref[...]
@@ -950,9 +965,9 @@
         {
             (0, 0): [begin],
             (0, "grads"): [first_read.wait],
-            (0, 1): [lambda: chips(2)],
-            (0, 3): [ff[2].chips_again, lambda: chips(3)],
-            (1, 0): [ins[2].cores],
+            (0, 1): [lambda: meet(every_partner()), ff[2].cores, ff[3].cores],
+            (0, 2): [lambda: chips(2)],
+            (1, 0): [ff[2].chips_again, lambda: chips(3), ins[2].cores],
             (1, 2): [ff[2].along],
             (1, 3): [ff[3].chips_again, ins[2].chips],
             (2, 0): [ff[3].along, ins[1].cores],
@@ -1162,8 +1177,11 @@
     second, back_low, slots, ff_refs, bias_ref, act_s, hid_s, rows, width, feed, back_second
 ):
     for i, slot in enumerate(slots):
-        up = ff_refs[i][:, 0:96, :].reshape(width, width)
-        down = ff_refs[i][:, 96:192, :].reshape(width, width)
+        if isinstance(ff_refs[i], tuple):
+            up, down = ff_refs[i][0][...], ff_refs[i][1][...]
+        else:
+            up = ff_refs[i][:, 0:96, :].reshape(width, width)
+            down = ff_refs[i][:, 96:192, :].reshape(width, width)
         hidden = nn(second, up) + bias_ref[slot, 0:1, 256:]
         half = 0.5 + 0.5 * lax.erf(hidden * (0.5**0.5))
         act = (hidden * half).astype(BF16)
@@ -1207,7 +1225,8 @@
     grad_ref,
     mixed_ref,
     out_w_ref,
-    own_ref,
+    own_up_ref,
+    own_down_ref,
     near_ref,
     bias_ref,
     vec_ref,
@@ -1242,8 +1261,7 @@
     )
 
     def begin():
-        greet(group_partners())
-        gff.spread(3)
+        signal(group_partners())
         mine.start()
         up_sum_ref[...] = jnp.zeros_like(up_sum_ref)
         second_t[width:, :] = jnp.ones((16, second_t.shape[1]), BF16)
@@ -1257,9 +1275,10 @@
     hook = hooks_of(
         {
             (0, "begin"): [begin],
-            (2, "begin"): [lambda: gff.forward(3), lambda: gff.spread(2)],
-            (4, "begin"): [lambda: gff.last(3)],
-            (5, "begin"): [lambda: gff.forward(2)],
+            (1, "begin"): [lambda: meet(group_partners()), lambda: gff.spread(3)],
+            (3, "begin"): [lambda: gff.forward(3), lambda: gff.spread(2)],
+            (5, "begin"): [lambda: gff.last(3)],
+            (6, "begin"): [lambda: gff.forward(2)],
             (7, "begin"): [lambda: gff.last(2)],
             (7, "end"): [end],
         },
@@ -1283,7 +1302,7 @@
             second,
             back_low,
             (0, 1),
-            (own_ref, near_ref),
+            ((own_up_ref, own_down_ref), near_ref),
             bias_ref,
             act_s,
             hid_s,
@@ -1346,9 +1365,7 @@
     def begin():
         own(1).start()
         own(0).start()
-        greet(group_partners())
-        ff[1].cores()
-        ff[0].cores()
+        signal(group_partners())
         small_ref[...] = jnp.zeros_like(small_ref)
         second_t[width:, :] = jnp.ones((16, second_t.shape[1]), BF16)
 
@@ -1364,8 +1381,9 @@
     hook = hooks_of(
         {
             (0, "begin"): [begin],
-            (1, "begin"): [lambda: chips(1)],
-            (3, "begin"): [ff[1].chips_again, lambda: chips(0)],
+            (1, "begin"): [lambda: meet(group_partners()), ff[1].cores, ff[0].cores],
+            (2, "begin"): [lambda: chips(1)],
+            (4, "begin"): [ff[1].chips_again, lambda: chips(0)],
             (5, "begin"): [ff[1].along],
             (6, "begin"): [ff[0].chips_again],
             (7, "begin"): [ff[0].along],
@@ -1437,7 +1455,7 @@
 
 
 def feed_first(
-    live, tokens, out_grad, mixed, in_all, ff_own, ff_near, bias_all, vectors, ff_pieces
+    live, tokens, out_grad, mixed, in_all, up_own, down_own, ff_near, bias_all, vectors, ff_pieces
 ):
     rows, width = tokens.shape
     anywhere = pl.BlockSpec(memory_space=pl.ANY)
@@ -1453,7 +1471,8 @@
             row,
             pl.BlockSpec((width, BLOCK), lambda s: (0, jnp.minimum(s, last))),
             pl.BlockSpec((4, 4, 48, width), lambda s: (0, 0, 3, 0), pipeline_mode=one),
-            pl.BlockSpec((8, 192, width), lambda s: (0, 0, 0), pipeline_mode=one),
+            pl.BlockSpec((width, width), lambda s: (0, 0), pipeline_mode=one),
+            pl.BlockSpec((width, width), lambda s: (0, 0), pipeline_mode=one),
             pl.BlockSpec((8, 192, width), lambda s: (0, 0, 0), pipeline_mode=one),
             pl.BlockSpec((4, 8, 1024), lambda s: (0, 0, 0), pipeline_mode=one),
             pl.BlockSpec((8, width), lambda s: (0, 0), pipeline_mode=one),
@@ -1493,7 +1512,7 @@
             flops=24_000_000_000, bytes_accessed=45_000_000, transcendentals=5_000_000
         ),
         name="feed_first",
-    )(live, tokens, out_grad, mixed, in_all, ff_own, ff_near, bias_all, vectors, ff_pieces)
+    )(live, tokens, out_grad, mixed, in_all, up_own, down_own, ff_near, bias_all, vectors, ff_pieces)
 
 
 def feed_last(
@@ -1602,9 +1621,6 @@
 ):
     width = tokens.shape[1]
     own_heads = project_in.shape[2] // HEAD_DIM
-    ff_own = jnp.concatenate(
-        [up_weight.reshape(8, -1, width), down_weight.reshape(8, -1, width)], axis=1
-    )
     pair_bias = query_value_bias.astype(F32).reshape(2, own_heads, HEAD_DIM)
     own_bias = jnp.concatenate([pair_bias[0], jnp.zeros_like(pair_bias[0]), pair_bias[1]], axis=1)
     bias_own = jnp.concatenate(
@@ -1621,7 +1637,13 @@
     ):
         vectors = jnp.where(row == i, vector[None], vectors)
     qkv, mixed, logsum, first, in_all, ff_near, ff_pieces, bias_all = attend(
-        tokens, vectors, project_in.transpose(1, 2, 0), project_out, ff_own, bias_own
+        tokens,
+        vectors,
+        project_in.transpose(1, 2, 0),
+        project_out,
+        up_weight.reshape(8, -1, width),
+        down_weight.reshape(8, -1, width),
+        bias_own,
     )
     residual, feed, back_second, near_grad, up_sums, ff_late = feed_first(
         live_images,
@@ -1629,7 +1651,8 @@
         out_grad,
         mixed,
         in_all,
-        ff_own,
+        up_weight,
+        down_weight,
         ff_near,
         bias_all,
         vectors,

time: 263 us -> 255 us (0.970)
  Pallas kernels: 239 us -> 235 us
  other arithmetic: 14.3 us -> 11.1 us
    concatenate x1 -> x0, other arithmetic: 3.18 us -> none  [local(): jnp.concatenate([up_weight.reshape(8, -1, width), down_weight.reshape(8,...]
where the time goes in v7:
time: 255 us
  Pallas kernels  235 us (92%)
  other arithmetic  11.1 us (4%)
  local copies, waits for them, and re-layouts  8.66 us (3%)
    pallas_call x1, Pallas kernels, attend_back(): pl.pallas_call(functools.partial(attend_back_kernel, blocks=blocks), grid...  93.5 us
    pallas_call x1, Pallas kernels, attend(): pl.pallas_call(attend_kernel, grid=(4,), in_specs=[pl.BlockSpec((rows, wi...  60.2 us
    pallas_call x1, Pallas kernels, feed_last(): pl.pallas_call(feed_last_kernel, grid=(FEED_BLOCKS + 2,), in_specs=[pl.Bl...  43.6 us
    pallas_call x1, Pallas kernels, feed_first(): pl.pallas_call(feed_first_kernel, grid=(FEED_BLOCKS + 2,), in_specs=[pl.B...  37.2 us

profile of v7, /device:TPU:0, one launch (start us, length us, event | category | flops | bytes accessed | tf_op | source)
XLA Modules:
  0.0 255.0 jit_solution(474636000469508802)
XLA Ops:
  0.7 0.1 pad.19.clone
  0.7 0.7 convert_element_type.21
  1.5 0.1 squeeze.27
  1.5 0.1 squeeze.28
  1.6 0.1 pad_maximum_fusion
  1.7 0.7 broadcast_in_dim.57
  2.4 1.5 select_select_fusion.vector_ref.vec_ref
  3.8 0.6 select_maximum_fusion.bias_own
  4.5 60.2 %attend.1 = (bf16[2304,1536]{1,0:T(8,128)(2,1)}, bf16[768,1536]{1,0:T(8,128)(2,1)}, f32[16,1,1536]{2,1,0:T(1,128)}, bf16[1536,768]{1,0:T(8,128)(2,1)}, bf16[4,4,...) custom-call(bf16[1536,768]{1,0:T(8,128)(2,1)} %tokens_ref.5, ...), custom_call_target="tpu_custom_call" | custom-call | flops 30000001024 | bytes 30000000 | tf_op jit(solution)/shard_map/attend/pallas_call | solution.py:420
  64.6 37.2 %feed_first.1 = (f32[1536,768]{1,0:T(8,128)}, f32[1536,768]{1,0:T(8,128)}, f32[1536,768]{1,0:T(8,128)}, bf16[2,8,192,768]{3,2,1,0:T(8,128)(2,1)}, f32[8,768]{1,0:T(8,128)}, /*index=5*/bf16[2,8,192,768]{3,2,1,0:T(8,128)(2,1)}) custom-call(s32[1,2]{1,0:T(1,128)} %live_ref.3, bf16[1536,768]{1,0:T(8,128)(2,1)} %tokens_ref.5, bf16[1536,768]{1,0:T(8,128)(2,1)} %grad_ref.3, ...), custom_call_target="tpu_custom_call" | custom-call | flops 24000000000 | bytes 45000000 | tf_op jit(solution)/shard_map/feed_first/pallas_call | solution.py:1465
  101.9 43.6 %feed_last.1 = (bf16[1536,768]{1,0:T(8,128)(2,1)}, f32[1536,768]{1,0:T(8,128)}, bf16[768,1536]{1,0:T(8,128)(2,1)}, bf16[2,8,192,768]{3,2,1,0:T(8,128)(2,1)}, bf1...) custom-call(s32[1,2]{1,0:T(1,128)} %live_ref.3, f32[1536,768]{1,0:T(8,128)} %get-tuple-element.46.residual_ref, ...), custom_call_target="tpu_custom_call" | custom-call | flops 28000000000 | bytes 55000000 | tf_op jit(solution)/shard_map/feed_last/pallas_call | solution.py:1537
  145.5 93.5 %attend_back.1 = (f32[1536,768]{1,0:T(8,128)}, f32[16,768]{1,0:T(8,128)}, bf16[8,96,768]{2,1,0:T(8,128)(2,1)}, bf16[768,768]{1,0:T(8,128)(2,1)}, bf16[3,192,768]{2,1,0:T(8,128)(2,1)}, /*index=5*/bf16[192,768]{1,0:T(8,128)(2,1)}) custom-call(bf16[2304,1536]{1,0:T(8,128)(2,1)} %get-tuple-element.52.qkv_ref, bf16[768,1536]{1,0:T(8,128)(2,1)} %get-tuple-element.53.back_ref, ...), custom_call_target="tpu_custom_call" | custom-call | flops 49999998976 | bytes 50000000 | tf_op jit(solution)/shard_map/attend_back/pallas_call | solution.py:1097
  239.0 0.0 copy-start.2
  239.0 0.8 slice_reduce_fusion.7
  239.9 1.6 slice_reduce_fusion
  241.5 0.1 reshape_squeeze.3
  241.6 0.1 stack_reshape_squeeze.6
  241.7 0.1 stack_reshape_squeeze.7
  241.8 0.6 pad_maximum_fusion.1
  242.3 1.8 convert_element_type.22
  244.2 0.0 copy-start.1
  244.2 2.6 %convert_bitcast_fusion = f32[768,3,192]{0,2,1:T(8,128)} fusion(bf16[3,192,768]{2,1,0:T(8,128)(2,1)} %get-tuple-element.64), kind=kLoop, calls=%fused_computation | loop fusion | flops 442368 | bytes 2654208 | tf_op jit(solution)/shard_map/transpose | solution.py:1692
  246.8 0.0 copy-done.2
  246.8 0.0 slice-start
  246.8 1.7 bitcast_convert_fusion
  248.4 0.0 copy-done.1
  248.4 0.0 copy-start
  248.4 0.0 slice-start.1
  248.4 1.6 convert_element_type.25
  250.0 1.4 copy-done
  251.4 1.4 copy.31
  252.8 0.0 slice-done
  252.8 0.0 slice-done.1
  252.8 2.2 copy.32
  (8 shorter events, 0.1 us)
Async XLA Ops:
  239.0 7.8 %copy-start.2 = (bf16[8,96,768]{2,1,0:T(8,128)(2,1)S(1)}, bf16[8,96,768]{2,1,0:T(8,128)(2,1)}, u32[]{:S(2)}) copy-start(bf16[8,96,768]{2,1,0:T(8,128)(2,1)} %get-tuple-element.66) | copy-start | bytes 3538948
  244.2 4.3 %copy-start.1 = (bf16[768,768]{1,0:T(8,128)(2,1)S(1)}, bf16[768,768]{1,0:T(8,128)(2,1)}, u32[]{:S(2)}) copy-start(bf16[768,768]{1,0:T(8,128)(2,1)} %get-tuple-element.67) | copy-start | bytes 3538948
  246.8 6.0 %slice-start = ((s8[4718592]{0:T(1024)(128)(4,1)}), s8[4194304]{0:T(1024)(128)(4,1)S(1)}, s32[]{:S(2)}) async-start(s8[4718592]{0:T(1024)(128)(4,1)} %bitcast.10), calls=%async_computation | async-start | bytes 8388608
  248.4 3.0 %copy-start = (bf16[1536,768]{1,0:T(8,128)(2,1)S(1)}, bf16[1536,768]{1,0:T(8,128)(2,1)}, u32[]{:S(2)}) copy-start(bf16[1536,768]{1,0:T(8,128)(2,1)} %get-tuple-element.99) | copy-start | bytes 7077892
  248.4 4.4 %slice-start.1 = ((s8[4718592]{0:T(1024)(128)(4,1)}), s8[524288]{0:T(1024)(128)(4,1)S(1)}, s32[]{:S(2)}) async-start(s8[4718592]{0:T(1024)(128)(4,1)} %bitcast.10), calls=%async_computation.1 | async-start | bytes 1048576

commit v8 on v7

--- a/solution.py
+++ b/solution.py
@@ -388,11 +388,11 @@
     slot = slot_order(step)
     hook("begin")
     bias_t = bias_all[slot, :, 0:256].T
+    weight = in_all[slot, :, :IN_ROWS].reshape(4 * IN_ROWS, first_ref.shape[1])
+    product = nt(weight, first_ref[...])
     for part in range(4):
-        product = nt(in_all[slot, part, :IN_ROWS], first_ref[...])
-        qkv_ref[part * IN_ROWS : (part + 1) * IN_ROWS, :] = (
-            product + bias_t[:IN_ROWS, part : part + 1]
-        ).astype(BF16)
+        rows = slice(part * IN_ROWS, (part + 1) * IN_ROWS)
+        qkv_ref[rows, :] = (product[rows] + bias_t[:IN_ROWS, part : part + 1]).astype(BF16)
     hook("heads")
 
     def one_head(head, carry):
@@ -1009,13 +1009,13 @@
 
         lax.fori_loop(0, 4, one_head, 0)
         hook("grads")
+        rows = back_qkv[pl.ds(pl.multiple_of(4 * slot * IN_ROWS, 16), 4 * IN_ROWS), :]
+        slot_grad = nn(rows, first_ref[...]).astype(BF16)
         for head in range(4):
-            rows = back_qkv[pl.ds(pl.multiple_of((4 * slot + head) * IN_ROWS, 16), IN_ROWS), :]
-            grad = nn(rows, first_ref[...]).astype(BF16)
+            grad = slot_grad[head * IN_ROWS : (head + 1) * IN_ROWS]
             grads[slot, head // 2, head % 2, 0] = grad[:96]
             grads[slot, head // 2, head % 2, 1, 0:48] = grad[96:]
             grads[slot, head // 2, head % 2, 1, 48:96] = out_grad_ref[0, head]
-        rows = back_qkv[pl.ds(pl.multiple_of(4 * slot * IN_ROWS, 16), 4 * IN_ROWS), :]
         row_sums = nt(jnp.ones((8, rows.shape[1]), BF16), rows)
         sums[0, pl.ds(8 + slot, 1), 0 : 4 * IN_ROWS] = row_sums[0:1]
 

time: 255 us -> 251 us (0.984)
  Pallas kernels: 235 us -> 230 us
    pallas_call x1, Pallas kernels: 60.2 us -> 55.3 us  [attend(): pl.pallas_call(attend_kernel, grid=(4,), in_specs=[pl.BlockSpec((rows, wi...]
where the time goes in v8:
time: 251 us
  Pallas kernels  230 us (92%)
  other arithmetic  11.1 us (4%)
  local copies, waits for them, and re-layouts  8.66 us (3%)
    pallas_call x1, Pallas kernels, attend_back(): pl.pallas_call(functools.partial(attend_back_kernel, blocks=blocks), grid...  94.1 us
    pallas_call x1, Pallas kernels, attend(): pl.pallas_call(attend_kernel, grid=(4,), in_specs=[pl.BlockSpec((rows, wi...  55.3 us
    pallas_call x1, Pallas kernels, feed_last(): pl.pallas_call(feed_last_kernel, grid=(FEED_BLOCKS + 2,), in_specs=[pl.Bl...  43.6 us
    pallas_call x1, Pallas kernels, feed_first(): pl.pallas_call(feed_first_kernel, grid=(FEED_BLOCKS + 2,), in_specs=[pl.B...  37.2 us

profile of v8, /device:TPU:0, one launch (start us, length us, event | category | flops | bytes accessed | tf_op | source)
XLA Modules:
  0.0 250.7 jit_solution(11468908928642796574)
XLA Ops:
  0.7 0.1 pad.19.clone
  0.7 0.7 convert_element_type.21
  1.5 0.1 squeeze.27
  1.5 0.1 squeeze.28
  1.6 0.1 pad_maximum_fusion
  1.7 0.7 broadcast_in_dim.57
  2.4 1.5 select_select_fusion.vector_ref.vec_ref
  3.8 0.6 select_maximum_fusion.bias_own
  4.5 55.3 %attend.1 = (bf16[2304,1536]{1,0:T(8,128)(2,1)}, bf16[768,1536]{1,0:T(8,128)(2,1)}, f32[16,1,1536]{2,1,0:T(1,128)}, bf16[1536,768]{1,0:T(8,128)(2,1)}, bf16[4,4,...) custom-call(bf16[1536,768]{1,0:T(8,128)(2,1)} %tokens_ref.5, ...), custom_call_target="tpu_custom_call" | custom-call | flops 30000001024 | bytes 30000000 | tf_op jit(solution)/shard_map/attend/pallas_call | solution.py:420
  59.8 37.2 %feed_first.1 = (f32[1536,768]{1,0:T(8,128)}, f32[1536,768]{1,0:T(8,128)}, f32[1536,768]{1,0:T(8,128)}, bf16[2,8,192,768]{3,2,1,0:T(8,128)(2,1)}, f32[8,768]{1,0:T(8,128)}, /*index=5*/bf16[2,8,192,768]{3,2,1,0:T(8,128)(2,1)}) custom-call(s32[1,2]{1,0:T(1,128)} %live_ref.3, bf16[1536,768]{1,0:T(8,128)(2,1)} %tokens_ref.5, bf16[1536,768]{1,0:T(8,128)(2,1)} %grad_ref.3, ...), custom_call_target="tpu_custom_call" | custom-call | flops 24000000000 | bytes 45000000 | tf_op jit(solution)/shard_map/feed_first/pallas_call | solution.py:1465
  97.0 43.6 %feed_last.1 = (bf16[1536,768]{1,0:T(8,128)(2,1)}, f32[1536,768]{1,0:T(8,128)}, bf16[768,1536]{1,0:T(8,128)(2,1)}, bf16[2,8,192,768]{3,2,1,0:T(8,128)(2,1)}, bf1...) custom-call(s32[1,2]{1,0:T(1,128)} %live_ref.3, f32[1536,768]{1,0:T(8,128)} %get-tuple-element.46.residual_ref, ...), custom_call_target="tpu_custom_call" | custom-call | flops 28000000000 | bytes 55000000 | tf_op jit(solution)/shard_map/feed_last/pallas_call | solution.py:1537
  140.7 94.1 %attend_back.1 = (f32[1536,768]{1,0:T(8,128)}, f32[16,768]{1,0:T(8,128)}, bf16[8,96,768]{2,1,0:T(8,128)(2,1)}, bf16[768,768]{1,0:T(8,128)(2,1)}, bf16[3,192,768]{2,1,0:T(8,128)(2,1)}, /*index=5*/bf16[192,768]{1,0:T(8,128)(2,1)}) custom-call(bf16[2304,1536]{1,0:T(8,128)(2,1)} %get-tuple-element.52.qkv_ref, bf16[768,1536]{1,0:T(8,128)(2,1)} %get-tuple-element.53.back_ref, ...), custom_call_target="tpu_custom_call" | custom-call | flops 49999998976 | bytes 50000000 | tf_op jit(solution)/shard_map/attend_back/pallas_call | solution.py:1097
  234.8 0.0 copy-start.2
  234.8 0.8 slice_reduce_fusion.7
  235.6 1.6 slice_reduce_fusion
  237.2 0.1 reshape_squeeze.3
  237.3 0.1 stack_reshape_squeeze.6
  237.4 0.1 stack_reshape_squeeze.7
  237.5 0.6 pad_maximum_fusion.1
  238.1 1.8 convert_element_type.22
  239.9 0.0 copy-start.1
  239.9 2.6 %convert_bitcast_fusion = f32[768,3,192]{0,2,1:T(8,128)} fusion(bf16[3,192,768]{2,1,0:T(8,128)(2,1)} %get-tuple-element.64), kind=kLoop, calls=%fused_computation | loop fusion | flops 442368 | bytes 2654208 | tf_op jit(solution)/shard_map/transpose | solution.py:1692
  242.5 0.0 copy-done.2
  242.5 0.0 slice-start
  242.5 1.7 bitcast_convert_fusion
  244.2 0.0 copy-done.1
  244.2 0.0 copy-start
  244.2 0.0 slice-start.1
  244.2 1.6 convert_element_type.25
  245.7 1.4 copy-done
  247.1 1.4 copy.31
  248.5 0.0 slice-done
  248.5 0.0 slice-done.1
  248.6 2.2 copy.32
  (8 shorter events, 0.1 us)
Async XLA Ops:
  234.8 7.8 %copy-start.2 = (bf16[8,96,768]{2,1,0:T(8,128)(2,1)S(1)}, bf16[8,96,768]{2,1,0:T(8,128)(2,1)}, u32[]{:S(2)}) copy-start(bf16[8,96,768]{2,1,0:T(8,128)(2,1)} %get-tuple-element.66) | copy-start | bytes 3538948
  239.9 4.3 %copy-start.1 = (bf16[768,768]{1,0:T(8,128)(2,1)S(1)}, bf16[768,768]{1,0:T(8,128)(2,1)}, u32[]{:S(2)}) copy-start(bf16[768,768]{1,0:T(8,128)(2,1)} %get-tuple-element.67) | copy-start | bytes 3538948
  242.5 6.0 %slice-start = ((s8[4718592]{0:T(1024)(128)(4,1)}), s8[4194304]{0:T(1024)(128)(4,1)S(1)}, s32[]{:S(2)}) async-start(s8[4718592]{0:T(1024)(128)(4,1)} %bitcast.10), calls=%async_computation | async-start | bytes 8388608
  244.2 3.0 %copy-start = (bf16[1536,768]{1,0:T(8,128)(2,1)S(1)}, bf16[1536,768]{1,0:T(8,128)(2,1)}, u32[]{:S(2)}) copy-start(bf16[1536,768]{1,0:T(8,128)(2,1)} %get-tuple-element.99) | copy-start | bytes 7077892
  244.2 4.4 %slice-start.1 = ((s8[4718592]{0:T(1024)(128)(4,1)}), s8[524288]{0:T(1024)(128)(4,1)S(1)}, s32[]{:S(2)}) async-start(s8[4718592]{0:T(1024)(128)(4,1)} %bitcast.10), calls=%async_computation.1 | async-start | bytes 1048576

commit v9 on v8

--- a/solution.py
+++ b/solution.py
@@ -330,7 +330,7 @@
         local_bias.start()
         signal(group_partners())
         for i, rows in enumerate(range(0, tokens_ref.shape[0], BLOCK)):
-            if i == 2:
+            if i == 1:
                 meet(group_partners())
                 for copy in own_copies:
                     copy.wait()
@@ -1621,15 +1621,12 @@
 ):
     width = tokens.shape[1]
     own_heads = project_in.shape[2] // HEAD_DIM
-    pair_bias = query_value_bias.astype(F32).reshape(2, own_heads, HEAD_DIM)
-    own_bias = jnp.concatenate([pair_bias[0], jnp.zeros_like(pair_bias[0]), pair_bias[1]], axis=1)
-    bias_own = jnp.concatenate(
-        [
-            jnp.pad(own_bias, ((0, 8 - own_heads), (0, 256 - own_bias.shape[1]))),
-            jnp.pad(up_bias.astype(F32)[None], ((0, 7), (0, 0))),
-        ],
-        axis=1,
-    )
+    pair_bias = query_value_bias.reshape(2, own_heads, HEAD_DIM)
+    place_of = lambda value, top, left: jnp.pad(
+        value, ((top, 8 - top - value.shape[0]), (left, 1024 - left - value.shape[1]))
+    )
+    bias_own = place_of(pair_bias[0], 0, 0) + place_of(pair_bias[1], 0, 2 * HEAD_DIM)
+    bias_own = (bias_own + place_of(up_bias[None], 0, 256)).astype(F32)
     row = lax.broadcasted_iota(jnp.int32, (8, width), 0)
     vectors = jnp.zeros((8, width), F32)
     for i, vector in enumerate(

time: 251 us -> 251 us (level)
  no operation moved by 1% of the time
where the time goes in v9:
time: 251 us
  Pallas kernels  230 us (92%)
  other arithmetic  10.4 us (4%)
  local copies, waits for them, and re-layouts  9.34 us (4%)
    pallas_call x1, Pallas kernels, attend_back(): pl.pallas_call(functools.partial(attend_back_kernel, blocks=blocks), grid...  94.1 us
    pallas_call x1, Pallas kernels, attend(): pl.pallas_call(attend_kernel, grid=(4,), in_specs=[pl.BlockSpec((rows, wi...  55.3 us
    pallas_call x1, Pallas kernels, feed_last(): pl.pallas_call(feed_last_kernel, grid=(FEED_BLOCKS + 2,), in_specs=[pl.Bl...  43.6 us
    pallas_call x1, Pallas kernels, feed_first(): pl.pallas_call(feed_first_kernel, grid=(FEED_BLOCKS + 2,), in_specs=[pl.B...  37.2 us

profile of v9, /device:TPU:0, one launch (start us, length us, event | category | flops | bytes accessed | tf_op | source)
XLA Modules:
  0.0 250.7 jit_solution(8107817604543096918)
XLA Ops:
  0.6 0.8 slice_reduce_fusion.11
  1.4 0.1 squeeze.27
  1.5 0.1 squeeze.28
  1.6 0.7 broadcast_in_dim.52
  2.3 1.5 select_select_fusion.vector_ref.vec_ref
  3.8 0.7 add_convert_fusion.bias_own
  4.4 55.3 %attend.1 = (bf16[2304,1536]{1,0:T(8,128)(2,1)}, bf16[768,1536]{1,0:T(8,128)(2,1)}, f32[16,1,1536]{2,1,0:T(1,128)}, bf16[1536,768]{1,0:T(8,128)(2,1)}, bf16[4,4,...) custom-call(bf16[1536,768]{1,0:T(8,128)(2,1)} %tokens_ref.5, ...), custom_call_target="tpu_custom_call" | custom-call | flops 30000001024 | bytes 30000000 | tf_op jit(solution)/shard_map/attend/pallas_call | solution.py:420
  59.8 37.2 %feed_first.1 = (f32[1536,768]{1,0:T(8,128)}, f32[1536,768]{1,0:T(8,128)}, f32[1536,768]{1,0:T(8,128)}, bf16[2,8,192,768]{3,2,1,0:T(8,128)(2,1)}, f32[8,768]{1,0:T(8,128)}, /*index=5*/bf16[2,8,192,768]{3,2,1,0:T(8,128)(2,1)}) custom-call(s32[1,2]{1,0:T(1,128)} %live_ref.3, bf16[1536,768]{1,0:T(8,128)(2,1)} %tokens_ref.5, bf16[1536,768]{1,0:T(8,128)(2,1)} %grad_ref.3, ...), custom_call_target="tpu_custom_call" | custom-call | flops 24000000000 | bytes 45000000 | tf_op jit(solution)/shard_map/feed_first/pallas_call | solution.py:1465
  97.0 43.6 %feed_last.1 = (bf16[1536,768]{1,0:T(8,128)(2,1)}, f32[1536,768]{1,0:T(8,128)}, bf16[768,1536]{1,0:T(8,128)(2,1)}, bf16[2,8,192,768]{3,2,1,0:T(8,128)(2,1)}, bf1...) custom-call(s32[1,2]{1,0:T(1,128)} %live_ref.3, f32[1536,768]{1,0:T(8,128)} %get-tuple-element.46.residual_ref, ...), custom_call_target="tpu_custom_call" | custom-call | flops 28000000000 | bytes 55000000 | tf_op jit(solution)/shard_map/feed_last/pallas_call | solution.py:1537
  140.6 94.1 %attend_back.1 = (f32[1536,768]{1,0:T(8,128)}, f32[16,768]{1,0:T(8,128)}, bf16[8,96,768]{2,1,0:T(8,128)(2,1)}, bf16[768,768]{1,0:T(8,128)(2,1)}, bf16[3,192,768]{2,1,0:T(8,128)(2,1)}, /*index=5*/bf16[192,768]{1,0:T(8,128)(2,1)}) custom-call(bf16[2304,1536]{1,0:T(8,128)(2,1)} %get-tuple-element.52.qkv_ref, bf16[768,1536]{1,0:T(8,128)(2,1)} %get-tuple-element.53.back_ref, ...), custom_call_target="tpu_custom_call" | custom-call | flops 49999998976 | bytes 50000000 | tf_op jit(solution)/shard_map/attend_back/pallas_call | solution.py:1097
  234.7 0.0 copy-start.2
  234.7 0.8 slice_reduce_fusion.7
  235.6 1.6 slice_reduce_fusion
  237.2 0.1 reshape_squeeze.3
  237.3 0.1 stack_reshape_squeeze.6
  237.4 0.1 stack_reshape_squeeze.7
  237.4 0.6 pad_maximum_fusion
  238.0 1.8 convert_element_type.23
  239.9 0.0 copy-start.1
  239.9 2.6 %convert_bitcast_fusion = f32[768,3,192]{0,2,1:T(8,128)} fusion(bf16[3,192,768]{2,1,0:T(8,128)(2,1)} %get-tuple-element.64), kind=kLoop, calls=%fused_computation | loop fusion | flops 442368 | bytes 2654208 | tf_op jit(solution)/shard_map/transpose | solution.py:1689
  242.5 0.0 copy-done.2
  242.5 0.0 slice-start
  242.5 1.7 bitcast_convert_fusion
  244.1 0.0 copy-done.1
  244.1 0.0 copy-start
  244.1 0.0 slice-start.1
  244.1 1.6 convert_element_type.26
  245.7 1.4 copy-done
  247.1 1.4 copy.31
  248.5 0.0 slice-done
  248.5 0.0 slice-done.1
  248.5 2.2 copy.32
  (5 shorter events, 0.0 us)
Async XLA Ops:
  234.7 7.8 %copy-start.2 = (bf16[8,96,768]{2,1,0:T(8,128)(2,1)S(1)}, bf16[8,96,768]{2,1,0:T(8,128)(2,1)}, u32[]{:S(2)}) copy-start(bf16[8,96,768]{2,1,0:T(8,128)(2,1)} %get-tuple-element.66) | copy-start | bytes 3538948
  239.9 4.3 %copy-start.1 = (bf16[768,768]{1,0:T(8,128)(2,1)S(1)}, bf16[768,768]{1,0:T(8,128)(2,1)}, u32[]{:S(2)}) copy-start(bf16[768,768]{1,0:T(8,128)(2,1)} %get-tuple-element.67) | copy-start | bytes 3538948
  242.5 6.0 %slice-start = ((s8[4718592]{0:T(1024)(128)(4,1)}), s8[4194304]{0:T(1024)(128)(4,1)S(1)}, s32[]{:S(2)}) async-start(s8[4718592]{0:T(1024)(128)(4,1)} %bitcast.10), calls=%async_computation | async-start | bytes 8388608
  244.1 3.0 %copy-start = (bf16[1536,768]{1,0:T(8,128)(2,1)S(1)}, bf16[1536,768]{1,0:T(8,128)(2,1)}, u32[]{:S(2)}) copy-start(bf16[1536,768]{1,0:T(8,128)(2,1)} %get-tuple-element.99) | copy-start | bytes 7077892
  244.1 4.4 %slice-start.1 = ((s8[4718592]{0:T(1024)(128)(4,1)}), s8[524288]{0:T(1024)(128)(4,1)S(1)}, s32[]{:S(2)}) async-start(s8[4718592]{0:T(1024)(128)(4,1)} %bitcast.10), calls=%async_computation.1 | async-start | bytes 1048576
